TPU v7x, 256 devices: a whole 4x4x8 slice. The times are simulated.
256 devices in a mesh: ctx: 8 (over z), exp: 32 (over x, y, core).
Axes of the slice: x: 4, y: 4, z: 8, core: 2. Of those that a mesh axis runs over, the one named last changes fastest.
Arguments:
- tokens: bfloat16 [8192, 2048], P(('ctx', 'exp')), may hold values from -6 to 6
- gain_in: float32 [2048], replicated, may hold values from 0.1 to 1.9
- w_heads: bfloat16 [2048, 16384], P(None, 'exp'), may hold values from -0.125 to 0.125
- w_scalar: bfloat16 [2048, 64], P(None, 'exp'), may hold values from -0.125 to 0.125
- strength_bias: float32 [32], P('exp'), may hold values from -8 to 1
- decay_rate: float32 [32], P('exp'), may hold values from 1e-06 to 0.05
- decay_bias: float32 [32], P('exp'), may hold values from -3 to 3
- state_init: float32 [32, 128, 128], P('exp'), may hold values from -1.5 to 1.5
- gain_head: float32 [128], replicated, may hold values from 0.1 to 1.9
- w_output: bfloat16 [4096, 2048], P('exp'), may hold values from -0.09375 to 0.09375
- gain_expert: float32 [2048], replicated, may hold values from 0.1 to 1.9
- expert_ids: int32 [8192, 10], P(('ctx', 'exp')), may hold values from 0 to 31, all different within a row; in each aligned block of 32 rows (0 to 31, 32 to 63, ...) at most 20 rows name the same one
- gate_weights: float32 [8192, 10], P(('ctx', 'exp')), may hold values from 0.5 to 1.5
- w_gate_up: bfloat16 [32, 2048, 1024], P('exp'), may hold values from -0.125 to 0.125
- w_down: bfloat16 [32, 512, 2048], P('exp'), may hold values from -0.25 to 0.25
Outputs:
- attn_out: bfloat16 [8192, 2048], P(('ctx', 'exp'))
- expert_out: bfloat16 [8192, 2048], P(('ctx', 'exp'))
Inputs may be any that keep to these rules, and one draw needn't show every extreme that they name: `expert_ids`: each row names 10 different experts. In every aligned block of 32 rows (the rows of one device) no expert is named by more than 20 rows, a bound that some block reaches.
All inputs are finite; a program needn't handle non-finite values.
Results may differ from a plain program's by a relative error of at most 0.029.
Values may be sent and summed in bfloat16 or wider, within the bound.
No kernel may reach another device: no remote copies, remote signals or barrier semaphores. Data moves between devices by JAX's collectives and lax.ppermute only.
A program may use at most 128 MiB of HBM per device.

v0:
```python
import jax
import jax.numpy as jnp
from jax import lax
from jax.sharding import PartitionSpec as P

STRETCH = 64


EPSILON = 1e-06
PRECISE = lax.Precision.HIGHEST


def shifted(value, axis, steps):
    count = lax.axis_size(axis)
    first, last = (max(0, -steps), min(count, count - steps))
    return lax.ppermute(value, axis, [(source, source + steps) for source in range(first, last)])


def rms_scale(values):
    return lax.rsqrt(jnp.mean(values * values, axis=-1, keepdims=True) + EPSILON)


def prepare(query, key_vec, value, strength, log_alpha):
    head_count, span_rows, head_dim = query.shape
    stretch_count = span_rows // STRETCH
    stretch_shape = (head_count, stretch_count, STRETCH, head_dim)
    query = query.reshape(stretch_shape)
    key_vec = key_vec.reshape(stretch_shape)
    value = value.reshape(stretch_shape)
    strength = strength.reshape(head_count, stretch_count, STRETCH)
    decay_sum = jnp.cumsum(log_alpha.reshape(head_count, stretch_count, STRETCH), axis=-1)
    decay_gap = decay_sum[..., :, None] - decay_sum[..., None, :]
    row_ids = lax.broadcasted_iota(jnp.int32, (STRETCH, STRETCH), 0)
    col_ids = lax.broadcasted_iota(jnp.int32, (STRETCH, STRETCH), 1)
    decay_pair = jnp.where(row_ids >= col_ids, jnp.exp(jnp.minimum(decay_gap, 0.0)), 0.0)
    key_gram = jnp.einsum("hncd,hnsd->hncs", key_vec, key_vec, precision=PRECISE)
    lower_part = jnp.where(row_ids > col_ids, key_gram * decay_pair * strength[..., :, None], 0.0)
    system = lower_part + jnp.eye(STRETCH, dtype=jnp.float32)
    growth = jnp.exp(decay_sum)
    right_sides = jnp.concatenate(
        [value * strength[..., None], key_vec * (strength * growth)[..., None]], axis=-1
    )
    solved = jax.scipy.linalg.solve_triangular(system, right_sides, lower=True, unit_diagonal=True)
    update = solved[..., :head_dim]
    correction = solved[..., head_dim:]
    within = jnp.einsum("hncd,hnsd->hncs", query, key_vec, precision=PRECISE) * decay_pair
    last_sum = decay_sum[..., -1]
    query_decay = query * growth[..., None]
    key_tail = key_vec * jnp.exp(last_sum[..., None] - decay_sum)[..., None]
    return (query_decay, key_tail, update, correction, within, jnp.exp(last_sum))


def emit_stretches(initial, parts):

    def emit_advance(carried, bundle):
        query_decay, key_tail, update, correction, within, stretch_fall = bundle
        pending = update - jnp.einsum("hcd,hvd->hcv", correction, carried, precision=PRECISE)
        result = jnp.einsum("hcd,hvd->hcv", query_decay, carried, precision=PRECISE)
        result = result + jnp.einsum("hcs,hsv->hcv", within, pending, precision=PRECISE)
        carried = stretch_fall[:, None, None] * carried + jnp.einsum(
            "hcv,hce->hve", pending, key_tail, precision=PRECISE
        )
        return (carried, result)

    _, results = lax.scan(
        emit_advance, initial, tuple((jnp.moveaxis(piece, 1, 0) for piece in parts))
    )
    results = jnp.moveaxis(results, 0, 1)
    return results.reshape(results.shape[0], results.shape[1] * results.shape[2], results.shape[3])


def block_maps(parts):
    query_decay, key_tail, update, correction, within, stretch_fall = parts
    head_count = key_tail.shape[0]
    head_dim = key_tail.shape[-1]
    identity = jnp.eye(head_dim, dtype=jnp.float32)

    def block_advance(carried, bundle):
        transfer, offset = carried
        tail_part, update_part, correction_part, fall_part = bundle
        local_map = fall_part[:, None, None] * identity - jnp.einsum(
            "hcd,hce->hde", correction_part, tail_part, precision=PRECISE
        )
        drive = jnp.einsum("hcv,hce->hve", update_part, tail_part, precision=PRECISE)
        transfer = jnp.einsum("hab,hbc->hac", transfer, local_map, precision=PRECISE)
        offset = jnp.einsum("hab,hbc->hac", offset, local_map, precision=PRECISE) + drive
        return ((transfer, offset), None)

    start_maps = (
        jnp.broadcast_to(identity, (head_count, head_dim, head_dim)),
        jnp.zeros((head_count, head_dim, head_dim), jnp.float32),
    )
    bundles = tuple(
        (jnp.moveaxis(piece, 1, 0) for piece in (key_tail, update, correction, stretch_fall))
    )
    (transfer, offset), _ = lax.scan(block_advance, start_maps, bundles)
    return (transfer, offset)


def shards(
    tokens,
    gain_in,
    w_heads,
    w_scalar,
    strength_bias,
    decay_rate,
    decay_bias,
    state_init,
    gain_head,
    w_output,
    gain_expert,
    expert_ids,
    gate_weights,
    w_gate_up,
    w_down,
):
    wide_in = tokens.astype(jnp.float32)
    normed_in = (wide_in * rms_scale(wide_in) * gain_in).astype(jnp.bfloat16)
    gathered = lax.all_gather(normed_in, "exp", axis=0, tiled=True)
    span_rows = gathered.shape[0]
    head_count = state_init.shape[0]
    head_dim = state_init.shape[-1]
    projected = jnp.dot(gathered, w_heads, preferred_element_type=jnp.float32)
    projected = projected.reshape(span_rows, head_count, 4, head_dim).transpose(1, 2, 0, 3)
    gate_logits = jnp.dot(gathered, w_scalar, preferred_element_type=jnp.float32)
    gate_logits = gate_logits.reshape(span_rows, head_count, 2).transpose(1, 2, 0)
    query = projected[:, 0]
    key_vec = projected[:, 1]
    value = projected[:, 2]
    gate_vec = projected[:, 3]
    strength = jax.nn.sigmoid(gate_logits[:, 0] + strength_bias[:, None])
    log_alpha = -decay_rate[:, None] * jax.nn.softplus(gate_logits[:, 1] + decay_bias[:, None])
    key_vec = key_vec * lax.rsqrt(jnp.sum(key_vec * key_vec, axis=-1, keepdims=True) + EPSILON)
    parts = prepare(query, key_vec, value, strength, log_alpha)
    transfer, offset = block_maps(parts)
    is_first = lax.axis_index("ctx") == 0
    carried = jnp.where(is_first, state_init, 0.0)
    for relay_turn in range(lax.axis_size("ctx") - 1):
        leaving = jnp.einsum("hab,hbc->hac", carried, transfer, precision=PRECISE) + offset
        arrived = shifted(leaving.astype(jnp.bfloat16), "ctx", 1).astype(leaving.dtype)
        carried = jnp.where(is_first, state_init, arrived)
    head_raw = emit_stretches(carried, parts)
    gated = (head_raw * rms_scale(head_raw) * gain_head * jax.nn.silu(gate_vec)).astype(
        jnp.bfloat16
    )
    gated = gated.transpose(1, 0, 2).reshape(span_rows, head_count * head_dim)
    tok_dev = tokens.shape[0]
    width = tokens.shape[1]
    summed = lax.psum_scatter(
        jnp.dot(gated, w_output, preferred_element_type=jnp.float32).astype(jnp.bfloat16),
        "exp",
        scatter_dimension=0,
        tiled=True,
    )
    hidden = wide_in + summed.astype(jnp.float32)
    normed_ffn = (hidden * rms_scale(hidden) * gain_expert).astype(jnp.bfloat16)
    top_count = expert_ids.shape[1]
    local_count = w_gate_up.shape[0]
    expert_total = local_count * lax.axis_size("exp")
    capacity = max(2, 2 * tok_dev * top_count // expert_total)
    hidden_units = w_down.shape[1]
    route_ids = expert_ids.reshape(-1)
    one_hot = (route_ids[:, None] == jnp.arange(expert_total, dtype=jnp.int32)[None, :]).astype(
        jnp.int32
    )
    slot_rank = jnp.sum((jnp.cumsum(one_hot, axis=0) - one_hot) * one_hot, axis=1)
    flat_slot = route_ids * capacity + slot_rank
    source_rows = jnp.repeat(normed_ffn, top_count, axis=0)
    outgoing = (
        jnp.zeros((expert_total * capacity, width), jnp.bfloat16).at[flat_slot].set(source_rows)
    )
    outgoing = outgoing.reshape(expert_total, capacity, width)
    received = lax.all_to_all(outgoing, "exp", split_axis=0, concat_axis=0, tiled=True)
    slot_count = received.shape[1]
    grouped = received.reshape(expert_total // local_count, local_count, slot_count, width)
    pre_act = jnp.einsum("slnd,ldf->slnf", grouped, w_gate_up, preferred_element_type=jnp.float32)
    activated = (jax.nn.silu(pre_act[..., :hidden_units]) * pre_act[..., hidden_units:]).astype(
        jnp.bfloat16
    )
    expert_rows = jnp.einsum(
        "slnf,lfd->slnd", activated, w_down, preferred_element_type=jnp.float32
    ).astype(jnp.bfloat16)
    expert_rows = expert_rows.reshape(expert_total, slot_count, width)
    returned_rows = lax.all_to_all(expert_rows, "exp", split_axis=0, concat_axis=0, tiled=True)
    picked = returned_rows.reshape(expert_total * capacity, width)[flat_slot].reshape(
        tok_dev, top_count, width
    )
    expert_out = jnp.einsum(
        "tk,tkd->td", gate_weights, picked.astype(jnp.float32), precision=PRECISE
    ).astype(jnp.bfloat16)
    return (summed, expert_out)


def solution(mesh):
    return jax.shard_map(
        shards,
        mesh=mesh,
        in_specs=(
            P(("ctx", "exp"), None),
            P(),
            P(None, "exp"),
            P(None, "exp"),
            P("exp"),
            P("exp"),
            P("exp"),
            P("exp", None, None),
            P(),
            P("exp", None),
            P(),
            P(("ctx", "exp"), None),
            P(("ctx", "exp"), None),
            P("exp", None, None),
            P("exp", None, None),
        ),
        out_specs=(P(("ctx", "exp"), None), P(("ctx", "exp"), None)),
        check_vma=False,
    )
```

profile of v0, /device:TPU:8, one launch (start us, length us, event | category | flops | bytes accessed | tf_op | source)
XLA Modules:
  0.0 607.3 jit_solution(3826642573789988676)
XLA Ops:
  12.2 52.6 %all-gather.2.cloned.1.call-done = bf16[1024,2048]{1,0:T(8,128)(2,1)} async-done(((bf16[32,2048]{1,0:T(8,128)(2,1)}), bf16[1024,2048]{1,0:T(8,128)(2,1)}) %all-gather.2.cloned.1.call-update) | async-done | bytes 4194320 | tf_op jit(solution)/shard_map/all_gather | solution.py:119
  64.8 3.4 convolution_bitcast_fusion.11
  68.8 5.2 fusion.135
  78.2 2.1 fusion.51
  80.3 80.0 %custom-call.4 = f32[16,1,64,64]{2,3,1,0:T(8,128)} custom-call(f32[16,1,64,64]{3,2,1,0:T(8,128)} %fusion.51), custom_call_target="InvertDiagBlocksLowerTriangular" | custom-call | tf_op jit(solution)/shard_map/jit(_solve_triangular)/vmap()/triangular_solve | solution.py:43
  160.8 2.1 convolution_bitcast_fusion.3
  165.1 63.8 %while.26 = (s32[]{:T(128)}, f32[1,128,128]{1,2,0:T(8,128)S(1)}, f32[1,128,128]{1,2,0:T(8,128)S(1)}, f32[16,1]{0,1:T(1,128)S(1)}, f32[16,1,64,128]{3,2,1,0:T(8,1...) while((s32[]{:T(128)}, f32[1,128,128]{1,2,0:T(8,128)S(1)}, ...), condition=%wide.region_4.5_spmd.clone, body=%wide.region_3.4_spmd.clone.sunk | while | flops 75563008 | bytes 854625 | solution.py:96
  165.7 1.7 convolution_subtract_fusion.5
  169.7 1.7 convolution_subtract_fusion.5
  173.7 1.7 convolution_subtract_fusion.5
  177.7 1.7 convolution_subtract_fusion.5
  181.7 1.7 convolution_subtract_fusion.5
  185.7 1.7 convolution_subtract_fusion.5
  189.7 1.7 convolution_subtract_fusion.5
  193.7 1.7 convolution_subtract_fusion.5
  197.7 1.7 convolution_subtract_fusion.5
  201.7 1.7 convolution_subtract_fusion.5
  205.6 1.7 convolution_subtract_fusion.5
  209.6 1.7 convolution_subtract_fusion.5
  213.6 1.7 convolution_subtract_fusion.5
  217.6 1.7 convolution_subtract_fusion.5
  221.6 1.7 convolution_subtract_fusion.5
  225.6 1.7 convolution_subtract_fusion.5
  229.4 3.5 collective-permute-start
  234.7 4.2 collective-permute-start.1
  240.8 4.2 collective-permute-start.2
  246.8 4.2 collective-permute-start.3
  252.9 4.3 collective-permute-start.4
  259.1 5.4 collective-permute-start.5
  266.4 5.6 collective-permute-start.6
  272.0 1.8 fusion.45
  273.9 94.0 %while.25 = (s32[]{:T(128)}, f32[1,128,128]{2,1,0:T(8,128)S(1)}, f32[16,1,64,128]{3,2,1,0:T(8,128)}, f32[16,1]{0,1:T(1,128)S(1)}, f32[16,1,64,128]{3,2,1,0:T(8,1...) while((s32[]{:T(128)}, f32[1,128,128]{2,1,0:T(8,128)S(1)}, ...), condition=%wide.region_6.7_spmd, body=%wide.region_5.6_spmd.sunk | while | flops 44089344 | bytes 626289 | solution.py:65
  307.4 1.7 fusion.177
  313.3 1.7 fusion.177
  348.5 1.7 fusion.177
  370.4 4.3 convolution_convert_fusion
  377.2 93.0 %reduce-scatter.2.cloned.1.call-done = bf16[32,2048]{1,0:T(8,128)(2,1)} async-done(((bf16[1024,2048]{1,0:T(8,128)(2,1)}), bf16[32,2048]{1,0:T(8,128)(2,1)}) %reduce-scatter.2.cloned.1.call-update) | async-done | bytes 131088 | tf_op jit(solution)/shard_map/reduce_scatter | solution.py:149
  473.9 2.5 reshape.628
  476.4 4.4 scatter_custom_fusion
  480.8 5.2 reshape.607
  486.0 44.1 %all_to_all.10 = bf16[32,20,2048]{2,1,0:T(8,128)(2,1)S(1)} all-to-all(bf16[32,20,2048]{2,1,0:T(8,128)(2,1)} %reshape.607), channel_id=1, replica_groups=mesh['ctx'=8,'exp'=32] {'exp'}, dimensions={0} | all-to-all | bytes 5242880 | tf_op jit(solution)/shard_map/all_to_all | solution.py:173
  530.0 3.6 fusion.37
  535.2 3.2 copy.94
  538.3 6.0 all-to-all-start.1
  544.5 39.5 %all-to-all-done.1 = bf16[32,20,2048]{2,1,0:T(8,128)(2,1)} async-done(((bf16[32,20,2048]{2,1,0:T(8,128)(2,1)}), bf16[32,20,2048]{2,1,0:T(8,128)(2,1)}, u32[]{:S(2)}, u32[]{:S(2)}) %all-to-all-start.1) | async-done | bytes 2621472 | tf_op jit(solution)/shard_map/all_to_all | solution.py:184
  583.9 5.2 reshape.611
  589.1 6.5 %gather_fusion = bf16[320,2048]{1,0:T(8,128)(2,1)S(1)} fusion(bf16[640,2048]{1,0:T(8,128)(2,1)} %reshape.611, s32[1024]{0:T(1024)S(1)} %pad_clamp_fusion), kind=kCustom, calls=%fused_computation | custom fusion | bytes 2622720 | tf_op jit(solution)/shard_map/gather | solution.py:185
  597.2 2.6 fusion.136
  (250 shorter events, 158.5 us)
Async XLA Ops:
  7.2 526.4 %copy-start = (bf16[1,512,2048]{2,1,0:T(8,128)(2,1)S(1)}, bf16[1,512,2048]{2,1,0:T(8,128)(2,1)}, u32[]{:S(2)}) copy-start(bf16[1,512,2048]{2,1,0:T(8,128)(2,1)} %param.33) | copy-start | bytes 6291460
  7.2 57.6 %all-gather.2.cloned.1.call-start = ((), (), s32[]{:S(2)}) async-start(), calls=%async_computation.3 | async-start | bytes 4325376 | tf_op jit(solution)/shard_map/all_gather | solution.py:119
  10.1 460.1 %reduce-scatter.2.cloned.1.call-start = ((), (), s32[]{:S(2)}) async-start(), calls=%async_computation.4 | async-start | bytes 4325376 | tf_op jit(solution)/shard_map/reduce_scatter | solution.py:149
  74.1 1.3 copy-start.2
  164.0 65.1 %copy-start.1 = (f32[1,128,128]{2,1,0:T(8,128)S(1)}, f32[1,128,128]{2,1,0:T(8,128)}, u32[]{:S(2)}) copy-start(f32[1,128,128]{2,1,0:T(8,128)} %param.26) | copy-start | bytes 196612
  229.4 5.0 collective-permute-start
  234.7 5.8 collective-permute-start.1
  240.8 5.8 collective-permute-start.2
  246.8 5.8 collective-permute-start.3
  252.9 5.9 collective-permute-start.4
  259.1 7.0 %collective-permute-start.5 = (bf16[1,128,128]{2,1,0:T(8,128)(2,1)S(1)}, bf16[1,128,128]{2,1,0:T(8,128)(2,1)S(1)}, u32[]{:S(2)}, u32[]{:S(2)}) collective-permute-start(bf16[1,128,128]{2,1,0:T(8,128)(2,1)S(1)} %fusion.60), channel_id=1, source_target_pairs={{0,32},{32,64},{64,96},{96,128},{128,160},{160,192},{192,224},{1,3... | collective-permute-start | bytes 98312 | tf_op jit(solution)/shard_map/ppermute | solution.py:16
  266.4 7.5 %collective-permute-start.6 = (bf16[1,128,128]{2,1,0:T(8,128)(2,1)S(1)}, bf16[1,128,128]{2,1,0:T(8,128)(2,1)S(1)}, u32[]{:S(2)}, u32[]{:S(2)}) collective-permute-start(bf16[1,128,128]{2,1,0:T(8,128)(2,1)S(1)} %fusion.59), channel_id=1, source_target_pairs={{0,32},{32,64},{64,96},{96,128},{128,160},{160,192},{192,224},{1,3... | collective-permute-start | bytes 98312 | tf_op jit(solution)/shard_map/ppermute | solution.py:16
  273.8 96.6 %copy-start.4 = (bf16[128,2048]{1,0:T(8,128)(2,1)S(1)}, bf16[128,2048]{1,0:T(8,128)(2,1)}, u32[]{:S(2)}) copy-start(bf16[128,2048]{1,0:T(8,128)(2,1)} %param.28) | copy-start | bytes 1572868
  273.9 96.6 %copy-start.8 = (f32[128]{0:T(128)S(1)}, f32[128]{0:T(128)}, u32[]{:S(2)}) copy-start(f32[128]{0:T(128)} %param.27) | copy-start | bytes 1540
  374.8 0.7 copy-start.5
  374.8 95.4 %copy-start.3 = (bf16[32,2048]{1,0:T(8,128)(2,1)S(1)}, bf16[32,2048]{1,0:T(8,128)(2,1)}, u32[]{:S(2)}) copy-start(bf16[32,2048]{1,0:T(8,128)(2,1)} %param.19) | copy-start | bytes 393220
  374.8 96.5 %copy-start.6 = (f32[2048]{0:T(1024)S(1)}, f32[2048]{0:T(1024)}, u32[]{:S(2)}) copy-start(f32[2048]{0:T(1024)} %param.29) | copy-start | bytes 24580
  486.0 44.1 %copy-start.9 = (bf16[1,2048,1024]{2,1,0:T(8,128)(2,1)S(1)}, bf16[1,2048,1024]{2,1,0:T(8,128)(2,1)}, u32[]{:S(2)}) copy-start(bf16[1,2048,1024]{2,1,0:T(8,128)(2,1)} %param.32) | copy-start | bytes 12582916
  538.3 6.0 copy-start.7
  538.3 45.6 %all-to-all-start.1 = ((bf16[32,20,2048]{2,1,0:T(8,128)(2,1)}), bf16[32,20,2048]{2,1,0:T(8,128)(2,1)}, u32[]{:S(2)}, u32[]{:S(2)}) async-start(bf16[32,20,2048]{2,1,0:T(8,128)(2,1)} %copy.94), calls=%async_computation.2 | async-start | bytes 6291456 | tf_op jit(solution)/shard_map/all_to_all | solution.py:184
Sparse Core Ops, SparseCore 0:
  11.1 53.6 all-gather.1
  374.9 95.2 reduce-scatter.1
where the time goes:
time: 617 us; the launch traced here: 607 us
  waiting for transfers between devices  192 us (31%)
  matrix products  166 us (27%)
  other arithmetic  91.6 us (15%)
  local copies, waits for them, and re-layouts  57.9 us (9%)
  blocking collectives  44.1 us (7%)
  starting transfers between devices  37.6 us (6%)
  between operations  16.3 us (3%)
    reduce_scatter x1, waiting for transfers between devices, shards(): lax.psum_scatter(jnp.dot(gated, w_output, preferred_element_type=jnp.floa...  93 us
    another operation x4, other arithmetic, prepare(): jax.scipy.linalg.solve_triangular(system, right_sides, lower=True, unit_d...  80.1 us
    all_gather x1, waiting for transfers between devices, shards(): gathered = lax.all_gather(normed_in, 'exp', axis=0, tiled=True)  52.6 us
    all_to_all x1, blocking collectives, shards(): lax.all_to_all(outgoing, 'exp', split_axis=0, concat_axis=0, tiled=True)  44.1 us
    all_to_all x1, waiting for transfers between devices, shards(): lax.all_to_all(expert_rows, 'exp', split_axis=0, concat_axis=0, tiled=True)  39.5 us
    ppermute x7, starting transfers between devices, shifted(): lax.ppermute(value, axis, [(source, source + steps) for source in range(f...  31.5 us
    dot_general x16, matrix products, block_advance(): jnp.einsum('hcd,hce->hde', correction_part, tail_part, precision=PRECISE)  27.3 us
    dot_general x16, matrix products, emit_advance(): jnp.einsum('hcv,hce->hve', pending, key_tail, precision=PRECISE)  27.3 us
  transfers between devices with their start and end apart: 10, of which 9 were waited for; matrix products, arithmetic and copies ran while one was open for 1% of the time, Pallas kernels for 0%

commit v1 on v0

v1 whole, which is shorter than its diff:
```python
import functools
import jax
import jax.numpy as jnp
from jax import lax
from jax.experimental import pallas as pl
from jax.experimental.pallas import tpu as pltpu
from jax.sharding import Mesh, PartitionSpec as P

EPSILON = 1e-06
F32 = jnp.float32
BF16 = jnp.bfloat16
CHUNK = 128


def mm(a, b):
    return jnp.dot(a.astype(BF16), b.astype(BF16), preferred_element_type=F32)


def pieces(a):
    high = a.astype(BF16)
    rest = a - high.astype(F32)
    middle = rest.astype(BF16)
    low = (rest - middle.astype(F32)).astype(BF16)
    return high, middle, low


def mixer_body(scal_ref, x_ref, w_ref, ws_ref, g_ref, h_ref, gate_ref, maps_ref, po_ref, *, per_step):
    dim = maps_ref.shape[0]
    step = pl.program_id(0)

    @pl.when(step == 0)
    def _():
        rows = lax.broadcasted_iota(jnp.int32, (dim, 2 * dim), 0)
        cols = lax.broadcasted_iota(jnp.int32, (dim, 2 * dim), 1)
        po_ref[...] = jnp.where(rows == cols, 1.0, 0.0).astype(F32)

    lift = scal_ref[0]
    rate = scal_ref[1]
    bias = scal_ref[2]
    rows = lax.broadcasted_iota(jnp.int32, (CHUNK, CHUNK), 0)
    cols = lax.broadcasted_iota(jnp.int32, (CHUNK, CHUNK), 1)
    differ = jnp.bitwise_xor(rows, cols)
    lower = rows >= cols
    strict = rows > cols
    lower_ones = jnp.where(lower, 1.0, 0.0).astype(BF16)
    upper_ones = jnp.where(rows <= cols, 1.0, 0.0).astype(BF16)
    eye = jnp.where(rows == cols, 1.0, 0.0).astype(F32)
    x = x_ref[...]
    projected = jnp.dot(x, w_ref[...], preferred_element_type=F32)
    logits = jnp.dot(x, ws_ref[...], preferred_element_type=F32)
    gate_ref[...] = projected[:, 3 * dim:]
    ready = []
    for n in range(per_step):
        at = slice(n * CHUNK, (n + 1) * CHUNK)
        query = projected[at, :dim]
        key_raw = projected[at, dim:2 * dim]
        value = projected[at, 2 * dim:3 * dim]
        strength = jax.nn.sigmoid(logits[at, 0:1] + lift)
        shifted_logit = logits[at, 1:2] + bias
        softplus = jnp.maximum(shifted_logit, 0.0) + jnp.log1p(jnp.exp(-jnp.abs(shifted_logit)))
        log_alpha = jnp.broadcast_to(-rate * softplus, (CHUNK, CHUNK))
        beta = jnp.broadcast_to(strength, (CHUNK, dim))
        high, middle, low = pieces(log_alpha)
        sum_col = (
            jnp.dot(lower_ones, high, preferred_element_type=F32)
            + jnp.dot(lower_ones, middle, preferred_element_type=F32)
            + jnp.dot(lower_ones, low, preferred_element_type=F32)
        )
        sum_row = sum_col.T
        key_vec = key_raw * lax.rsqrt(jnp.sum(key_raw * key_raw, axis=-1, keepdims=True) + EPSILON)
        key_t = key_vec.T
        last = sum_col[CHUNK - 1:CHUNK, :]
        fall = jnp.exp(last)
        growth = jnp.exp(sum_col)
        tail_row = jnp.exp(sum_row[:, CHUNK - 1:CHUNK] - sum_row)
        decay = jnp.where(lower, jnp.exp(jnp.minimum(sum_col - sum_row, 0.0)), 0.0)
        gram = mm(jnp.concatenate([key_vec, query], axis=0), key_t)
        lower_part = jnp.where(strict, gram[:CHUNK] * decay * beta, 0.0)
        inverse = eye - jnp.where(differ < 2, lower_part, 0.0)
        width = 2
        while width < CHUNK:
            corner = jnp.where((differ >= width) & (differ < 2 * width), lower_part, 0.0)
            inverse = inverse - mm(mm(inverse, corner), inverse)
            width *= 2
        sides = jnp.concatenate([value * beta, key_vec * (beta * growth)], axis=1)
        solved = mm(inverse, sides)
        mixed = mm(gram[CHUNK:] * decay, solved)
        query_eff = query * growth - mixed[:, dim:]
        drive = mm(key_t * tail_row, solved)
        ready.append((query_eff, mixed[:, :dim], drive, fall))
    carried = po_ref[...]
    for n in range(per_step):
        at = slice(n * CHUNK, (n + 1) * CHUNK)
        query_eff, base, drive, fall = ready[n]
        both = mm(query_eff, carried)
        g_ref[at, :] = both[:, :dim].astype(BF16)
        h_ref[at, :] = both[:, dim:] + base
        falls = jnp.concatenate([fall, fall], axis=1)
        moved = falls * carried - mm(drive[:, dim:], carried)
        carried = jnp.concatenate([moved[:, :dim], moved[:, dim:] + drive[:, :dim]], axis=1)
    po_ref[...] = carried

    @pl.when(step == pl.num_programs(0) - 1)
    def _():
        maps_ref[...] = carried.astype(maps_ref.dtype)


def mixer(scalars, x, w, ws, dim, per_step):
    span, width = x.shape
    rows = per_step * CHUNK
    by_rows = pl.BlockSpec((rows, dim), lambda i: (i, 0))
    return pl.pallas_call(
        functools.partial(mixer_body, per_step=per_step),
        grid=(span // rows,),
        in_specs=[
            pl.BlockSpec(memory_space=pltpu.SMEM),
            pl.BlockSpec((rows, width), lambda i: (i, 0)),
            pl.BlockSpec(w.shape, lambda i: (0, 0)),
            pl.BlockSpec(ws.shape, lambda i: (0, 0)),
        ],
        out_specs=[by_rows, by_rows, by_rows, pl.BlockSpec((dim, 2 * dim), lambda i: (0, 0))],
        out_shape=[
            jax.ShapeDtypeStruct((span, dim), BF16),
            jax.ShapeDtypeStruct((span, dim), F32),
            jax.ShapeDtypeStruct((span, dim), F32),
            jax.ShapeDtypeStruct((dim, 2 * dim), BF16),
        ],
        scratch_shapes=[pltpu.VMEM((dim, 2 * dim), F32)],
        name="mixer",
    )(scalars, x, w, ws)


def rms_scale(values):
    return lax.rsqrt(jnp.mean(values * values, axis=-1, keepdims=True) + EPSILON)


def norm_body(tokens_ref, gain_ref, out_ref):
    wide = tokens_ref[...].astype(F32)
    normed = (wide * rms_scale(wide) * gain_ref[...]).astype(BF16)
    out_ref[...] = jnp.broadcast_to(normed[None], out_ref.shape)


def norm_copies(tokens, gain, copies):
    return pl.pallas_call(
        norm_body,
        out_shape=jax.ShapeDtypeStruct((copies,) + tokens.shape, BF16),
        name="norm_copies",
    )(tokens, gain[None])


def emit_body(place_ref, maps_ref, init_ref, g_ref, h_ref, gate_ref, gain_ref, out_ref, state_ref):
    dim = init_ref.shape[0]

    @pl.when(pl.program_id(0) == 0)
    def _():
        state = init_ref[...].T
        for block in range(maps_ref.shape[0] - 1):
            maps = maps_ref[block]
            moved = mm(maps[:, :dim], state) + maps[:, dim:].astype(F32)
            state = jnp.where(block < place_ref[0], moved, state)
        state_ref[...] = state

    head_raw = mm(g_ref[...], state_ref[...]) + h_ref[...]
    gate = gate_ref[...]
    gated = head_raw * rms_scale(head_raw) * gain_ref[...] * (gate * jax.nn.sigmoid(gate))
    out_ref[...] = gated.astype(BF16).reshape(out_ref.shape)


def emit(place, maps, init, g, h, gate, gain, outer, inner):
    span, dim = g.shape
    rows = span // outer
    each = rows // inner
    by_rows = pl.BlockSpec((rows, dim), lambda i: (i, 0))
    return pl.pallas_call(
        emit_body,
        grid=(outer,),
        in_specs=[
            pl.BlockSpec(memory_space=pltpu.SMEM),
            pl.BlockSpec(maps.shape, lambda i: (0, 0, 0)),
            pl.BlockSpec(init.shape, lambda i: (0, 0)),
            by_rows,
            by_rows,
            by_rows,
            pl.BlockSpec((1, dim), lambda i: (0, 0)),
        ],
        out_specs=pl.BlockSpec((inner, 1, each, dim), lambda i: (0, i, 0, 0)),
        out_shape=jax.ShapeDtypeStruct((inner, outer, each, dim), BF16),
        scratch_shapes=[pltpu.VMEM((dim, dim), F32)],
        name="emit",
    )(place, maps, init, g, h, gate, gain[None])


def project_body(gated_ref, w_ref, out_ref):
    total = None
    heads, _, dim = gated_ref.shape
    left = jnp.concatenate([gated_ref[head] for head in range(heads)], axis=1)
    total = jnp.dot(left, w_ref[...], preferred_element_type=F32)
    out_ref[...] = total.astype(BF16)


def project(gated, w, tile):
    heads, rows, dim = gated.shape
    width = w.shape[1]
    return pl.pallas_call(
        project_body,
        grid=(width // tile,),
        in_specs=[
            pl.BlockSpec(gated.shape, lambda i: (0, 0, 0)),
            pl.BlockSpec((heads * dim, tile), lambda i: (0, i)),
        ],
        out_specs=pl.BlockSpec((rows, tile), lambda i: (0, i)),
        out_shape=jax.ShapeDtypeStruct((rows, width), BF16),
        name="project",
    )(gated, w)


def join_body(parts_ref, tokens_ref, gain_ref, out_ref, copies_ref):
    total = parts_ref[0].astype(F32)
    for part in range(1, parts_ref.shape[0]):
        total = total + parts_ref[part].astype(F32)
    summed = total.astype(BF16)
    out_ref[...] = summed
    hidden = tokens_ref[...].astype(F32) + summed.astype(F32)
    normed = (hidden * rms_scale(hidden) * gain_ref[...]).astype(BF16)
    copies_ref[...] = jnp.broadcast_to(normed[None], copies_ref.shape)


def join(parts, tokens, gain, copies):
    return pl.pallas_call(
        join_body,
        out_shape=[
            jax.ShapeDtypeStruct(tokens.shape, BF16),
            jax.ShapeDtypeStruct((copies,) + tokens.shape, BF16),
        ],
        name="join",
    )(parts, tokens, gain[None])


def total_body(parts_ref, out_ref):
    total = parts_ref[0].astype(F32)
    for part in range(1, parts_ref.shape[0]):
        total = total + parts_ref[part].astype(F32)
    out_ref[...] = total.astype(BF16)


def total_of(parts):
    return pl.pallas_call(
        total_body,
        out_shape=jax.ShapeDtypeStruct(parts.shape[1:], BF16),
        name="total",
    )(parts)


def swap_cores(value):
    return lax.ppermute(value, "core", [(0, 1), (1, 0)])


def exchange(value, axes):
    return lax.all_to_all(value, axes, split_axis=0, concat_axis=0, tiled=True)


def expert(x, w_gate_up, w_down, weights):
    hidden_units = w_down.shape[0]
    pre = jnp.dot(x, w_gate_up, preferred_element_type=F32)
    activated = (jax.nn.silu(pre[:, :hidden_units]) * pre[:, hidden_units:]).astype(BF16)
    rows = jnp.dot(activated, w_down, preferred_element_type=F32).astype(BF16)
    return rows.astype(F32) * weights


def shards(
    tokens,
    gain_in,
    w_heads,
    w_scalar,
    strength_bias,
    decay_rate,
    decay_bias,
    state_init,
    gain_head,
    w_output,
    gain_expert,
    expert_ids,
    gate_weights,
    w_gate_up,
    w_down,
):
    tok_dev, width = tokens.shape
    dim = state_init.shape[-1]
    x_count, y_count, core_count = (lax.axis_size(axis) for axis in ("x", "y", "core"))
    chips = x_count * y_count
    expert_total = chips * core_count
    span = expert_total * tok_dev

    experts = jnp.arange(expert_total, dtype=jnp.int32)
    named = expert_ids[:, :, None] == experts[None, None, :]
    dense_gate = jnp.sum(jnp.where(named, gate_weights[:, :, None], 0.0), axis=1)
    dense_gate = dense_gate.reshape(tok_dev, chips, core_count).transpose(1, 0, 2)
    gates = exchange(dense_gate, ("x", "y")).reshape(chips * tok_dev, core_count)
    other_gate_up = swap_cores(w_gate_up)
    other_down = swap_cores(w_down)

    copies = norm_copies(tokens, gain_in, chips)
    mine = exchange(copies, ("x", "y"))
    gathered = lax.all_gather(mine, "core", axis=1, tiled=False).reshape(span, width)
    w_wide = lax.all_gather(w_output, ("y", "core"), axis=0, tiled=True)

    scalars = jnp.concatenate([strength_bias, decay_rate, decay_bias])
    w_logit = jnp.pad(w_scalar, ((0, 0), (0, 128 - w_scalar.shape[1])))
    g, h, gate, maps = mixer(scalars, gathered, w_heads, w_logit, dim, 2)
    all_maps = lax.all_gather(maps, "ctx", axis=0, tiled=False)
    place = lax.axis_index("ctx").astype(jnp.int32)[None]
    gated = emit(
        place, all_maps, state_init[0], g, h, gate, gain_head, x_count, y_count * core_count
    )
    heads = y_count * core_count
    gated = exchange(gated, ("y", "core")).reshape(heads, x_count * tok_dev, dim)
    partial = project(gated, w_wide, 512).reshape(x_count, tok_dev, width)
    summed, copies = join(exchange(partial, "x"), tokens, gain_expert, chips)

    received = exchange(copies, ("x", "y")).reshape(chips * tok_dev, width)
    core = lax.axis_index("core")
    own_gate = jnp.where(core == 0, gates[:, 0:1], gates[:, 1:2])
    other_gate = jnp.where(core == 0, gates[:, 1:2], gates[:, 0:1])
    outputs = expert(received, w_gate_up[0], w_down[0], own_gate)
    outputs = outputs + expert(received, other_gate_up[0], other_down[0], other_gate)
    outputs = outputs.astype(BF16).reshape(chips, tok_dev, width)
    expert_out = total_of(exchange(outputs, ("x", "y")))
    return (summed, expert_out)


def solution(mesh):
    fine = Mesh(mesh.devices.reshape(mesh.shape["ctx"], 4, 4, 2), ("ctx", "x", "y", "core"))
    exp = ("x", "y", "core")
    rows = ("ctx", "x", "y", "core")
    return jax.shard_map(
        shards,
        mesh=fine,
        in_specs=(
            P(rows, None),
            P(),
            P(None, exp),
            P(None, exp),
            P(exp),
            P(exp),
            P(exp),
            P(exp, None, None),
            P(),
            P(exp, None),
            P(),
            P(rows, None),
            P(rows, None),
            P(exp, None, None),
            P(exp, None, None),
        ),
        out_specs=(P(rows, None), P(rows, None)),
        check_vma=False,
    )
```

time: 617 us -> 245 us (0.40); the launches traced: 607 us -> 245 us
  matrix products: 166 us -> 13.5 us
  waiting for transfers between devices: 192 us -> 53.7 us
  other arithmetic: 91.6 us -> 0.77 us
  blocking collectives: 44.1 us -> 103 us
  local copies, waits for them, and re-layouts: 57.9 us -> 1.99 us
  Pallas kernels: 0 us -> 41.1 us
  starting transfers between devices: 37.6 us -> 14.1 us
    dot_general x143 -> x4, matrix products: 164 us -> 13.5 us  [the longest x2 9.18 us: expert(): pre = jnp.dot(x, w_gate_up, preferred_element_type=F32)]
    reduce_scatter x1 -> x0, waiting for transfers between devices: 93 us -> none  [shards(): lax.psum_scatter(jnp.dot(gated, w_output, preferred_element_type=jnp.floa...]
    another operation x9 -> x0, other arithmetic: 81.3 us -> none  [the longest x4 80.1 us: prepare(): jax.scipy.linalg.solve_triangular(system, right_sides, lower=True, unit_d...]
    pallas_call x0 -> x6, Pallas kernels: none -> 41.1 us  [the longest x1 23.6 us: mixer(): pl.pallas_call(functools.partial(mixer_body, per_step=per_step), grid=(sp...]
    all_gather x1 -> x2, waiting for transfers between devices: 52.6 us -> 15.5 us  [the longest x1 15.5 us: shards(): lax.all_gather(mine, 'core', axis=1, tiled=False).reshape(span, width)]
    ppermute x7 -> x2, starting transfers between devices: 31.5 us -> 0.1 us  [swap_cores(): return lax.ppermute(value, 'core', [(0, 1), (1, 0)])]
    all_to_all x1 -> x3, blocking collectives: 44.1 us -> 74.3 us  [exchange(): return lax.all_to_all(value, axes, split_axis=0, concat_axis=0, tiled=True)]
    all_gather x0 -> x1, blocking collectives: none -> 28.9 us  [shards(): all_maps = lax.all_gather(maps, 'ctx', axis=0, tiled=False)]
  transfers between devices with their start and end apart: 10 -> 7, of which waited for: 9 -> 4; matrix products, arithmetic and copies ran while one was open for 1% -> 5% of each run, Pallas kernels for 0% -> 15%
where the time goes in v1:
time: 245 us
  blocking collectives  103 us (42%)
  waiting for transfers between devices  53.7 us (22%)
  Pallas kernels  41.1 us (17%)
  between operations  16.1 us (7%)
  starting transfers between devices  14.1 us (6%)
  matrix products  13.5 us (6%)
    all_to_all x3, blocking collectives, exchange(): return lax.all_to_all(value, axes, split_axis=0, concat_axis=0, tiled=True)  74.3 us
    all_to_all x3, waiting for transfers between devices, exchange(): return lax.all_to_all(value, axes, split_axis=0, concat_axis=0, tiled=True)  37.5 us
    all_gather x1, blocking collectives, shards(): all_maps = lax.all_gather(maps, 'ctx', axis=0, tiled=False)  28.9 us
    pallas_call x1, Pallas kernels, mixer(): pl.pallas_call(functools.partial(mixer_body, per_step=per_step), grid=(sp...  23.6 us
    all_gather x1, waiting for transfers between devices, shards(): lax.all_gather(mine, 'core', axis=1, tiled=False).reshape(span, width)  15.5 us
    all_to_all x3, starting transfers between devices, exchange(): return lax.all_to_all(value, axes, split_axis=0, concat_axis=0, tiled=True)  13.9 us
    dot_general x2, matrix products, expert(): pre = jnp.dot(x, w_gate_up, preferred_element_type=F32)  9.18 us
    pallas_call x1, Pallas kernels, emit(): pl.pallas_call(emit_body, grid=(outer,), in_specs=[pl.BlockSpec(memory_sp...  5.17 us
  transfers between devices with their start and end apart: 7, of which 4 were waited for; matrix products, arithmetic and copies ran while one was open for 5% of the time, Pallas kernels for 15%

profile of v1, /device:TPU:8, one launch (start us, length us, event | category | flops | bytes accessed | tf_op | source)
XLA Modules:
  0.0 244.6 jit_solution(12769110943745899905)
XLA Ops:
  7.2 0.0 all-gather.7.cloned.1.call-start
  7.2 2.5 %norm_copies.1 = bf16[16,32,2048]{2,1,0:T(8,128)(2,1)} custom-call(bf16[32,2048]{1,0:T(8,128)(2,1)} %tokens_ref.3, f32[1,2048]{1,0:T(1,128)} %bitcast.40), custom_call_target="tpu_custom_call" | custom-call | tf_op jit(solution)/shard_map/norm_copies/pallas_call | solution.py:144
  9.7 34.1 %all_to_all.30 = bf16[16,32,2048]{2,1,0:T(8,128)(2,1)} all-to-all(bf16[16,32,2048]{2,1,0:T(8,128)(2,1)} %norm_copies.1), channel_id=1, replica_groups=mesh['ctx'=8,'x'=4,'y'=4,'core'=2] {'x','y'}, dimensions={0} | all-to-all | bytes 4194304 | tf_op jit(solution)/shard_map/all_to_all | solution.py:259
  43.8 0.0 copy-start.1
  43.8 0.0 all-gather.7.cloned.1.call-update
  43.9 0.0 all-gather.5.cloned.1.call-start
  43.9 0.7 all-gather.5.cloned.1.call-update
  44.6 0.1 collective-permute-start
  44.7 0.0 copy-done.1
  44.7 0.3 copy.27
  47.0 0.9 pad.4.ws_ref
  47.9 0.6 pad_maximum_fusion.scal_ref
  48.5 15.5 %all-gather.7.cloned.1.call-done = bf16[16,64,2048]{2,1,0:T(8,128)(2,1)} async-done(((bf16[16,32,2048]{2,1,0:T(8,128)(2,1)}), bf16[16,64,2048]{2,1,0:T(8,128)(2,1)}) %all-gather.7.cloned.1.call-update) | async-done | bytes 4194320 | tf_op jit(solution)/shard_map/all_gather | solution.py:304
  64.0 23.6 %mixer.1 = (bf16[1024,128]{1,0:T(8,128)(2,1)}, f32[1024,128]{1,0:T(8,128)}, f32[1024,128]{1,0:T(8,128)}, bf16[128,256]{1,0:T(8,128)(2,1)}) custom-call(f32[3]{0:T(128)} %pad_maximum_fusion.scal_ref, bf16[1024,2048]{1,0:T(8,128)(2,1)} %bitcast.32, bf16[2048,512]{1,0:T(8,128)(2,1)} %w_ref.1, bf16[2048,128]{1,0:T(8,128)(2,1)} %pad.4.ws_ref), custom_call_target="tpu_custom_call" | custom-call | tf_op jit(solution)/shard_map/mixer/pallas_call | solution.py:112
  87.6 28.9 %all-gather.1 = bf16[1024,256]{1,0:T(8,128)(2,1)} all-gather(bf16[128,256]{1,0:T(8,128)(2,1)} %get-tuple-element.8), channel_id=3, replica_groups=mesh['ctx'=8,'x'=4,'y'=4,'core'=2] {'ctx'}, dimensions={0}, use_global_device_ids=true | all-gather | bytes 589824 | tf_op jit(solution)/shard_map/all_gather | solution.py:310
  116.5 5.2 %emit.1 = bf16[8,4,32,128]{3,2,1,0:T(8,128)(2,1)} custom-call(s32[1]{0:T(128)} %bitcast.place_ref, bf16[8,128,256]{2,1,0:T(8,128)(2,1)} %bitcast.37, f32[128,128]{1,0:T(8,128)} %bitcast.39, bf16[1024,128]{1,0:T(8,128)(2,1)} %get-tuple-element.9.g_ref, f32[1024,128]{1,0:T(8,128)} %get-tuple-element.10.h_ref, f32[1024,128]{1,0:T(8,128)} %get-tuple-element.11.gate_ref, ...), custom_call_target="tpu_custom_call" | custom-call | tf_op jit(solution)/shard_map/emit/pallas_call | solution.py:174
  121.7 11.0 %all_to_all.31 = bf16[8,4,32,128]{3,2,1,0:T(8,128)(2,1)} all-to-all(bf16[8,4,32,128]{3,2,1,0:T(8,128)(2,1)} %emit.1), channel_id=1, replica_groups=mesh['ctx'=8,'x'=4,'y'=4,'core'=2] {'y','core'}, dimensions={0} | all-to-all | bytes 524288 | tf_op jit(solution)/shard_map/all_to_all | solution.py:259
  132.7 0.0 all-gather.5.cloned.1.call-done.w_ref
  132.7 0.0 copy-start.2
  132.7 0.0 copy-start.3
  132.7 4.6 %project.1 = bf16[128,2048]{1,0:T(8,128)(2,1)} custom-call(bf16[8,128,128]{2,1,0:T(8,128)(2,1)} %bitcast.38, bf16[1024,2048]{1,0:T(8,128)(2,1)} %all-gather.5.cloned.1.call-done.w_ref), custom_call_target="tpu_custom_call" | custom-call | tf_op jit(solution)/shard_map/project/pallas_call | solution.py:204
  137.3 4.2 %all-to-all-start.2 = ((bf16[4,32,2048]{2,1,0:T(8,128)(2,1)}), bf16[4,32,2048]{2,1,0:T(8,128)(2,1)S(1)}, u32[]{:S(2)}, u32[]{:S(2)}) async-start(bf16[4,32,2048]{2,1,0:T(8,128)(2,1)} %bitcast.33), calls=%async_computation.2 | async-start | bytes 1048576 | tf_op jit(solution)/shard_map/all_to_all | solution.py:259
  141.5 0.0 copy-done.2
  141.5 0.0 copy-done.3
  141.5 0.1 select_reduce_fusion
  141.7 0.7 copy.28
  142.4 8.3 %all-to-all-done.2.parts_ref = bf16[4,32,2048]{2,1,0:T(8,128)(2,1)S(1)} async-done(((bf16[4,32,2048]{2,1,0:T(8,128)(2,1)}), bf16[4,32,2048]{2,1,0:T(8,128)(2,1)S(1)}, u32[]{:S(2)}, u32[]{:S(2)}) %all-to-all-start.2) | async-done | bytes 524320 | tf_op jit(solution)/shard_map/all_to_all | solution.py:259
  150.6 0.0 copy-start
  150.6 4.7 %all-to-all-start.4 = ((f32[16,32,2]{1,2,0:T(2,128)}), f32[16,32,2]{1,2,0:T(2,128)S(1)}, u32[]{:S(2)}, u32[]{:S(2)}) async-start(f32[16,32,2]{1,2,0:T(2,128)} %bitcast.13), calls=%async_computation.4 | async-start | bytes 32768 | tf_op jit(solution)/shard_map/all_to_all | solution.py:259
  155.4 0.0 copy-done
  155.4 2.8 %join.1 = (bf16[32,2048]{1,0:T(8,128)(2,1)}, bf16[16,32,2048]{2,1,0:T(8,128)(2,1)}) custom-call(bf16[4,32,2048]{2,1,0:T(8,128)(2,1)} %copy-done, bf16[32,2048]{1,0:T(8,128)(2,1)} %tokens_ref.3, f32[1,2048]{1,0:T(1,128)} %bitcast.41), custom_call_target="tpu_custom_call" | custom-call | tf_op jit(solution)/shard_map/join/pallas_call | solution.py:229
  158.2 3.5 %all-to-all-done.4 = f32[16,32,2]{1,2,0:T(2,128)S(1)} async-done(((f32[16,32,2]{1,2,0:T(2,128)}), f32[16,32,2]{1,2,0:T(2,128)S(1)}, u32[]{:S(2)}, u32[]{:S(2)}) %all-to-all-start.4) | async-done | bytes 4128 | tf_op jit(solution)/shard_map/all_to_all | solution.py:259
  161.7 5.0 %all-to-all-start.3 = ((bf16[16,32,2048]{2,1,0:T(8,128)(2,1)}), bf16[16,32,2048]{2,1,0:T(8,128)(2,1)S(1)}, u32[]{:S(2)}, u32[]{:S(2)}) async-start(bf16[16,32,2048]{2,1,0:T(8,128)(2,1)} %get-tuple-element.13), calls=%async_computation.3 | async-start | bytes 4194304 | tf_op jit(solution)/shard_map/all_to_all | solution.py:259
  166.6 0.0 collective-permute-start.1
  166.7 0.1 reshape.32
  166.8 25.7 %all-to-all-done.3 = bf16[16,32,2048]{2,1,0:T(8,128)(2,1)S(1)} async-done(((bf16[16,32,2048]{2,1,0:T(8,128)(2,1)}), bf16[16,32,2048]{2,1,0:T(8,128)(2,1)S(1)}, u32[]{:S(2)}, u32[]{:S(2)}) %all-to-all-start.3) | async-done | bytes 2097184 | tf_op jit(solution)/shard_map/all_to_all | solution.py:259
  192.5 0.0 copy-start.4
  192.5 4.7 %fusion.2 = f32[512,1024]{1,0:T(8,128)S(1)} fusion(bf16[512,2048]{1,0:T(8,128)(2,1)S(1)} %bitcast.34, bf16[1,2048,1024]{2,1,0:T(8,128)(2,1)} %param.28), kind=kOutput, calls=%fused_computation.2 | convolution fusion | flops 2147483648 | bytes 8388608 | tf_op jit(solution)/shard_map/dot_general | solution.py:264
  197.2 0.0 copy-done.4
  197.2 1.3 convolution_convert_fusion.1
  198.5 0.0 collective-permute-done
  198.5 4.5 %fusion = f32[512,1024]{1,0:T(8,128)S(1)} fusion(bf16[512,2048]{1,0:T(8,128)(2,1)S(1)} %bitcast.35, bf16[1,2048,1024]{2,1,0:T(8,128)(2,1)} %collective-permute-done), kind=kOutput, calls=%fused_computation | convolution fusion | flops 2147483648 | bytes 8388608 | tf_op jit(solution)/shard_map/dot_general | solution.py:264
  203.0 0.0 collective-permute-done.1
  203.0 3.0 %add_convert_fusion = bf16[512,2048]{1,0:T(8,128)(2,1)S(1)} fusion(bf16[512,2048]{1,0:T(8,128)(2,1)S(1)} %convolution_convert_fusion.1, bf16[1,512,2048]{2,1,0:T(8,128)(2,1)} %collective-permute-done.1, f32[512]{0:T(512)S(1)} %bitcast.43, f32[512]{0:T(512)S(1)} %bitcast.42, f32[512,1024]{1,0:T(8,128)S(1)} %fusion), kind=kOutput, calls=%fused_computation.4 | convolution fusion | flops 1082654720 | bytes 8392704 | tf_op jit(solution)/shard_map/dot_general | solution.py:266
  206.0 29.2 %all_to_all.32.parts_ref = bf16[16,32,2048]{2,1,0:T(8,128)(2,1)} all-to-all(bf16[16,32,2048]{2,1,0:T(8,128)(2,1)S(1)} %bitcast.36), channel_id=1, replica_groups=mesh['ctx'=8,'x'=4,'y'=4,'core'=2] {'x','y'}, dimensions={0} | all-to-all | bytes 4194304 | tf_op jit(solution)/shard_map/all_to_all | solution.py:259
  235.3 2.5 %total.1 = bf16[32,2048]{1,0:T(8,128)(2,1)} custom-call(bf16[16,32,2048]{2,1,0:T(8,128)(2,1)} %all_to_all.32.parts_ref), custom_call_target="tpu_custom_call" | custom-call | tf_op jit(solution)/shard_map/total/pallas_call | solution.py:247
  (2 shorter events, 0.0 us)
Async XLA Ops:
  7.2 56.8 %all-gather.7.cloned.1.call-start = ((), (), s32[]{:S(2)}) async-start(), calls=%async_computation.7 | async-start | bytes 6291456 | tf_op jit(solution)/shard_map/all_gather | solution.py:304
  43.8 0.9 copy-start.1
  43.9 88.8 %all-gather.5.cloned.1.call-start = ((), (), s32[]{:S(2)}) async-start(), calls=%async_computation.6 | async-start | bytes 4718592 | tf_op jit(solution)/shard_map/all_gather | solution.py:305
  44.6 153.9 %collective-permute-start = (bf16[1,2048,1024]{2,1,0:T(8,128)(2,1)}, bf16[1,2048,1024]{2,1,0:T(8,128)(2,1)}, u32[]{:S(2)}, u32[]{:S(2)}) collective-permute-start(bf16[1,2048,1024]{2,1,0:T(8,128)(2,1)} %param.28), channel_id=1, source_target_pairs={{0,1},{1,0},{2,3},{3,2},{4,5},{5,4},{6,7},{7,6},{8,9},{9,8},{10,11... | collective-permute-start | bytes 12582920 | tf_op jit(solution)/shard_map/ppermute | solution.py:255
  132.7 8.9 %copy-start.2 = (f32[32,10]{0,1:T(8,128)S(1)}, f32[32,10]{0,1:T(8,128)}, u32[]{:S(2)}) copy-start(f32[32,10]{0,1:T(8,128)} %param.27) | copy-start | bytes 3844
  132.7 8.9 %copy-start.3 = (s32[32,10]{0,1:T(8,128)S(1)}, s32[32,10]{0,1:T(8,128)}, u32[]{:S(2)}) copy-start(s32[32,10]{0,1:T(8,128)} %param.26) | copy-start | bytes 3844
  137.3 13.4 %all-to-all-start.2 = ((bf16[4,32,2048]{2,1,0:T(8,128)(2,1)}), bf16[4,32,2048]{2,1,0:T(8,128)(2,1)S(1)}, u32[]{:S(2)}, u32[]{:S(2)}) async-start(bf16[4,32,2048]{2,1,0:T(8,128)(2,1)} %bitcast.33), calls=%async_computation.2 | async-start | bytes 1048576 | tf_op jit(solution)/shard_map/all_to_all | solution.py:259
  150.6 4.7 %copy-start = (bf16[4,32,2048]{2,1,0:T(8,128)(2,1)}, bf16[4,32,2048]{2,1,0:T(8,128)(2,1)S(1)}, u32[]{:S(2)}) copy-start(bf16[4,32,2048]{2,1,0:T(8,128)(2,1)S(1)} %all-to-all-done.2.parts_ref) | copy-start | bytes 1572868
  150.6 11.0 %all-to-all-start.4 = ((f32[16,32,2]{1,2,0:T(2,128)}), f32[16,32,2]{1,2,0:T(2,128)S(1)}, u32[]{:S(2)}, u32[]{:S(2)}) async-start(f32[16,32,2]{1,2,0:T(2,128)} %bitcast.13), calls=%async_computation.4 | async-start | bytes 32768 | tf_op jit(solution)/shard_map/all_to_all | solution.py:259
  161.7 30.8 %all-to-all-start.3 = ((bf16[16,32,2048]{2,1,0:T(8,128)(2,1)}), bf16[16,32,2048]{2,1,0:T(8,128)(2,1)S(1)}, u32[]{:S(2)}, u32[]{:S(2)}) async-start(bf16[16,32,2048]{2,1,0:T(8,128)(2,1)} %get-tuple-element.13), calls=%async_computation.3 | async-start | bytes 4194304 | tf_op jit(solution)/shard_map/all_to_all | solution.py:259
  166.6 36.4 %collective-permute-start.1 = (bf16[1,512,2048]{2,1,0:T(8,128)(2,1)}, bf16[1,512,2048]{2,1,0:T(8,128)(2,1)}, u32[]{:S(2)}, u32[]{:S(2)}) collective-permute-start(bf16[1,512,2048]{2,1,0:T(8,128)(2,1)} %param.29), channel_id=1, source_target_pairs={{0,1},{1,0},{2,3},{3,2},{4,5},{5,4},{6,7},{7,6},{8,9},{9,8},{10,11... | collective-permute-start | bytes 6291464 | tf_op jit(solution)/shard_map/ppermute | solution.py:255
  192.5 4.7 %copy-start.4 = (bf16[1,512,2048]{2,1,0:T(8,128)(2,1)S(1)}, bf16[1,512,2048]{2,1,0:T(8,128)(2,1)}, u32[]{:S(2)}) copy-start(bf16[1,512,2048]{2,1,0:T(8,128)(2,1)} %param.29) | copy-start | bytes 6291460
Sparse Core Ops, SparseCore 0:
  44.0 19.9 all-gather.6
  65.8 34.9 all-gather.4

commit v2 on v1

v2 whole, which is shorter than its diff:
```python
import functools
import jax
import jax.numpy as jnp
from jax import lax
from jax.experimental import pallas as pl
from jax.experimental.pallas import tpu as pltpu
from jax.sharding import Mesh, PartitionSpec as P

EPSILON = 1e-06
F32 = jnp.float32
BF16 = jnp.bfloat16
CHUNK = 128
LANES = 128


def mm(a, b):
    return jnp.dot(a.astype(BF16), b.astype(BF16), preferred_element_type=F32)


def pieces(a):
    high = a.astype(BF16)
    rest = a - high.astype(F32)
    middle = rest.astype(BF16)
    low = (rest - middle.astype(F32)).astype(BF16)
    return high, middle, low


def rms_scale(values):
    return lax.rsqrt(jnp.mean(values * values, axis=-1, keepdims=True) + EPSILON)


def chunk_of(n):
    return slice(n * CHUNK, (n + 1) * CHUNK)


def resident():
    return pl.BlockSpec(memory_space=pltpu.VMEM)


def whole(shape):
    return pl.BlockSpec(shape, lambda i: (0,) * len(shape))


def project_rows(core, mine_ref, theirs_ref, w):
    groups, each, width = mine_ref.shape
    ours = jnp.dot(mine_ref[...].reshape(groups * each, width), w, preferred_element_type=F32)
    others = jnp.dot(theirs_ref[...].reshape(groups * each, width), w, preferred_element_type=F32)
    even = jnp.where(core == 0, ours, others)
    odd = jnp.where(core == 0, others, ours)
    rows = []
    for group in range(groups):
        at = slice(group * each, (group + 1) * each)
        rows += [even[at], odd[at]]
    return jnp.concatenate(rows, axis=0)


def maps_body(
    core_ref, scal_ref, mine_ref, theirs_ref, wk_ref, wv_ref, ws_ref,
    key_ref, decay_ref, growth_ref, solved_ref, start_ref, maps_ref, carry_ref,
    *, per_step,
):
    dim = wk_ref.shape[1]
    step = pl.program_id(0)

    @pl.when(step == 0)
    def _():
        rows = lax.broadcasted_iota(jnp.int32, (dim, 2 * dim), 0)
        cols = lax.broadcasted_iota(jnp.int32, (dim, 2 * dim), 1)
        carry_ref[...] = jnp.where(rows == cols, 1.0, 0.0).astype(F32)

    lift = scal_ref[0]
    rate = scal_ref[1]
    bias = scal_ref[2]
    rows = lax.broadcasted_iota(jnp.int32, (CHUNK, CHUNK), 0)
    cols = lax.broadcasted_iota(jnp.int32, (CHUNK, CHUNK), 1)
    differ = jnp.bitwise_xor(rows, cols)
    lower = rows >= cols
    strict = rows > cols
    lower_ones = jnp.where(lower, 1.0, 0.0).astype(BF16)
    eye = jnp.where(rows == cols, 1.0, 0.0).astype(F32)
    w_all = jnp.concatenate([wk_ref[...], wv_ref[...], ws_ref[...]], axis=1)
    projected = project_rows(core_ref[0], mine_ref, theirs_ref, w_all)
    logits = projected[:, 2 * dim:]
    every = range(per_step)
    key_raw = [projected[chunk_of(n), :dim] for n in every]
    value = [projected[chunk_of(n), dim:2 * dim] for n in every]
    strength = [jax.nn.sigmoid(logits[chunk_of(n), 0:1] + lift) for n in every]
    beta = [jnp.broadcast_to(s, (CHUNK, dim)) for s in strength]
    sums = []
    for n in every:
        moved = logits[chunk_of(n), 1:2] + bias
        softplus = jnp.maximum(moved, 0.0) + jnp.log1p(jnp.exp(-jnp.abs(moved)))
        high, middle, low = pieces(jnp.broadcast_to(-rate * softplus, (CHUNK, CHUNK)))
        sums.append(
            jnp.dot(lower_ones, high, preferred_element_type=F32)
            + jnp.dot(lower_ones, middle, preferred_element_type=F32)
            + jnp.dot(lower_ones, low, preferred_element_type=F32)
        )
    sums_t = [s.T for s in sums]
    key_vec = [
        k * lax.rsqrt(jnp.sum(k * k, axis=-1, keepdims=True) + EPSILON) for k in key_raw
    ]
    key_t = [k.T for k in key_vec]
    growth = [jnp.exp(s) for s in sums]
    fall = [jnp.exp(s[CHUNK - 1:CHUNK, :]) for s in sums]
    decay = [
        jnp.where(lower, jnp.exp(jnp.minimum(s - t, 0.0)), 0.0) for s, t in zip(sums, sums_t)
    ]
    gram = [mm(k, t) for k, t in zip(key_vec, key_t)]
    below = [
        jnp.where(strict, gram[n] * decay[n] * beta[n], 0.0) for n in every
    ]
    inverse = [eye - jnp.where(differ < 2, b, 0.0) for b in below]
    width = 2
    while width < CHUNK:
        ring = (differ >= width) & (differ < 2 * width)
        corner = [jnp.where(ring, b, 0.0) for b in below]
        half = [mm(inverse[n], corner[n]) for n in every]
        inverse = [inverse[n] - mm(half[n], inverse[n]) for n in every]
        width *= 2
    solved = [
        mm(
            inverse[n],
            jnp.concatenate([value[n] * beta[n], key_vec[n] * (beta[n] * growth[n])], axis=1),
        ).astype(BF16)
        for n in every
    ]
    tails = [jnp.exp(t[:, CHUNK - 1:CHUNK] - t) for t in sums_t]
    drive = [mm(key_t[n] * tails[n], solved[n]) for n in every]
    for n in every:
        key_ref[n] = key_t[n].astype(BF16)
        decay_ref[n] = decay[n]
        growth_ref[n] = growth[n]
        solved_ref[n] = solved[n]
    carried = carry_ref[...]
    for n in every:
        start_ref[n] = carried.astype(BF16)
        falls = jnp.concatenate([fall[n], fall[n]], axis=1)
        moved = falls * carried - mm(drive[n][:, dim:], carried)
        carried = jnp.concatenate([moved[:, :dim], moved[:, dim:] + drive[n][:, :dim]], axis=1)
    carry_ref[...] = carried
    maps_ref[...] = carried.astype(BF16)


def block_maps(core, scalars, mine, theirs, w, ws, dim, per_step):
    groups, each, width = mine.shape
    span = 2 * groups * each
    rows = per_step * CHUNK
    x_spec = pl.BlockSpec((rows // (2 * each), each, width), lambda i: (i, 0, 0))
    count = span // CHUNK

    def stacked(size):
        return pl.BlockSpec((per_step, CHUNK, size), lambda i: (i, 0, 0))

    return pl.pallas_call(
        functools.partial(maps_body, per_step=per_step),
        grid=(span // rows,),
        in_specs=[
            pl.BlockSpec(memory_space=pltpu.SMEM),
            pl.BlockSpec(memory_space=pltpu.SMEM),
            x_spec,
            x_spec,
            pl.BlockSpec((width, dim), lambda i: (0, 1)),
            pl.BlockSpec((width, dim), lambda i: (0, 2)),
            whole(ws.shape),
        ],
        out_specs=[
            stacked(CHUNK), stacked(CHUNK), stacked(dim), stacked(2 * dim), stacked(2 * dim),
            whole((dim, 2 * dim)),
        ],
        out_shape=[
            jax.ShapeDtypeStruct((count, dim, CHUNK), BF16),
            jax.ShapeDtypeStruct((count, CHUNK, CHUNK), F32),
            jax.ShapeDtypeStruct((count, CHUNK, dim), F32),
            jax.ShapeDtypeStruct((count, CHUNK, 2 * dim), BF16),
            jax.ShapeDtypeStruct((count, dim, 2 * dim), BF16),
            jax.ShapeDtypeStruct((dim, 2 * dim), BF16),
        ],
        scratch_shapes=[pltpu.VMEM((dim, 2 * dim), F32)],
        name="block_maps",
    )(core, scalars, mine, theirs, w, w, ws)


def reads_body(
    core_ref, mine_ref, theirs_ref, wq_ref, wg_ref, gain_ref, key_ref, decay_ref, growth_ref, solved_ref, start_ref,
    slope_ref, base_ref, gate_ref,
    *, per_step,
):
    dim = wq_ref.shape[1]
    w_pair = jnp.concatenate([wq_ref[...], wg_ref[...]], axis=1)
    projected = project_rows(core_ref[0], mine_ref, theirs_ref, w_pair)
    every = range(per_step)
    query = [projected[chunk_of(n), :dim] for n in every]
    scores = [mm(query[n], key_ref[n]) * decay_ref[n] for n in every]
    mixed = [mm(scores[n], solved_ref[n]) for n in every]
    both = [mm(query[n] * growth_ref[n] - mixed[n][:, dim:], start_ref[n]) for n in every]
    for n in every:
        slope_ref[chunk_of(n), :] = both[n][:, :dim].astype(BF16)
        base_ref[chunk_of(n), :] = both[n][:, dim:] + mixed[n][:, :dim]
    gate = projected[:, dim:]
    gate_ref[...] = gate * jax.nn.sigmoid(gate) * gain_ref[...]


def block_reads(core, mine, theirs, w, gain, parts, dim, per_step):
    key_t, decay, growth, solved, starts = parts
    groups, each, width = mine.shape
    span = 2 * groups * each
    rows = per_step * CHUNK
    x_spec = pl.BlockSpec((rows // (2 * each), each, width), lambda i: (i, 0, 0))

    def stacked(size):
        return pl.BlockSpec((per_step, CHUNK, size), lambda i: (i, 0, 0))

    by_rows = pl.BlockSpec((rows, dim), lambda i: (i, 0))
    return pl.pallas_call(
        functools.partial(reads_body, per_step=per_step),
        grid=(span // rows,),
        in_specs=[
            pl.BlockSpec(memory_space=pltpu.SMEM),
            x_spec,
            x_spec,
            pl.BlockSpec((width, dim), lambda i: (0, 0)),
            pl.BlockSpec((width, dim), lambda i: (0, 3)),
            whole((1, dim)),
            stacked(CHUNK), stacked(CHUNK), stacked(dim), stacked(2 * dim), stacked(2 * dim),
        ],
        out_specs=[by_rows, by_rows, by_rows],
        out_shape=[
            jax.ShapeDtypeStruct((span, dim), BF16),
            jax.ShapeDtypeStruct((span, dim), F32),
            jax.ShapeDtypeStruct((span, dim), F32),
        ],
        name="block_reads",
    )(core, mine, theirs, w, w, gain[None], key_t, decay, growth, solved, starts)


def norm_body(tokens_ref, gain_ref, out_ref):
    wide = tokens_ref[...].astype(F32)
    normed = (wide * rms_scale(wide) * gain_ref[...]).astype(BF16)
    out_ref[...] = jnp.broadcast_to(normed[None], out_ref.shape)


def norm_copies(tokens, gain, copies):
    return pl.pallas_call(
        norm_body,
        out_shape=jax.ShapeDtypeStruct((copies,) + tokens.shape, BF16),
        name="norm_copies",
    )(tokens, gain[None])


def emit_body(place_ref, maps_ref, init_ref, slope_ref, base_ref, gate_ref, out_ref, state_ref):
    dim = init_ref.shape[0]

    @pl.when(pl.program_id(0) == 0)
    def _():
        state = init_ref[...].T
        for block in range(maps_ref.shape[0] - 1):
            maps = maps_ref[block]
            moved = mm(maps[:, :dim], state) + maps[:, dim:].astype(F32)
            state = jnp.where(block < place_ref[0], moved, state)
        state_ref[...] = state

    head_raw = mm(slope_ref[...], state_ref[...]) + base_ref[...]
    gated = head_raw * rms_scale(head_raw) * gate_ref[...]
    out_ref[...] = gated.astype(BF16).reshape(out_ref.shape)


def emit(place, maps, init, slope, base, gate, outer, inner):
    span, dim = slope.shape
    rows = span // outer
    each = rows // inner
    by_rows = pl.BlockSpec((rows, dim), lambda i: (i, 0))
    return pl.pallas_call(
        emit_body,
        grid=(outer,),
        in_specs=[
            pl.BlockSpec(memory_space=pltpu.SMEM),
            resident(),
            whole(init.shape),
            by_rows,
            by_rows,
            by_rows,
        ],
        out_specs=pl.BlockSpec((inner, 1, each, dim), lambda i: (0, i, 0, 0)),
        out_shape=jax.ShapeDtypeStruct((inner, outer, each, dim), BF16),
        scratch_shapes=[pltpu.VMEM((dim, dim), F32)],
        name="emit",
    )(place, near(maps), init, slope, base, gate)


def project_body(place_ref, gated_ref, *refs):
    *w_refs, out_ref = refs
    core = place_ref[0]
    row = place_ref[1]
    count = len(w_refs) // 2
    left = []
    for at in range(2 * count):
        head = 2 * lax.rem(row + count - at % count, count)
        left.append(gated_ref[head + (core if at < count else 1 - core)])
    total = jnp.dot(
        jnp.concatenate(left, axis=1),
        jnp.concatenate([ref[...] for ref in w_refs], axis=0),
        preferred_element_type=F32,
    )
    out_ref[...] = total.astype(BF16)


def project(place, gated, weights, tile):
    heads, rows, dim = gated.shape
    width = weights[0].shape[1]
    w_spec = pl.BlockSpec((dim, tile), lambda i: (0, i))
    return pl.pallas_call(
        project_body,
        grid=(width // tile,),
        in_specs=[pl.BlockSpec(memory_space=pltpu.SMEM), resident()] + [w_spec] * heads,
        out_specs=pl.BlockSpec((rows, tile), lambda i: (0, i)),
        out_shape=jax.ShapeDtypeStruct((rows, width), BF16),
        name="project",
    )(place, near(gated), *weights)


def join_body(parts_ref, tokens_ref, gain_ref, routes_ref, out_ref, copies_ref):
    width = tokens_ref.shape[1]
    total = parts_ref[0].astype(F32)
    for part in range(1, parts_ref.shape[0]):
        total = total + parts_ref[part].astype(F32)
    summed = total.astype(BF16)
    out_ref[...] = summed
    hidden = tokens_ref[...].astype(F32) + summed.astype(F32)
    normed = (hidden * rms_scale(hidden) * gain_ref[...]).astype(BF16)
    copies = copies_ref.shape[0]
    copies_ref[:, :, :width] = jnp.broadcast_to(normed[None], (copies,) + normed.shape)
    copies_ref[:, :, width:] = routes_ref[...]


def join(parts, tokens, gain, routes):
    copies, rows, extra = routes.shape
    return pl.pallas_call(
        join_body,
        out_shape=[
            jax.ShapeDtypeStruct(tokens.shape, BF16),
            jax.ShapeDtypeStruct((copies, rows, tokens.shape[1] + extra), BF16),
        ],
        name="join",
    )(near(parts), tokens, gain[None], routes)


def experts_body(
    x_ref, gate_a_ref, up_a_ref, down_a_ref, gate_b_ref, up_b_ref, down_b_ref, out_ref,
    rows_ref, total_ref,
    *, tiles,
):
    step = pl.program_id(0)
    width = out_ref.shape[1]

    def tile(gate_ref, up_ref, down_ref):
        x = x_ref[:, :width]
        gate = jnp.dot(x, gate_ref[0], preferred_element_type=F32)
        up = jnp.dot(x, up_ref[0], preferred_element_type=F32)
        activated = (gate * jax.nn.sigmoid(gate) * up).astype(BF16)
        return jnp.dot(activated, down_ref[0], preferred_element_type=F32)

    def weight(which):
        extra = x_ref[:, width:].astype(F32)
        first = 3 * which
        return (
            extra[:, first:first + 1]
            + extra[:, first + 1:first + 2]
            + extra[:, first + 2:first + 3]
        )

    for which, refs in enumerate(
        ((gate_a_ref, up_a_ref, down_a_ref), (gate_b_ref, up_b_ref, down_b_ref))
    ):
        for part in range(tiles):

            @pl.when(step == which * tiles + part)
            def _(refs=refs, which=which, part=part):
                rows = tile(*refs)
                if part > 0:
                    rows = rows_ref[...] + rows
                if part < tiles - 1:
                    rows_ref[...] = rows
                else:
                    scaled = rows.astype(BF16).astype(F32) * weight(which)
                    if which == 0:
                        total_ref[...] = scaled
                    else:
                        out_ref[...] = (total_ref[...] + scaled).astype(BF16)


def experts_of(x, first, second, tiles):
    rows, wide = x.shape
    hidden_units, width = first[1].shape[1:]
    tile = hidden_units // tiles

    def specs(start):
        def at(i):
            return jnp.clip(i - start, 0, tiles - 1)

        return [
            pl.BlockSpec((1, width, tile), lambda i: (0, 0, at(i))),
            pl.BlockSpec((1, width, tile), lambda i: (0, 0, tiles + at(i))),
            pl.BlockSpec((1, tile, width), lambda i: (0, at(i), 0)),
        ]

    return pl.pallas_call(
        functools.partial(experts_body, tiles=tiles),
        grid=(2 * tiles,),
        in_specs=[resident()] + specs(0) + specs(tiles),
        out_specs=whole((rows, width)),
        out_shape=jax.ShapeDtypeStruct((rows, width), BF16),
        scratch_shapes=[pltpu.VMEM((rows, width), F32), pltpu.VMEM((rows, width), F32)],
        name="experts",
    )(near(x), first[0], first[0], first[1], second[0], second[0], second[1])


def total_body(parts_ref, out_ref):
    total = parts_ref[0].astype(F32)
    for part in range(1, parts_ref.shape[0]):
        total = total + parts_ref[part].astype(F32)
    out_ref[...] = total.astype(BF16)


def total_of(parts):
    return pl.pallas_call(
        total_body,
        out_shape=jax.ShapeDtypeStruct(parts.shape[1:], BF16),
        name="total",
    )(near(parts))


def shift_y(value, steps):
    count = lax.axis_size("y")
    return lax.ppermute(value, "y", [(at, (at + steps) % count) for at in range(count)])


def near(value):
    return pltpu.with_memory_space_constraint(value, pltpu.VMEM)


def swap_cores(value):
    return lax.ppermute(value, "core", [(0, 1), (1, 0)])


def exchange(value, axes):
    return lax.all_to_all(value, axes, split_axis=0, concat_axis=0, tiled=True)


def shards(
    tokens,
    gain_in,
    w_heads,
    w_scalar,
    strength_bias,
    decay_rate,
    decay_bias,
    state_init,
    gain_head,
    w_output,
    gain_expert,
    expert_ids,
    gate_weights,
    w_gate_up,
    w_down,
):
    tok_dev, width = tokens.shape
    dim = state_init.shape[-1]
    x_count, y_count, core_count = (lax.axis_size(axis) for axis in ("x", "y", "core"))
    ctx_count = lax.axis_size("ctx")
    chips = x_count * y_count
    expert_total = chips * core_count
    core = lax.axis_index("core").astype(jnp.int32)
    place = lax.axis_index("ctx").astype(jnp.int32)

    copies = norm_copies(tokens, gain_in, chips)
    mine = exchange(copies, ("x", "y"))
    theirs = swap_cores(mine)
    w_here, _ = lax.optimization_barrier((w_output, mine))
    w_rows = [w_here] + [shift_y(w_here, steps) for steps in range(1, y_count)]

    scalars = jnp.concatenate([strength_bias, decay_rate, decay_bias])
    w_logit = jnp.pad(w_scalar, ((0, 0), (0, LANES - w_scalar.shape[1])))
    *parts, maps = block_maps(core[None], scalars, mine, theirs, w_heads, w_logit, dim, PER_STEP)
    maps = jnp.broadcast_to(maps[None], (ctx_count,) + maps.shape)
    all_maps = exchange(maps, "ctx")
    slope, base, gate = block_reads(core[None], mine, theirs, w_heads, gain_head, parts, dim, PER_STEP)
    *w_rows, slope = lax.optimization_barrier((*w_rows, slope))
    w_rows = w_rows + [swap_cores(rows) for rows in w_rows]
    gated = emit(
        place[None], all_maps, state_init[0], slope, base, gate, x_count, y_count * core_count
    )
    heads = y_count * core_count
    gated = exchange(gated, ("y", "core")).reshape(heads, x_count * tok_dev, dim)
    partial = project(jnp.stack([core, lax.axis_index("y").astype(jnp.int32)]), gated, w_rows, 512).reshape(x_count, tok_dev, width)

    other_gate_up = swap_cores(w_gate_up)
    other_down = swap_cores(w_down)
    numbers = jnp.arange(expert_total, dtype=jnp.int32)
    named = expert_ids[:, :, None] == numbers[None, None, :]
    routes = jnp.sum(jnp.where(named, gate_weights[:, :, None], 0.0), axis=1)
    routes = routes.reshape(tok_dev, chips, core_count).transpose(1, 0, 2)
    routes = jnp.where(core == 0, routes, routes[:, :, ::-1])
    routes = jnp.stack(pieces(routes), axis=-1).reshape(chips, tok_dev, -1)
    routes = jnp.pad(routes, ((0, 0), (0, 0), (0, LANES - routes.shape[-1])))

    summed, copies = join(exchange(partial, "x"), tokens, gain_expert, routes)
    received = exchange(copies, ("x", "y")).reshape(chips * tok_dev, -1)
    outputs = experts_of(received, (w_gate_up, w_down), (other_gate_up, other_down), 2)
    outputs = outputs.reshape(chips, tok_dev, width)
    expert_out = total_of(exchange(outputs, ("x", "y")))
    return (summed, expert_out)


PER_STEP = 4


def solution(mesh):
    fine = Mesh(mesh.devices.reshape(mesh.shape["ctx"], 4, 4, 2), ("ctx", "x", "y", "core"))
    exp = ("x", "y", "core")
    rows = ("ctx", "x", "y", "core")
    return jax.shard_map(
        shards,
        mesh=fine,
        in_specs=(
            P(rows, None),
            P(),
            P(None, exp),
            P(None, exp),
            P(exp),
            P(exp),
            P(exp),
            P(exp, None, None),
            P(),
            P(exp, None),
            P(),
            P(rows, None),
            P(rows, None),
            P(exp, None, None),
            P(exp, None, None),
        ),
        out_specs=(P(rows, None), P(rows, None)),
        check_vma=False,
    )
```

time: 245 us -> 208 us (0.85)
  blocking collectives: 103 us -> 63.8 us
  starting transfers between devices: 14.1 us -> 28.4 us
  matrix products: 13.5 us -> 0 us
  between operations: 16.1 us -> 2.74 us
  waiting for transfers between devices: 53.7 us -> 61.4 us
  Pallas kernels: 41.1 us -> 44.3 us
    all_gather x1 -> x0, blocking collectives: 28.9 us -> none  [shards(): all_maps = lax.all_gather(maps, 'ctx', axis=0, tiled=False)]
    ppermute x0 -> x3, waiting for transfers between devices: none -> 16.8 us  [shift_y(): lax.ppermute(value, 'y', [(at, (at + steps) % count) for at in range(coun...]
    all_gather x2 -> x0, waiting for transfers between devices: 15.5 us -> none  [the longest x1 15.5 us: shards(): lax.all_gather(mine, 'core', axis=1, tiled=False).reshape(span, width)]
    dot_general x4 -> x0, matrix products: 13.5 us -> none  [the longest x2 9.18 us: expert(): pre = jnp.dot(x, w_gate_up, preferred_element_type=F32)]
    all_to_all x3 -> x2, blocking collectives: 74.3 us -> 63.8 us  [exchange(): return lax.all_to_all(value, axes, split_axis=0, concat_axis=0, tiled=True)]
    all_to_all x3 -> x4, starting transfers between devices: 13.9 us -> 22.5 us  [exchange(): return lax.all_to_all(value, axes, split_axis=0, concat_axis=0, tiled=True)]
    pallas_call x1 -> x3, Pallas kernels: 23.6 us -> 28.7 us  [the longest x1 12 us: experts_of(): pl.pallas_call(functools.partial(experts_body, tiles=tiles), grid=(2 * ti...]
    all_to_all x3 -> x4, waiting for transfers between devices: 37.5 us -> 41.8 us  [exchange(): return lax.all_to_all(value, axes, split_axis=0, concat_axis=0, tiled=True)]
  transfers between devices with their start and end apart: 7 -> 14, of which waited for: 4 -> 7; matrix products, arithmetic and copies ran while one was open for 5% -> 3% of each run, Pallas kernels for 15% -> 14%
where the time goes in v2:
time: 208 us; the launch traced here: 206 us
  blocking collectives  63.8 us (31%)
  waiting for transfers between devices  61.4 us (30%)
  Pallas kernels  44.3 us (21%)
  starting transfers between devices  28.4 us (14%)
  local copies, waits for them, and re-layouts  4.01 us (2%)
  between operations  2.74 us (1%)
    all_to_all x2, blocking collectives, exchange(): return lax.all_to_all(value, axes, split_axis=0, concat_axis=0, tiled=True)  63.8 us
    all_to_all x4, waiting for transfers between devices, exchange(): return lax.all_to_all(value, axes, split_axis=0, concat_axis=0, tiled=True)  41.8 us
    all_to_all x4, starting transfers between devices, exchange(): return lax.all_to_all(value, axes, split_axis=0, concat_axis=0, tiled=True)  22.5 us
    ppermute x3, waiting for transfers between devices, shift_y(): lax.ppermute(value, 'y', [(at, (at + steps) % count) for at in range(coun...  16.8 us
    pallas_call x1, Pallas kernels, experts_of(): pl.pallas_call(functools.partial(experts_body, tiles=tiles), grid=(2 * ti...  12 us
    pallas_call x1, Pallas kernels, block_maps(): pl.pallas_call(functools.partial(maps_body, per_step=per_step), grid=(spa...  10.9 us
    pallas_call x1, Pallas kernels, block_reads(): pl.pallas_call(functools.partial(reads_body, per_step=per_step), grid=(sp...  5.79 us
    pallas_call x1, Pallas kernels, emit(): pl.pallas_call(emit_body, grid=(outer,), in_specs=[pl.BlockSpec(memory_sp...  4.91 us
  transfers between devices with their start and end apart: 14, of which 7 were waited for; matrix products, arithmetic and copies ran while one was open for 3% of the time, Pallas kernels for 14%

profile of v2, /device:TPU:8, one launch (start us, length us, event | category | flops | bytes accessed | tf_op | source)
XLA Modules:
  0.0 206.1 jit_solution(6766989164694905157)
XLA Ops:
  0.6 2.5 %norm_copies.1 = bf16[16,32,2048]{2,1,0:T(8,128)(2,1)} custom-call(bf16[32,2048]{1,0:T(8,128)(2,1)} %tokens_ref.3, f32[1,2048]{1,0:T(1,128)} %bitcast.29), custom_call_target="tpu_custom_call" | custom-call | tf_op jit(solution)/shard_map/norm_copies/pallas_call | solution.py:244
  3.1 34.1 %all_to_all.30.mine_ref = bf16[16,32,2048]{2,1,0:T(8,128)(2,1)S(1)} all-to-all(bf16[16,32,2048]{2,1,0:T(8,128)(2,1)} %norm_copies.1), channel_id=1, replica_groups=mesh['ctx'=8,'x'=4,'y'=4,'core'=2] {'x','y'}, dimensions={0} | all-to-all | bytes 4194304 | tf_op jit(solution)/shard_map/all_to_all | solution.py:447
  37.3 0.0 collective-permute-start
  37.3 0.5 collective-permute-start.8
  39.8 0.3 copy.29
  40.1 1.0 pad.8.ws_ref
  41.1 0.7 pad_maximum_fusion.1.scal_ref
  41.7 2.8 %collective-permute-done.theirs_ref = bf16[16,32,2048]{2,1,0:T(8,128)(2,1)} collective-permute-done((bf16[16,32,2048]{2,1,0:T(8,128)(2,1)S(1)}, bf16[16,32,2048]{2,1,0:T(8,128)(2,1)}, u32[]{:S(2)}, u32[]{:S(2)}) %collective-permute-start) | collective-permute-done | bytes 2097184 | tf_op jit(solution)/shard_map/ppermute | solution.py:443
  44.5 10.9 %block_maps.1 = (bf16[8,128,128]{2,1,0:T(8,128)(2,1)}, f32[8,128,128]{2,1,0:T(8,128)}, f32[8,128,128]{2,1,0:T(8,128)}, bf16[8,128,256]{2,1,0:T(8,128)(2,1)}, bf1...) custom-call(s32[1]{0:T(128)} %bitcast.core_ref, f32[3]{0:T(128)} %pad_maximum_fusion.1.scal_ref, ...), custom_call_target="tpu_custom_call" | custom-call | tf_op jit(solution)/shard_map/block_maps/pallas_call | solution.py:155
  55.4 1.7 broadcast_in_dim.37
  57.1 8.5 %all-to-all-start.1 = ((bf16[8,128,256]{2,1,0:T(8,128)(2,1)}), bf16[8,128,256]{2,1,0:T(8,128)(2,1)S(1)}, u32[]{:S(2)}, u32[]{:S(2)}) async-start(bf16[8,128,256]{2,1,0:T(8,128)(2,1)} %broadcast_in_dim.37), calls=%async_computation.1 | async-start | bytes 1048576 | tf_op jit(solution)/shard_map/all_to_all | solution.py:447
  65.6 1.8 collective-permute-start.3
  67.4 0.9 collective-permute-start.2
  68.2 1.6 collective-permute-start.1
  69.8 5.8 %block_reads.1 = (bf16[1024,128]{1,0:T(8,128)(2,1)}, f32[1024,128]{1,0:T(8,128)}, f32[1024,128]{1,0:T(8,128)}) custom-call(s32[1]{0:T(128)} %bitcast.core_ref, bf16[16,32,2048]{2,1,0:T(8,128)(2,1)} %copy-done, bf16[16,32,2048]{2,1,0:T(8,128)(2,1)} %collective-permute-done.theirs_ref, bf16[2048,512]{1,0:T(8,128)(2,1)} %wg_ref.1, bf16[2048,512]{1,0:T(8,128)(2,1)} %wg_ref.1, ...), custom_call_target="tpu_custom_call" | custom-call | tf_op jit(solution)/shard_map/block_reads/pallas_call | solution.py:215
  75.6 0.0 copy-start.8
  75.6 4.3 %collective-permute-done.3.refs_3_ = bf16[128,2048]{1,0:T(8,128)(2,1)S(1)} collective-permute-done((bf16[128,2048]{1,0:T(8,128)(2,1)S(1)}, bf16[128,2048]{1,0:T(8,128)(2,1)S(1)}, u32[]{:S(2)}, u32[]{:S(2)}) %collective-permute-start.3) | collective-permute-done | bytes 524320 | tf_op jit(solution)/shard_map/ppermute | solution.py:435
  79.9 11.2 %collective-permute-done.2.refs_2_ = bf16[128,2048]{1,0:T(8,128)(2,1)S(1)} collective-permute-done((bf16[128,2048]{1,0:T(8,128)(2,1)S(1)}, bf16[128,2048]{1,0:T(8,128)(2,1)S(1)}, u32[]{:S(2)}, u32[]{:S(2)}) %collective-permute-start.2) | collective-permute-done | bytes 524320 | tf_op jit(solution)/shard_map/ppermute | solution.py:435
  91.1 1.3 collective-permute-done.1.refs_1_
  92.4 0.0 collective-permute-start.4
  92.4 0.5 collective-permute-start.5
  92.9 0.0 collective-permute-start.6
  92.9 0.5 collective-permute-start.7
  93.4 0.0 all-to-all-done.1.maps_ref
  93.4 4.9 %emit.1 = bf16[8,4,32,128]{3,2,1,0:T(8,128)(2,1)} custom-call(s32[1]{0:T(128)} %bitcast.2.place_ref, bf16[8,128,256]{2,1,0:T(8,128)(2,1)S(1)} %all-to-all-done.1.maps_ref, f32[128,128]{1,0:T(8,128)} %bitcast.28, bf16[1024,128]{1,0:T(8,128)(2,1)} %get-tuple-element.27.slope_ref, f32[1024,128]{1,0:T(8,128)} %get-tuple-element.28.base_ref, ...), custom_call_target="tpu_custom_call" | custom-call | tf_op jit(solution)/shard_map/emit/pallas_call | solution.py:273
  98.3 5.4 %all-to-all-start.2 = ((bf16[8,4,32,128]{3,2,1,0:T(8,128)(2,1)}), bf16[8,4,32,128]{3,2,1,0:T(8,128)(2,1)S(1)}, u32[]{:S(2)}, u32[]{:S(2)}) async-start(bf16[8,4,32,128]{3,2,1,0:T(8,128)(2,1)} %emit.1), calls=%async_computation.2 | async-start | bytes 524288 | tf_op jit(solution)/shard_map/all_to_all | solution.py:447
  103.8 0.2 select_reduce_fusion
  103.9 0.1 copy.30
  104.0 0.6 pad_add_fusion.place_ref
  104.7 0.0 collective-permute-done.4.refs_4_
  104.7 0.1 collective-permute-start.9
  104.8 0.0 collective-permute-done.5.refs_5_
  104.8 0.0 collective-permute-done.6.refs_6_
  104.8 0.0 collective-permute-done.7.refs_7_
  104.8 5.0 %all-to-all-done.2 = bf16[8,4,32,128]{3,2,1,0:T(8,128)(2,1)S(1)} async-done(((bf16[8,4,32,128]{3,2,1,0:T(8,128)(2,1)}), bf16[8,4,32,128]{3,2,1,0:T(8,128)(2,1)S(1)}, u32[]{:S(2)}, u32[]{:S(2)}) %all-to-all-start.2) | async-done | bytes 262176 | tf_op jit(solution)/shard_map/all_to_all | solution.py:447
  109.9 4.6 %project.1 = bf16[128,2048]{1,0:T(8,128)(2,1)} custom-call(s32[2]{0:T(128)} %pad_add_fusion.place_ref, bf16[8,128,128]{2,1,0:T(8,128)(2,1)S(1)} %bitcast.22, bf16[128,2048]{1,0:T(8,128)(2,1)} %refs_0_, bf16[128,2048]{1,0:T(8,128)(2,1)} %copy-done.4, bf16[128,2048]{1,0:T(8,128)(2,1)} %copy-done.3, bf16[128,2048]{1,0:T(8,128)(2,1)} %copy-done.2, ...), custom_call_target="tpu_custom_call" | custom-call | tf_op jit(solution)/shard_map/project/pallas_call | solution.py:312
  114.5 3.6 %all-to-all-start.3 = ((bf16[4,32,2048]{2,1,0:T(8,128)(2,1)}), bf16[4,32,2048]{2,1,0:T(8,128)(2,1)S(1)}, u32[]{:S(2)}, u32[]{:S(2)}) async-start(bf16[4,32,2048]{2,1,0:T(8,128)(2,1)} %bitcast.24), calls=%async_computation.3 | async-start | bytes 1048576 | tf_op jit(solution)/shard_map/all_to_all | solution.py:447
  118.2 0.2 copy.34
  118.5 0.7 pad.9.routes_ref
  119.1 8.2 %all-to-all-done.3.parts_ref = bf16[4,32,2048]{2,1,0:T(8,128)(2,1)S(1)} async-done(((bf16[4,32,2048]{2,1,0:T(8,128)(2,1)}), bf16[4,32,2048]{2,1,0:T(8,128)(2,1)S(1)}, u32[]{:S(2)}, u32[]{:S(2)}) %all-to-all-start.3) | async-done | bytes 524320 | tf_op jit(solution)/shard_map/all_to_all | solution.py:447
  127.3 2.7 %join.1 = (bf16[32,2048]{1,0:T(8,128)(2,1)}, bf16[16,32,2176]{2,1,0:T(8,128)(2,1)}) custom-call(bf16[4,32,2048]{2,1,0:T(8,128)(2,1)S(1)} %all-to-all-done.3.parts_ref, bf16[32,2048]{1,0:T(8,128)(2,1)} %tokens_ref.3, f32[1,2048]{1,0:T(1,128)} %bitcast.30, bf16[16,32,128]{2,1,0:T(8,128)(2,1)} %pad.9.routes_ref), custom_call_target="tpu_custom_call" | custom-call | tf_op jit(solution)/shard_map/join/pallas_call | solution.py:338
  130.0 5.0 %all-to-all-start.4 = ((bf16[16,32,2176]{2,1,0:T(8,128)(2,1)}), bf16[16,32,2176]{2,1,0:T(8,128)(2,1)S(1)}, u32[]{:S(2)}, u32[]{:S(2)}) async-start(bf16[16,32,2176]{2,1,0:T(8,128)(2,1)} %get-tuple-element.35), calls=%async_computation.4 | async-start | bytes 4456448 | tf_op jit(solution)/shard_map/all_to_all | solution.py:447
  135.0 0.0 collective-permute-done.9.down_b_ref
  135.0 0.0 collective-permute-done.8.gate_b_ref.up_b_ref
  135.0 28.7 %all-to-all-done.4 = bf16[16,32,2176]{2,1,0:T(8,128)(2,1)S(1)} async-done(((bf16[16,32,2176]{2,1,0:T(8,128)(2,1)}), bf16[16,32,2176]{2,1,0:T(8,128)(2,1)S(1)}, u32[]{:S(2)}, u32[]{:S(2)}) %all-to-all-start.4) | async-done | bytes 2228256 | tf_op jit(solution)/shard_map/all_to_all | solution.py:447
  163.6 12.0 %experts.1 = bf16[512,2048]{1,0:T(8,128)(2,1)} custom-call(bf16[512,2176]{1,0:T(8,128)(2,1)S(1)} %bitcast.21, bf16[1,2048,1024]{2,1,0:T(8,128)(2,1)} %up_a_ref.1, bf16[1,2048,1024]{2,1,0:T(8,128)(2,1)} %up_a_ref.1, bf16[1,512,2048]{2,1,0:T(8,128)(2,1)} %down_a_ref.1, bf16[1,2048,1024]{2,1,0:T(8,128)(2,1)} %collective-permute-done.8.gate_b_ref.up_b_ref, ...), custom_call_target="tpu_custom_call" | custom-call | tf_op jit(solution)/shard_map/experts/pallas_call | solution.py:407
  175.6 29.6 %all_to_all.31.parts_ref = bf16[16,32,2048]{2,1,0:T(8,128)(2,1)S(1)} all-to-all(bf16[16,32,2048]{2,1,0:T(8,128)(2,1)} %bitcast.23), channel_id=1, replica_groups=mesh['ctx'=8,'x'=4,'y'=4,'core'=2] {'x','y'}, dimensions={0} | all-to-all | bytes 4194304 | tf_op jit(solution)/shard_map/all_to_all | solution.py:447
  205.2 0.9 total.1
  (22 shorter events, 0.2 us)
Async XLA Ops:
  3.1 36.6 %copy-start.6 = (bf16[2048,2]{0,1:T(2,128)(2,1)S(1)}, bf16[2048,2]{0,1:T(2,128)(2,1)}, u32[]{:S(2)}) copy-start(bf16[2048,2]{0,1:T(2,128)(2,1)} %param.18) | copy-start | bytes 24580
  37.3 7.3 %copy-start = (bf16[16,32,2048]{2,1,0:T(8,128)(2,1)}, bf16[16,32,2048]{2,1,0:T(8,128)(2,1)S(1)}, u32[]{:S(2)}) copy-start(bf16[16,32,2048]{2,1,0:T(8,128)(2,1)S(1)} %all_to_all.30.mine_ref) | copy-start | bytes 6291460
  37.3 7.3 %collective-permute-start = (bf16[16,32,2048]{2,1,0:T(8,128)(2,1)S(1)}, bf16[16,32,2048]{2,1,0:T(8,128)(2,1)}, u32[]{:S(2)}, u32[]{:S(2)}) collective-permute-start(bf16[16,32,2048]{2,1,0:T(8,128)(2,1)S(1)} %all_to_all.30.mine_ref), channel_id=1, source_target_pairs={{0,1},{1,0},{2,3},{3,2},{4,5},{5,4},{6,7},{7,6},{8,9},{9,8},{10,11... | collective-permute-start | bytes 6291464 | tf_op jit(solution)/shard_map/ppermute | solution.py:443
  37.3 97.7 %collective-permute-start.8 = (bf16[1,2048,1024]{2,1,0:T(8,128)(2,1)}, bf16[1,2048,1024]{2,1,0:T(8,128)(2,1)}, u32[]{:S(2)}, u32[]{:S(2)}) collective-permute-start(bf16[1,2048,1024]{2,1,0:T(8,128)(2,1)} %up_a_ref.1), channel_id=1, source_target_pairs={{0,1},{1,0},{2,3},{3,2},{4,5},{5,4},{6,7},{7,6},{8,9},{9,8},{10,11... | collective-permute-start | bytes 12582920 | tf_op jit(solution)/shard_map/ppermute | solution.py:443
  44.5 21.1 %copy-start.1 = (bf16[128,2048]{1,0:T(8,128)(2,1)S(1)}, bf16[128,2048]{1,0:T(8,128)(2,1)}, u32[]{:S(2)}) copy-start(bf16[128,2048]{1,0:T(8,128)(2,1)} %refs_0_) | copy-start | bytes 1572868
  57.1 36.3 %all-to-all-start.1 = ((bf16[8,128,256]{2,1,0:T(8,128)(2,1)}), bf16[8,128,256]{2,1,0:T(8,128)(2,1)S(1)}, u32[]{:S(2)}, u32[]{:S(2)}) async-start(bf16[8,128,256]{2,1,0:T(8,128)(2,1)} %broadcast_in_dim.37), calls=%async_computation.1 | async-start | bytes 1048576 | tf_op jit(solution)/shard_map/all_to_all | solution.py:447
  65.6 14.3 %collective-permute-start.3 = (bf16[128,2048]{1,0:T(8,128)(2,1)S(1)}, bf16[128,2048]{1,0:T(8,128)(2,1)S(1)}, u32[]{:S(2)}, u32[]{:S(2)}) collective-permute-start(bf16[128,2048]{1,0:T(8,128)(2,1)S(1)} %copy-done.1), channel_id=1, source_target_pairs={{0,6},{2,0},{4,2},{6,4},{1,7},{3,1},{5,3},{7,5},{8,14},{10,8},{12,... | collective-permute-start | bytes 1572872 | tf_op jit(solution)/shard_map/ppermute | solution.py:435
  67.4 23.8 %collective-permute-start.2 = (bf16[128,2048]{1,0:T(8,128)(2,1)S(1)}, bf16[128,2048]{1,0:T(8,128)(2,1)S(1)}, u32[]{:S(2)}, u32[]{:S(2)}) collective-permute-start(bf16[128,2048]{1,0:T(8,128)(2,1)S(1)} %copy-done.1), channel_id=1, source_target_pairs={{0,4},{2,6},{4,0},{6,2},{1,5},{3,7},{5,1},{7,3},{8,12},{10,14},{12... | collective-permute-start | bytes 1572872 | tf_op jit(solution)/shard_map/ppermute | solution.py:435
  68.2 24.2 %collective-permute-start.1 = (bf16[128,2048]{1,0:T(8,128)(2,1)S(1)}, bf16[128,2048]{1,0:T(8,128)(2,1)S(1)}, u32[]{:S(2)}, u32[]{:S(2)}) collective-permute-start(bf16[128,2048]{1,0:T(8,128)(2,1)S(1)} %copy-done.1), channel_id=1, source_target_pairs={{0,2},{2,4},{4,6},{6,0},{1,3},{3,5},{5,7},{7,1},{8,10},{10,12},{12... | collective-permute-start | bytes 1572872 | tf_op jit(solution)/shard_map/ppermute | solution.py:435
  75.6 28.1 %copy-start.7 = (f32[32,10]{0,1:T(8,128)S(1)}, f32[32,10]{0,1:T(8,128)}, u32[]{:S(2)}) copy-start(f32[32,10]{0,1:T(8,128)} %param.27) | copy-start | bytes 3844
  75.6 28.1 %copy-start.8 = (s32[32,10]{0,1:T(8,128)S(1)}, s32[32,10]{0,1:T(8,128)}, u32[]{:S(2)}) copy-start(s32[32,10]{0,1:T(8,128)} %param.26) | copy-start | bytes 3844
  79.9 29.9 %copy-start.2 = (bf16[128,2048]{1,0:T(8,128)(2,1)}, bf16[128,2048]{1,0:T(8,128)(2,1)S(1)}, u32[]{:S(2)}) copy-start(bf16[128,2048]{1,0:T(8,128)(2,1)S(1)} %collective-permute-done.3.refs_3_) | copy-start | bytes 1572868
  91.1 18.7 %copy-start.3 = (bf16[128,2048]{1,0:T(8,128)(2,1)}, bf16[128,2048]{1,0:T(8,128)(2,1)S(1)}, u32[]{:S(2)}) copy-start(bf16[128,2048]{1,0:T(8,128)(2,1)S(1)} %collective-permute-done.2.refs_2_) | copy-start | bytes 1572868
  92.4 17.5 %copy-start.4 = (bf16[128,2048]{1,0:T(8,128)(2,1)}, bf16[128,2048]{1,0:T(8,128)(2,1)S(1)}, u32[]{:S(2)}) copy-start(bf16[128,2048]{1,0:T(8,128)(2,1)S(1)} %collective-permute-done.1.refs_1_) | copy-start | bytes 1572868
  92.4 12.2 %collective-permute-start.4 = (bf16[128,2048]{1,0:T(8,128)(2,1)S(1)}, bf16[128,2048]{1,0:T(8,128)(2,1)S(1)}, u32[]{:S(2)}, u32[]{:S(2)}) collective-permute-start(bf16[128,2048]{1,0:T(8,128)(2,1)S(1)} %copy-done.1), channel_id=1, source_target_pairs={{0,1},{1,0},{2,3},{3,2},{4,5},{5,4},{6,7},{7,6},{8,9},{9,8},{10,11... | collective-permute-start | bytes 1572872 | tf_op jit(solution)/shard_map/ppermute | solution.py:443
  92.4 12.4 %collective-permute-start.5 = (bf16[128,2048]{1,0:T(8,128)(2,1)S(1)}, bf16[128,2048]{1,0:T(8,128)(2,1)}, u32[]{:S(2)}, u32[]{:S(2)}) collective-permute-start(bf16[128,2048]{1,0:T(8,128)(2,1)S(1)} %collective-permute-done.1.refs_1_), channel_id=1, source_target_pairs={{0,1},{1,0},{2,3},{3,2},{4,5},{5,4},{6,7},{7,6},{8,9},{9,8},{10,11... | collective-permute-start | bytes 1572872 | tf_op jit(solution)/shard_map/ppermute | solution.py:443
  92.9 11.9 %collective-permute-start.6 = (bf16[128,2048]{1,0:T(8,128)(2,1)S(1)}, bf16[128,2048]{1,0:T(8,128)(2,1)}, u32[]{:S(2)}, u32[]{:S(2)}) collective-permute-start(bf16[128,2048]{1,0:T(8,128)(2,1)S(1)} %collective-permute-done.2.refs_2_), channel_id=1, source_target_pairs={{0,1},{1,0},{2,3},{3,2},{4,5},{5,4},{6,7},{7,6},{8,9},{9,8},{10,11... | collective-permute-start | bytes 1572872 | tf_op jit(solution)/shard_map/ppermute | solution.py:443
  92.9 11.9 %collective-permute-start.7 = (bf16[128,2048]{1,0:T(8,128)(2,1)S(1)}, bf16[128,2048]{1,0:T(8,128)(2,1)}, u32[]{:S(2)}, u32[]{:S(2)}) collective-permute-start(bf16[128,2048]{1,0:T(8,128)(2,1)S(1)} %collective-permute-done.3.refs_3_), channel_id=1, source_target_pairs={{0,1},{1,0},{2,3},{3,2},{4,5},{5,4},{6,7},{7,6},{8,9},{9,8},{10,11... | collective-permute-start | bytes 1572872 | tf_op jit(solution)/shard_map/ppermute | solution.py:443
  98.3 11.5 %all-to-all-start.2 = ((bf16[8,4,32,128]{3,2,1,0:T(8,128)(2,1)}), bf16[8,4,32,128]{3,2,1,0:T(8,128)(2,1)S(1)}, u32[]{:S(2)}, u32[]{:S(2)}) async-start(bf16[8,4,32,128]{3,2,1,0:T(8,128)(2,1)} %emit.1), calls=%async_computation.2 | async-start | bytes 524288 | tf_op jit(solution)/shard_map/all_to_all | solution.py:447
  104.7 5.2 %copy-start.5 = (bf16[128,2048]{1,0:T(8,128)(2,1)}, bf16[128,2048]{1,0:T(8,128)(2,1)S(1)}, u32[]{:S(2)}) copy-start(bf16[128,2048]{1,0:T(8,128)(2,1)S(1)} %collective-permute-done.4.refs_4_) | copy-start | bytes 1572868
  104.7 30.3 %collective-permute-start.9 = (bf16[1,512,2048]{2,1,0:T(8,128)(2,1)}, bf16[1,512,2048]{2,1,0:T(8,128)(2,1)}, u32[]{:S(2)}, u32[]{:S(2)}) collective-permute-start(bf16[1,512,2048]{2,1,0:T(8,128)(2,1)} %down_a_ref.1), channel_id=1, source_target_pairs={{0,1},{1,0},{2,3},{3,2},{4,5},{5,4},{6,7},{7,6},{8,9},{9,8},{10,11... | collective-permute-start | bytes 6291464 | tf_op jit(solution)/shard_map/ppermute | solution.py:443
  114.5 12.8 %all-to-all-start.3 = ((bf16[4,32,2048]{2,1,0:T(8,128)(2,1)}), bf16[4,32,2048]{2,1,0:T(8,128)(2,1)S(1)}, u32[]{:S(2)}, u32[]{:S(2)}) async-start(bf16[4,32,2048]{2,1,0:T(8,128)(2,1)} %bitcast.24), calls=%async_computation.3 | async-start | bytes 1048576 | tf_op jit(solution)/shard_map/all_to_all | solution.py:447
  130.0 33.6 %all-to-all-start.4 = ((bf16[16,32,2176]{2,1,0:T(8,128)(2,1)}), bf16[16,32,2176]{2,1,0:T(8,128)(2,1)S(1)}, u32[]{:S(2)}, u32[]{:S(2)}) async-start(bf16[16,32,2176]{2,1,0:T(8,128)(2,1)} %get-tuple-element.35), calls=%async_computation.4 | async-start | bytes 4456448 | tf_op jit(solution)/shard_map/all_to_all | solution.py:447

commit v3 on v2

--- a/solution.py
+++ b/solution.py
@@ -139,10 +139,13 @@
         moved = falls * carried - mm(drive[n][:, dim:], carried)
         carried = jnp.concatenate([moved[:, :dim], moved[:, dim:] + drive[n][:, :dim]], axis=1)
     carry_ref[...] = carried
-    maps_ref[...] = carried.astype(BF16)
-
-
-def block_maps(core, scalars, mine, theirs, w, ws, dim, per_step):
+
+    @pl.when(step == pl.num_programs(0) - 1)
+    def _():
+        maps_ref[...] = jnp.broadcast_to(carried.astype(BF16)[None], maps_ref.shape)
+
+
+def block_maps(core, scalars, mine, theirs, w, ws, dim, copies, per_step):
     groups, each, width = mine.shape
     span = 2 * groups * each
     rows = per_step * CHUNK
@@ -166,7 +169,7 @@
         ],
         out_specs=[
             stacked(CHUNK), stacked(CHUNK), stacked(dim), stacked(2 * dim), stacked(2 * dim),
-            whole((dim, 2 * dim)),
+            whole((copies, dim, 2 * dim)),
         ],
         out_shape=[
             jax.ShapeDtypeStruct((count, dim, CHUNK), BF16),
@@ -174,7 +177,7 @@
             jax.ShapeDtypeStruct((count, CHUNK, dim), F32),
             jax.ShapeDtypeStruct((count, CHUNK, 2 * dim), BF16),
             jax.ShapeDtypeStruct((count, dim, 2 * dim), BF16),
-            jax.ShapeDtypeStruct((dim, 2 * dim), BF16),
+            jax.ShapeDtypeStruct((copies, dim, 2 * dim), BF16),
         ],
         scratch_shapes=[pltpu.VMEM((dim, 2 * dim), F32)],
         name="block_maps",
@@ -253,11 +256,29 @@
 
     @pl.when(pl.program_id(0) == 0)
     def _():
-        state = init_ref[...].T
-        for block in range(maps_ref.shape[0] - 1):
-            maps = maps_ref[block]
-            moved = mm(maps[:, :dim], state) + maps[:, dim:].astype(F32)
-            state = jnp.where(block < place_ref[0], moved, state)
+        rows = lax.broadcasted_iota(jnp.int32, (dim, 2 * dim), 0)
+        cols = lax.broadcasted_iota(jnp.int32, (dim, 2 * dim), 1)
+        still = jnp.where(rows == cols, 1.0, 0.0).astype(F32)
+        steps = [
+            jnp.where(block < place_ref[0], maps_ref[block].astype(F32), still)
+            for block in range(maps_ref.shape[0] - 1)
+        ]
+
+        def after(later, earlier):
+            both = mm(later[:, :dim], earlier)
+            return jnp.concatenate([both[:, :dim], both[:, dim:] + later[:, dim:]], axis=1)
+
+        state = mm(steps[0][:, :dim], init_ref[...].T) + steps[0][:, dim:]
+        steps = steps[1:]
+        while steps:
+            rest = [after(b, a) for a, b in zip(steps[1::2], steps[2::2])]
+            if len(steps) % 2 == 0:
+                pairs = [after(b, a) for a, b in zip(steps[0::2], steps[1::2])]
+                state = mm(pairs[0][:, :dim], state) + pairs[0][:, dim:]
+                steps = pairs[1:]
+            else:
+                state = mm(steps[0][:, :dim], state) + steps[0][:, dim:]
+                steps = rest
         state_ref[...] = state
 
     head_raw = mm(slope_ref[...], state_ref[...]) + base_ref[...]
@@ -292,29 +313,31 @@
     *w_refs, out_ref = refs
     core = place_ref[0]
     row = place_ref[1]
-    count = len(w_refs) // 2
-    left = []
-    for at in range(2 * count):
-        head = 2 * lax.rem(row + count - at % count, count)
-        left.append(gated_ref[head + (core if at < count else 1 - core)])
+    count = gated_ref.shape[0] // 2
+    step = 2 * core - 1 + count
+    rows = [row, row, row + step, row + step, row + 2, row + count - step + count,
+            row + count - step + count, row + 2]
+    cores = [core, 1 - core, core, 1 - core, core, 1 - core, core, 1 - core]
+    left = [gated_ref[2 * lax.rem(at, count) + side] for at, side in zip(rows, cores)]
     total = jnp.dot(
         jnp.concatenate(left, axis=1),
         jnp.concatenate([ref[...] for ref in w_refs], axis=0),
         preferred_element_type=F32,
     )
-    out_ref[...] = total.astype(BF16)
-
-
-def project(place, gated, weights, tile):
+    out_ref[...] = total.astype(BF16).reshape(out_ref.shape)
+
+
+def project(place, gated, weights, parts, tile):
     heads, rows, dim = gated.shape
     width = weights[0].shape[1]
-    w_spec = pl.BlockSpec((dim, tile), lambda i: (0, i))
     return pl.pallas_call(
         project_body,
         grid=(width // tile,),
-        in_specs=[pl.BlockSpec(memory_space=pltpu.SMEM), resident()] + [w_spec] * heads,
-        out_specs=pl.BlockSpec((rows, tile), lambda i: (0, i)),
-        out_shape=jax.ShapeDtypeStruct((rows, width), BF16),
+        in_specs=[pl.BlockSpec(memory_space=pltpu.SMEM), resident()] + [
+            pl.BlockSpec((rows.shape[0], tile), lambda i: (0, i)) for rows in weights
+        ],
+        out_specs=pl.BlockSpec((parts, rows // parts, tile), lambda i: (0, 0, i)),
+        out_shape=jax.ShapeDtypeStruct((parts, rows // parts, width), BF16),
         name="project",
     )(place, near(gated), *weights)
 
@@ -351,17 +374,18 @@
     *, tiles,
 ):
     step = pl.program_id(0)
-    width = out_ref.shape[1]
+    groups, each, width = out_ref.shape
+    count = groups * each
 
     def tile(gate_ref, up_ref, down_ref):
-        x = x_ref[:, :width]
+        x = x_ref[:, :, :width].reshape(count, width)
         gate = jnp.dot(x, gate_ref[0], preferred_element_type=F32)
         up = jnp.dot(x, up_ref[0], preferred_element_type=F32)
         activated = (gate * jax.nn.sigmoid(gate) * up).astype(BF16)
         return jnp.dot(activated, down_ref[0], preferred_element_type=F32)
 
     def weight(which):
-        extra = x_ref[:, width:].astype(F32)
+        extra = x_ref[:, :, width:].astype(F32).reshape(count, -1)
         first = 3 * which
         return (
             extra[:, first:first + 1]
@@ -386,11 +410,12 @@
                     if which == 0:
                         total_ref[...] = scaled
                     else:
-                        out_ref[...] = (total_ref[...] + scaled).astype(BF16)
+                        out_ref[...] = (total_ref[...] + scaled).astype(BF16).reshape(out_ref.shape)
 
 
 def experts_of(x, first, second, tiles):
-    rows, wide = x.shape
+    groups, each, wide = x.shape
+    rows = groups * each
     hidden_units, width = first[1].shape[1:]
     tile = hidden_units // tiles
 
@@ -408,8 +433,8 @@
         functools.partial(experts_body, tiles=tiles),
         grid=(2 * tiles,),
         in_specs=[resident()] + specs(0) + specs(tiles),
-        out_specs=whole((rows, width)),
-        out_shape=jax.ShapeDtypeStruct((rows, width), BF16),
+        out_specs=resident(),
+        out_shape=jax.ShapeDtypeStruct((groups, each, width), BF16),
         scratch_shapes=[pltpu.VMEM((rows, width), F32), pltpu.VMEM((rows, width), F32)],
         name="experts",
     )(near(x), first[0], first[0], first[1], second[0], second[0], second[1])
@@ -430,9 +455,11 @@
     )(near(parts))
 
 
-def shift_y(value, steps):
+def send_y(value):
     count = lax.axis_size("y")
-    return lax.ppermute(value, "y", [(at, (at + steps) % count) for at in range(count)])
+    up = [(2 * at, 2 * ((at + 1) % count)) for at in range(count)]
+    down = [(2 * at + 1, 2 * ((at + count - 1) % count) + 1) for at in range(count)]
+    return lax.ppermute(value, ("y", "core"), up + down)
 
 
 def near(value):
@@ -476,26 +503,30 @@
     copies = norm_copies(tokens, gain_in, chips)
     mine = exchange(copies, ("x", "y"))
     theirs = swap_cores(mine)
-    w_here, _ = lax.optimization_barrier((w_output, mine))
-    w_rows = [w_here] + [shift_y(w_here, steps) for steps in range(1, y_count)]
+    pair = jnp.concatenate([w_output, swap_cores(w_output)], axis=0)
+    pair, _ = lax.optimization_barrier((pair, mine))
+    beside = send_y(pair)
 
     scalars = jnp.concatenate([strength_bias, decay_rate, decay_bias])
     w_logit = jnp.pad(w_scalar, ((0, 0), (0, LANES - w_scalar.shape[1])))
-    *parts, maps = block_maps(core[None], scalars, mine, theirs, w_heads, w_logit, dim, PER_STEP)
-    maps = jnp.broadcast_to(maps[None], (ctx_count,) + maps.shape)
+    *parts, maps = block_maps(core[None], scalars, mine, theirs, w_heads, w_logit, dim, ctx_count, PER_STEP)
+    beside, maps, far_gate_up, far_down = lax.optimization_barrier(
+        (beside, maps, w_gate_up, w_down)
+    )
+    across = send_y(beside[:dim])
     all_maps = exchange(maps, "ctx")
     slope, base, gate = block_reads(core[None], mine, theirs, w_heads, gain_head, parts, dim, PER_STEP)
-    *w_rows, slope = lax.optimization_barrier((*w_rows, slope))
-    w_rows = w_rows + [swap_cores(rows) for rows in w_rows]
+    across, slope = lax.optimization_barrier((across, slope))
+    w_rows = [pair, beside, across, swap_cores(beside), swap_cores(across)]
     gated = emit(
         place[None], all_maps, state_init[0], slope, base, gate, x_count, y_count * core_count
     )
     heads = y_count * core_count
     gated = exchange(gated, ("y", "core")).reshape(heads, x_count * tok_dev, dim)
-    partial = project(jnp.stack([core, lax.axis_index("y").astype(jnp.int32)]), gated, w_rows, 512).reshape(x_count, tok_dev, width)
-
-    other_gate_up = swap_cores(w_gate_up)
-    other_down = swap_cores(w_down)
+    partial = project(jnp.stack([core, lax.axis_index("y").astype(jnp.int32)]), gated, w_rows, x_count, 512)
+
+    other_gate_up = swap_cores(far_gate_up)
+    other_down = swap_cores(far_down)
     numbers = jnp.arange(expert_total, dtype=jnp.int32)
     named = expert_ids[:, :, None] == numbers[None, None, :]
     routes = jnp.sum(jnp.where(named, gate_weights[:, :, None], 0.0), axis=1)
@@ -505,9 +536,8 @@
     routes = jnp.pad(routes, ((0, 0), (0, 0), (0, LANES - routes.shape[-1])))
 
     summed, copies = join(exchange(partial, "x"), tokens, gain_expert, routes)
-    received = exchange(copies, ("x", "y")).reshape(chips * tok_dev, -1)
+    received = exchange(copies, ("x", "y"))
     outputs = experts_of(received, (w_gate_up, w_down), (other_gate_up, other_down), 2)
-    outputs = outputs.reshape(chips, tok_dev, width)
     expert_out = total_of(exchange(outputs, ("x", "y")))
     return (summed, expert_out)
 

time: 208 us -> 199 us (0.957)
  waiting for transfers between devices: 61.4 us -> 56.4 us
  starting transfers between devices: 28.4 us -> 24.9 us
    ppermute x3 -> x2, waiting for transfers between devices: 16.8 us -> 2.96 us  [send_y(): return lax.ppermute(value, ('y', 'core'), up + down)]
    all_to_all x4, waiting for transfers between devices: 41.8 us -> 49.4 us  [exchange(): return lax.all_to_all(value, axes, split_axis=0, concat_axis=0, tiled=True)]
    ppermute x3 -> x2, starting transfers between devices: 4.22 us -> 1.58 us  [send_y(): return lax.ppermute(value, ('y', 'core'), up + down)]
  transfers between devices with their start and end apart: 14 -> 12, of which waited for: 7 -> 6; matrix products, arithmetic and copies ran while one was open for 3% -> 3% of each run, Pallas kernels for 14% -> 15%
where the time goes in v3:
time: 199 us
  blocking collectives  63.7 us (32%)
  waiting for transfers between devices  56.4 us (28%)
  Pallas kernels  44.2 us (22%)
  starting transfers between devices  24.9 us (13%)
  local copies, waits for them, and re-layouts  5.14 us (3%)
  between operations  2.74 us (1%)
    all_to_all x2, blocking collectives, exchange(): return lax.all_to_all(value, axes, split_axis=0, concat_axis=0, tiled=True)  63.7 us
    all_to_all x4, waiting for transfers between devices, exchange(): return lax.all_to_all(value, axes, split_axis=0, concat_axis=0, tiled=True)  49.4 us
    all_to_all x4, starting transfers between devices, exchange(): return lax.all_to_all(value, axes, split_axis=0, concat_axis=0, tiled=True)  21.9 us
    pallas_call x1, Pallas kernels, experts_of(): pl.pallas_call(functools.partial(experts_body, tiles=tiles), grid=(2 * ti...  12 us
    pallas_call x1, Pallas kernels, block_maps(): pl.pallas_call(functools.partial(maps_body, per_step=per_step), grid=(spa...  11.5 us
    pallas_call x1, Pallas kernels, block_reads(): pl.pallas_call(functools.partial(reads_body, per_step=per_step), grid=(sp...  5.78 us
    pallas_call x1, Pallas kernels, project(): pl.pallas_call(project_body, grid=(width // tile,), in_specs=[pl.BlockSpe...  4.44 us
    pallas_call x1, Pallas kernels, emit(): pl.pallas_call(emit_body, grid=(outer,), in_specs=[pl.BlockSpec(memory_sp...  4.42 us
  transfers between devices with their start and end apart: 12, of which 6 were waited for; matrix products, arithmetic and copies ran while one was open for 3% of the time, Pallas kernels for 15%

profile of v3, /device:TPU:8, one launch (start us, length us, event | category | flops | bytes accessed | tf_op | source)
XLA Modules:
  0.0 198.6 jit_solution(5004159304526684670)
XLA Ops:
  0.6 2.5 %norm_copies.1 = bf16[16,32,2048]{2,1,0:T(8,128)(2,1)} custom-call(bf16[32,2048]{1,0:T(8,128)(2,1)} %tokens_ref.3, f32[1,2048]{1,0:T(1,128)} %bitcast.23), custom_call_target="tpu_custom_call" | custom-call | tf_op jit(solution)/shard_map/norm_copies/pallas_call | solution.py:247
  3.1 34.1 %all_to_all.30.mine_ref = bf16[16,32,2048]{2,1,0:T(8,128)(2,1)S(1)} all-to-all(bf16[16,32,2048]{2,1,0:T(8,128)(2,1)} %norm_copies.1), channel_id=1, replica_groups=mesh['ctx'=8,'x'=4,'y'=4,'core'=2] {'x','y'}, dimensions={0} | all-to-all | bytes 4194304 | tf_op jit(solution)/shard_map/all_to_all | solution.py:474
  37.3 0.0 collective-permute-start.2
  37.3 0.0 copy-done.5
  37.3 0.5 collective-permute-start
  37.8 4.0 %collective-permute-done = bf16[128,2048]{1,0:T(8,128)(2,1)S(1)} collective-permute-done((bf16[128,2048]{1,0:T(8,128)(2,1)S(1)}, bf16[128,2048]{1,0:T(8,128)(2,1)S(1)}, u32[]{:S(2)}, u32[]{:S(2)}) %collective-permute-start) | collective-permute-done | bytes 524320 | tf_op jit(solution)/shard_map/ppermute | solution.py:470
  41.8 0.1 pad_maximum_fusion.refs_0_
  41.9 0.0 copy-start.1
  41.9 1.2 collective-permute-start.1
  45.0 1.1 copy.29
  46.1 1.9 pad.8.ws_ref
  48.1 0.6 pad_maximum_fusion.2.scal_ref
  48.6 0.0 collective-permute-done.2.theirs_ref
  48.6 11.5 %block_maps.1 = (bf16[8,128,128]{2,1,0:T(8,128)(2,1)}, f32[8,128,128]{2,1,0:T(8,128)}, f32[8,128,128]{2,1,0:T(8,128)}, bf16[8,128,256]{2,1,0:T(8,128)(2,1)}, bf1...) custom-call(s32[1]{0:T(128)} %bitcast.core_ref, f32[3]{0:T(128)} %pad_maximum_fusion.2.scal_ref, ...), custom_call_target="tpu_custom_call" | custom-call | tf_op jit(solution)/shard_map/block_maps/pallas_call | solution.py:158
  60.2 0.0 copy-done.1
  60.2 0.0 collective-permute-done.1.refs_1_
  60.2 0.8 collective-permute-start.6
  61.0 8.5 %all-to-all-start.1 = ((bf16[8,128,256]{2,1,0:T(8,128)(2,1)}), bf16[8,128,256]{2,1,0:T(8,128)(2,1)S(1)}, u32[]{:S(2)}, u32[]{:S(2)}) async-start(bf16[8,128,256]{2,1,0:T(8,128)(2,1)} %get-tuple-element.22), calls=%async_computation.1 | async-start | bytes 1048576 | tf_op jit(solution)/shard_map/all_to_all | solution.py:474
  69.4 1.1 slice.3
  70.5 0.4 collective-permute-start.3
  70.9 0.1 collective-permute-start.4
  71.0 5.8 %block_reads.1 = (bf16[1024,128]{1,0:T(8,128)(2,1)}, f32[1024,128]{1,0:T(8,128)}, f32[1024,128]{1,0:T(8,128)}) custom-call(s32[1]{0:T(128)} %bitcast.core_ref, bf16[16,32,2048]{2,1,0:T(8,128)(2,1)} %copy-done, bf16[16,32,2048]{2,1,0:T(8,128)(2,1)} %collective-permute-done.2.theirs_ref, bf16[2048,512]{1,0:T(8,128)(2,1)} %wg_ref.1, bf16[2048,512]{1,0:T(8,128)(2,1)} %wg_ref.1, ...), custom_call_target="tpu_custom_call" | custom-call | tf_op jit(solution)/shard_map/block_reads/pallas_call | solution.py:218
  76.8 0.0 copy-start.8
  76.8 3.0 %collective-permute-done.3.refs_2_ = bf16[128,2048]{1,0:T(8,128)(2,1)S(1)} collective-permute-done((bf16[128,2048]{1,0:T(8,128)(2,1)S(1)}, bf16[128,2048]{1,0:T(8,128)(2,1)S(1)}, u32[]{:S(2)}, u32[]{:S(2)}) %collective-permute-start.3) | collective-permute-done | bytes 524320 | tf_op jit(solution)/shard_map/ppermute | solution.py:462
  79.8 0.0 collective-permute-start.5
  79.8 7.3 %all-to-all-done.1.maps_ref = bf16[8,128,256]{2,1,0:T(8,128)(2,1)S(1)} async-done(((bf16[8,128,256]{2,1,0:T(8,128)(2,1)}), bf16[8,128,256]{2,1,0:T(8,128)(2,1)S(1)}, u32[]{:S(2)}, u32[]{:S(2)}) %all-to-all-start.1) | async-done | bytes 524320 | tf_op jit(solution)/shard_map/all_to_all | solution.py:474
  87.1 4.4 %emit.1 = bf16[8,4,32,128]{3,2,1,0:T(8,128)(2,1)} custom-call(s32[1]{0:T(128)} %bitcast.2.place_ref, bf16[8,128,256]{2,1,0:T(8,128)(2,1)S(1)} %all-to-all-done.1.maps_ref, f32[128,128]{1,0:T(8,128)} %bitcast.22, bf16[1024,128]{1,0:T(8,128)(2,1)} %get-tuple-element.30.slope_ref, f32[1024,128]{1,0:T(8,128)} %get-tuple-element.31.base_ref, ...), custom_call_target="tpu_custom_call" | custom-call | tf_op jit(solution)/shard_map/emit/pallas_call | solution.py:294
  91.5 4.9 %all-to-all-start.2 = ((bf16[8,4,32,128]{3,2,1,0:T(8,128)(2,1)}), bf16[8,4,32,128]{3,2,1,0:T(8,128)(2,1)S(1)}, u32[]{:S(2)}, u32[]{:S(2)}) async-start(bf16[8,4,32,128]{3,2,1,0:T(8,128)(2,1)} %emit.1), calls=%async_computation.2 | async-start | bytes 524288 | tf_op jit(solution)/shard_map/all_to_all | solution.py:474
  96.5 0.2 select_reduce_fusion
  96.6 0.1 copy.30
  96.8 0.6 pad_add_fusion.place_ref
  97.4 0.0 collective-permute-done.5.refs_4_
  97.4 0.0 collective-permute-done.4.refs_3_
  97.4 5.2 %all-to-all-done.2 = bf16[8,4,32,128]{3,2,1,0:T(8,128)(2,1)S(1)} async-done(((bf16[8,4,32,128]{3,2,1,0:T(8,128)(2,1)}), bf16[8,4,32,128]{3,2,1,0:T(8,128)(2,1)S(1)}, u32[]{:S(2)}, u32[]{:S(2)}) %all-to-all-start.2) | async-done | bytes 262176 | tf_op jit(solution)/shard_map/all_to_all | solution.py:474
  102.6 4.4 %project.1 = bf16[4,32,2048]{2,1,0:T(8,128)(2,1)} custom-call(s32[2]{0:T(128)} %pad_add_fusion.place_ref, bf16[8,128,128]{2,1,0:T(8,128)(2,1)S(1)} %bitcast.18, bf16[256,2048]{1,0:T(8,128)(2,1)} %copy-done.1, bf16[256,2048]{1,0:T(8,128)(2,1)} %collective-permute-done.1.refs_1_, bf16[128,2048]{1,0:T(8,128)(2,1)} %copy-done.3, bf16[256,2048]{1,0:T(8,128)(2,1)} %copy-done.2, ...), custom_call_target="tpu_custom_call" | custom-call | tf_op jit(solution)/shard_map/project/pallas_call | solution.py:333
  107.0 3.5 %all-to-all-start.3 = ((bf16[4,32,2048]{2,1,0:T(8,128)(2,1)}), bf16[4,32,2048]{2,1,0:T(8,128)(2,1)S(1)}, u32[]{:S(2)}, u32[]{:S(2)}) async-start(bf16[4,32,2048]{2,1,0:T(8,128)(2,1)} %project.1), calls=%async_computation.3 | async-start | bytes 1048576 | tf_op jit(solution)/shard_map/all_to_all | solution.py:474
  110.5 0.1 collective-permute-start.7
  110.7 0.2 copy.34
  110.9 0.7 pad.9.routes_ref
  111.6 8.2 %all-to-all-done.3.parts_ref = bf16[4,32,2048]{2,1,0:T(8,128)(2,1)S(1)} async-done(((bf16[4,32,2048]{2,1,0:T(8,128)(2,1)}), bf16[4,32,2048]{2,1,0:T(8,128)(2,1)S(1)}, u32[]{:S(2)}, u32[]{:S(2)}) %all-to-all-start.3) | async-done | bytes 524320 | tf_op jit(solution)/shard_map/all_to_all | solution.py:474
  119.8 2.7 %join.1 = (bf16[32,2048]{1,0:T(8,128)(2,1)}, bf16[16,32,2176]{2,1,0:T(8,128)(2,1)}) custom-call(bf16[4,32,2048]{2,1,0:T(8,128)(2,1)S(1)} %all-to-all-done.3.parts_ref, bf16[32,2048]{1,0:T(8,128)(2,1)} %tokens_ref.3, f32[1,2048]{1,0:T(1,128)} %bitcast.24, bf16[16,32,128]{2,1,0:T(8,128)(2,1)} %pad.9.routes_ref), custom_call_target="tpu_custom_call" | custom-call | tf_op jit(solution)/shard_map/join/pallas_call | solution.py:361
  122.5 5.0 %all-to-all-start.4 = ((bf16[16,32,2176]{2,1,0:T(8,128)(2,1)}), bf16[16,32,2176]{2,1,0:T(8,128)(2,1)S(1)}, u32[]{:S(2)}, u32[]{:S(2)}) async-start(bf16[16,32,2176]{2,1,0:T(8,128)(2,1)} %get-tuple-element.35), calls=%async_computation.4 | async-start | bytes 4456448 | tf_op jit(solution)/shard_map/all_to_all | solution.py:474
  127.5 0.0 collective-permute-done.7.down_b_ref
  127.5 28.7 %all-to-all-done.4.x_ref = bf16[16,32,2176]{2,1,0:T(8,128)(2,1)S(1)} async-done(((bf16[16,32,2176]{2,1,0:T(8,128)(2,1)}), bf16[16,32,2176]{2,1,0:T(8,128)(2,1)S(1)}, u32[]{:S(2)}, u32[]{:S(2)}) %all-to-all-start.4) | async-done | bytes 2228256 | tf_op jit(solution)/shard_map/all_to_all | solution.py:474
  156.2 0.0 collective-permute-done.6.gate_b_ref.up_b_ref
  156.2 12.0 %experts.1 = bf16[16,32,2048]{2,1,0:T(8,128)(2,1)} custom-call(bf16[16,32,2176]{2,1,0:T(8,128)(2,1)S(1)} %all-to-all-done.4.x_ref, bf16[1,2048,1024]{2,1,0:T(8,128)(2,1)} %up_a_ref.1, bf16[1,2048,1024]{2,1,0:T(8,128)(2,1)} %up_a_ref.1, bf16[1,512,2048]{2,1,0:T(8,128)(2,1)} %down_a_ref.1, bf16[1,2048,1024]{2,1,0:T(8,128)(2,1)} %collective-permute-done.6.gate_b_ref.up_b_ref, ...), custom_call_target="tpu_custom_call" | custom-call | tf_op jit(solution)/shard_map/experts/pallas_call | solution.py:432
  168.2 29.6 %all_to_all.31.parts_ref = bf16[16,32,2048]{2,1,0:T(8,128)(2,1)S(1)} all-to-all(bf16[16,32,2048]{2,1,0:T(8,128)(2,1)} %experts.1), channel_id=1, replica_groups=mesh['ctx'=8,'x'=4,'y'=4,'core'=2] {'x','y'}, dimensions={0} | all-to-all | bytes 4194304 | tf_op jit(solution)/shard_map/all_to_all | solution.py:474
  197.7 0.9 total.1
  (19 shorter events, 0.2 us)
Async XLA Ops:
  3.1 34.2 %copy-start.5 = (bf16[128,2048]{1,0:T(8,128)(2,1)S(1)}, bf16[128,2048]{1,0:T(8,128)(2,1)}, u32[]{:S(2)}) copy-start(bf16[128,2048]{1,0:T(8,128)(2,1)} %param.24) | copy-start | bytes 1572868
  37.3 11.4 %copy-start = (bf16[16,32,2048]{2,1,0:T(8,128)(2,1)}, bf16[16,32,2048]{2,1,0:T(8,128)(2,1)S(1)}, u32[]{:S(2)}) copy-start(bf16[16,32,2048]{2,1,0:T(8,128)(2,1)S(1)} %all_to_all.30.mine_ref) | copy-start | bytes 6291460
  37.3 7.8 %copy-start.6 = (bf16[2048,2]{0,1:T(2,128)(2,1)S(1)}, bf16[2048,2]{0,1:T(2,128)(2,1)}, u32[]{:S(2)}) copy-start(bf16[2048,2]{0,1:T(2,128)(2,1)} %param.18) | copy-start | bytes 24580
  37.3 11.4 %collective-permute-start.2 = (bf16[16,32,2048]{2,1,0:T(8,128)(2,1)S(1)}, bf16[16,32,2048]{2,1,0:T(8,128)(2,1)}, u32[]{:S(2)}, u32[]{:S(2)}) collective-permute-start(bf16[16,32,2048]{2,1,0:T(8,128)(2,1)S(1)} %all_to_all.30.mine_ref), channel_id=1, source_target_pairs={{0,1},{1,0},{2,3},{3,2},{4,5},{5,4},{6,7},{7,6},{8,9},{9,8},{10,11... | collective-permute-start | bytes 6291464 | tf_op jit(solution)/shard_map/ppermute | solution.py:470
  37.3 4.5 %collective-permute-start = (bf16[128,2048]{1,0:T(8,128)(2,1)S(1)}, bf16[128,2048]{1,0:T(8,128)(2,1)S(1)}, u32[]{:S(2)}, u32[]{:S(2)}) collective-permute-start(bf16[128,2048]{1,0:T(8,128)(2,1)S(1)} %copy-done.5), channel_id=1, source_target_pairs={{0,1},{1,0},{2,3},{3,2},{4,5},{5,4},{6,7},{7,6},{8,9},{9,8},{10,11... | collective-permute-start | bytes 1572872 | tf_op jit(solution)/shard_map/ppermute | solution.py:470
  41.9 18.3 %copy-start.1 = (bf16[256,2048]{1,0:T(8,128)(2,1)}, bf16[256,2048]{1,0:T(8,128)(2,1)S(1)}, u32[]{:S(2)}) copy-start(bf16[256,2048]{1,0:T(8,128)(2,1)S(1)} %pad_maximum_fusion.refs_0_) | copy-start | bytes 3145732
  41.9 18.3 %collective-permute-start.1 = (bf16[256,2048]{1,0:T(8,128)(2,1)S(1)}, bf16[256,2048]{1,0:T(8,128)(2,1)}, u32[]{:S(2)}, u32[]{:S(2)}) collective-permute-start(bf16[256,2048]{1,0:T(8,128)(2,1)S(1)} %pad_maximum_fusion.refs_0_), channel_id=1, source_target_pairs={{0,2},{2,4},{4,6},{6,0},{1,7},{3,1},{5,3},{7,5},{8,10},{10,12},{12... | collective-permute-start | bytes 3145736 | tf_op jit(solution)/shard_map/ppermute | solution.py:462
  60.2 96.0 %collective-permute-start.6 = (bf16[1,2048,1024]{2,1,0:T(8,128)(2,1)}, bf16[1,2048,1024]{2,1,0:T(8,128)(2,1)}, u32[]{:S(2)}, u32[]{:S(2)}) collective-permute-start(bf16[1,2048,1024]{2,1,0:T(8,128)(2,1)} %up_a_ref.1), channel_id=1, source_target_pairs={{0,1},{1,0},{2,3},{3,2},{4,5},{5,4},{6,7},{7,6},{8,9},{9,8},{10,11... | collective-permute-start | bytes 12582920 | tf_op jit(solution)/shard_map/ppermute | solution.py:470
  61.0 26.2 %all-to-all-start.1 = ((bf16[8,128,256]{2,1,0:T(8,128)(2,1)}), bf16[8,128,256]{2,1,0:T(8,128)(2,1)S(1)}, u32[]{:S(2)}, u32[]{:S(2)}) async-start(bf16[8,128,256]{2,1,0:T(8,128)(2,1)} %get-tuple-element.22), calls=%async_computation.1 | async-start | bytes 1048576 | tf_op jit(solution)/shard_map/all_to_all | solution.py:474
  70.5 9.3 %collective-permute-start.3 = (bf16[128,2048]{1,0:T(8,128)(2,1)S(1)}, bf16[128,2048]{1,0:T(8,128)(2,1)S(1)}, u32[]{:S(2)}, u32[]{:S(2)}) collective-permute-start(bf16[128,2048]{1,0:T(8,128)(2,1)S(1)} %slice.3), channel_id=1, source_target_pairs={{0,2},{2,4},{4,6},{6,0},{1,7},{3,1},{5,3},{7,5},{8,10},{10,12},{12... | collective-permute-start | bytes 1572872 | tf_op jit(solution)/shard_map/ppermute | solution.py:462
  70.9 26.5 %collective-permute-start.4 = (bf16[256,2048]{1,0:T(8,128)(2,1)}, bf16[256,2048]{1,0:T(8,128)(2,1)S(1)}, u32[]{:S(2)}, u32[]{:S(2)}) collective-permute-start(bf16[256,2048]{1,0:T(8,128)(2,1)} %collective-permute-done.1.refs_1_), channel_id=1, source_target_pairs={{0,1},{1,0},{2,3},{3,2},{4,5},{5,4},{6,7},{7,6},{8,9},{9,8},{10,11... | collective-permute-start | bytes 3145736 | tf_op jit(solution)/shard_map/ppermute | solution.py:470
  76.8 19.7 %copy-start.7 = (f32[32,10]{0,1:T(8,128)S(1)}, f32[32,10]{0,1:T(8,128)}, u32[]{:S(2)}) copy-start(f32[32,10]{0,1:T(8,128)} %param.27) | copy-start | bytes 3844
  76.8 19.7 %copy-start.8 = (s32[32,10]{0,1:T(8,128)S(1)}, s32[32,10]{0,1:T(8,128)}, u32[]{:S(2)}) copy-start(s32[32,10]{0,1:T(8,128)} %param.26) | copy-start | bytes 3844
  79.8 22.8 %copy-start.3 = (bf16[128,2048]{1,0:T(8,128)(2,1)}, bf16[128,2048]{1,0:T(8,128)(2,1)S(1)}, u32[]{:S(2)}) copy-start(bf16[128,2048]{1,0:T(8,128)(2,1)S(1)} %collective-permute-done.3.refs_2_) | copy-start | bytes 1572868
  79.8 17.6 %collective-permute-start.5 = (bf16[128,2048]{1,0:T(8,128)(2,1)S(1)}, bf16[128,2048]{1,0:T(8,128)(2,1)S(1)}, u32[]{:S(2)}, u32[]{:S(2)}) collective-permute-start(bf16[128,2048]{1,0:T(8,128)(2,1)S(1)} %collective-permute-done.3.refs_2_), channel_id=1, source_target_pairs={{0,1},{1,0},{2,3},{3,2},{4,5},{5,4},{6,7},{7,6},{8,9},{9,8},{10,11... | collective-permute-start | bytes 1572872 | tf_op jit(solution)/shard_map/ppermute | solution.py:470
  91.5 11.0 %all-to-all-start.2 = ((bf16[8,4,32,128]{3,2,1,0:T(8,128)(2,1)}), bf16[8,4,32,128]{3,2,1,0:T(8,128)(2,1)S(1)}, u32[]{:S(2)}, u32[]{:S(2)}) async-start(bf16[8,4,32,128]{3,2,1,0:T(8,128)(2,1)} %emit.1), calls=%async_computation.2 | async-start | bytes 524288 | tf_op jit(solution)/shard_map/all_to_all | solution.py:474
  97.4 5.2 %copy-start.4 = (bf16[128,2048]{1,0:T(8,128)(2,1)}, bf16[128,2048]{1,0:T(8,128)(2,1)S(1)}, u32[]{:S(2)}) copy-start(bf16[128,2048]{1,0:T(8,128)(2,1)S(1)} %collective-permute-done.5.refs_4_) | copy-start | bytes 1572868
  97.4 5.2 %copy-start.2 = (bf16[256,2048]{1,0:T(8,128)(2,1)}, bf16[256,2048]{1,0:T(8,128)(2,1)S(1)}, u32[]{:S(2)}) copy-start(bf16[256,2048]{1,0:T(8,128)(2,1)S(1)} %collective-permute-done.4.refs_3_) | copy-start | bytes 3145732
  107.0 12.8 %all-to-all-start.3 = ((bf16[4,32,2048]{2,1,0:T(8,128)(2,1)}), bf16[4,32,2048]{2,1,0:T(8,128)(2,1)S(1)}, u32[]{:S(2)}, u32[]{:S(2)}) async-start(bf16[4,32,2048]{2,1,0:T(8,128)(2,1)} %project.1), calls=%async_computation.3 | async-start | bytes 1048576 | tf_op jit(solution)/shard_map/all_to_all | solution.py:474
  110.5 17.0 %collective-permute-start.7 = (bf16[1,512,2048]{2,1,0:T(8,128)(2,1)}, bf16[1,512,2048]{2,1,0:T(8,128)(2,1)}, u32[]{:S(2)}, u32[]{:S(2)}) collective-permute-start(bf16[1,512,2048]{2,1,0:T(8,128)(2,1)} %down_a_ref.1), channel_id=1, source_target_pairs={{0,1},{1,0},{2,3},{3,2},{4,5},{5,4},{6,7},{7,6},{8,9},{9,8},{10,11... | collective-permute-start | bytes 6291464 | tf_op jit(solution)/shard_map/ppermute | solution.py:470
  122.5 33.6 %all-to-all-start.4 = ((bf16[16,32,2176]{2,1,0:T(8,128)(2,1)}), bf16[16,32,2176]{2,1,0:T(8,128)(2,1)S(1)}, u32[]{:S(2)}, u32[]{:S(2)}) async-start(bf16[16,32,2176]{2,1,0:T(8,128)(2,1)} %get-tuple-element.35), calls=%async_computation.4 | async-start | bytes 4456448 | tf_op jit(solution)/shard_map/all_to_all | solution.py:474

commit v4 on v3

--- a/solution.py
+++ b/solution.py
@@ -237,74 +237,76 @@
     )(core, mine, theirs, w, w, gain[None], key_t, decay, growth, solved, starts)
 
 
-def norm_body(tokens_ref, gain_ref, out_ref):
+def send_copies(copies):
+    for copy in copies:
+        copy.start()
+    for copy in copies:
+        copy.wait()
+
+
+def norm_body(tokens_ref, gain_ref, out_ref, normed_ref, sems):
     wide = tokens_ref[...].astype(F32)
-    normed = (wide * rms_scale(wide) * gain_ref[...]).astype(BF16)
-    out_ref[...] = jnp.broadcast_to(normed[None], out_ref.shape)
+    normed_ref[...] = (wide * rms_scale(wide) * gain_ref[...]).astype(BF16)
+    send_copies(
+        [
+            pltpu.make_async_copy(normed_ref, out_ref.at[at], sems.at[at])
+            for at in range(out_ref.shape[0])
+        ]
+    )
 
 
 def norm_copies(tokens, gain, copies):
     return pl.pallas_call(
         norm_body,
+        out_specs=pl.BlockSpec(memory_space=pl.ANY),
         out_shape=jax.ShapeDtypeStruct((copies,) + tokens.shape, BF16),
+        scratch_shapes=[pltpu.VMEM(tokens.shape, BF16), pltpu.SemaphoreType.DMA((copies,))],
         name="norm_copies",
     )(tokens, gain[None])
 
 
-def emit_body(place_ref, maps_ref, init_ref, slope_ref, base_ref, gate_ref, out_ref, state_ref):
+def emit_body(place_ref, maps_ref, init_ref, slope_ref, base_ref, gate_ref, out_ref):
     dim = init_ref.shape[0]
-
-    @pl.when(pl.program_id(0) == 0)
-    def _():
-        rows = lax.broadcasted_iota(jnp.int32, (dim, 2 * dim), 0)
-        cols = lax.broadcasted_iota(jnp.int32, (dim, 2 * dim), 1)
-        still = jnp.where(rows == cols, 1.0, 0.0).astype(F32)
-        steps = [
-            jnp.where(block < place_ref[0], maps_ref[block].astype(F32), still)
-            for block in range(maps_ref.shape[0] - 1)
-        ]
-
-        def after(later, earlier):
-            both = mm(later[:, :dim], earlier)
-            return jnp.concatenate([both[:, :dim], both[:, dim:] + later[:, dim:]], axis=1)
-
-        state = mm(steps[0][:, :dim], init_ref[...].T) + steps[0][:, dim:]
-        steps = steps[1:]
-        while steps:
-            rest = [after(b, a) for a, b in zip(steps[1::2], steps[2::2])]
-            if len(steps) % 2 == 0:
-                pairs = [after(b, a) for a, b in zip(steps[0::2], steps[1::2])]
-                state = mm(pairs[0][:, :dim], state) + pairs[0][:, dim:]
-                steps = pairs[1:]
-            else:
-                state = mm(steps[0][:, :dim], state) + steps[0][:, dim:]
-                steps = rest
-        state_ref[...] = state
-
-    head_raw = mm(slope_ref[...], state_ref[...]) + base_ref[...]
-    gated = head_raw * rms_scale(head_raw) * gate_ref[...]
-    out_ref[...] = gated.astype(BF16).reshape(out_ref.shape)
+    place = place_ref[2]
+    rows = lax.broadcasted_iota(jnp.int32, (dim, 2 * dim), 0)
+    cols = lax.broadcasted_iota(jnp.int32, (dim, 2 * dim), 1)
+    still = jnp.where(rows == cols, 1.0, 0.0).astype(F32)
+    steps = [
+        jnp.where(block < place, maps_ref[block].astype(F32), still)
+        for block in range(maps_ref.shape[0] - 1)
+    ]
+
+    def after(later, earlier):
+        both = mm(later[:, :dim], earlier)
+        return jnp.concatenate([both[:, :dim], both[:, dim:] + later[:, dim:]], axis=1)
+
+    state = mm(steps[0][:, :dim], init_ref[...].T) + steps[0][:, dim:]
+    steps = steps[1:]
+    while steps:
+        odd = len(steps) % 2
+        if odd:
+            state = mm(steps[0][:, :dim], state) + steps[0][:, dim:]
+            steps = steps[1:]
+        steps = [after(later, earlier) for earlier, later in zip(steps[0::2], steps[1::2])]
+        if steps and not odd:
+            state = mm(steps[0][:, :dim], state) + steps[0][:, dim:]
+            steps = steps[1:]
+    inner, outer, each, _ = out_ref.shape
+    for part in range(outer):
+        at = slice(part * inner * each, (part + 1) * inner * each)
+        head_raw = mm(slope_ref[at, :], state) + base_ref[at, :]
+        gated = head_raw * rms_scale(head_raw) * gate_ref[at, :]
+        out_ref[:, part] = gated.astype(BF16).reshape(inner, each, dim)
 
 
 def emit(place, maps, init, slope, base, gate, outer, inner):
     span, dim = slope.shape
-    rows = span // outer
-    each = rows // inner
-    by_rows = pl.BlockSpec((rows, dim), lambda i: (i, 0))
+    each = span // (outer * inner)
     return pl.pallas_call(
         emit_body,
-        grid=(outer,),
-        in_specs=[
-            pl.BlockSpec(memory_space=pltpu.SMEM),
-            resident(),
-            whole(init.shape),
-            by_rows,
-            by_rows,
-            by_rows,
-        ],
-        out_specs=pl.BlockSpec((inner, 1, each, dim), lambda i: (0, i, 0, 0)),
+        in_specs=[pl.BlockSpec(memory_space=pltpu.SMEM)] + [resident()] * 5,
+        out_specs=resident(),
         out_shape=jax.ShapeDtypeStruct((inner, outer, each, dim), BF16),
-        scratch_shapes=[pltpu.VMEM((dim, dim), F32)],
         name="emit",
     )(place, near(maps), init, slope, base, gate)
 
@@ -342,27 +344,56 @@
     )(place, near(gated), *weights)
 
 
-def join_body(parts_ref, tokens_ref, gain_ref, routes_ref, out_ref, copies_ref):
-    width = tokens_ref.shape[1]
+def join_body(parts_ref, tokens_ref, gain_ref, routes_ref, out_ref, *refs, halves):
+    copies_refs, (normed_ref, sems) = refs[:halves], refs[halves:]
+    rows, width = tokens_ref.shape
+    copies = routes_ref.shape[0]
+    each = rows // halves
+    extra = [
+        pltpu.make_async_copy(
+            routes_ref.at[:, pl.ds(half * each, each), :],
+            copies_refs[half].at[:, :, pl.ds(width, routes_ref.shape[2])],
+            sems.at[half * (copies + 1) + copies],
+        )
+        for half in range(halves)
+    ]
+    for copy in extra:
+        copy.start()
     total = parts_ref[0].astype(F32)
     for part in range(1, parts_ref.shape[0]):
         total = total + parts_ref[part].astype(F32)
     summed = total.astype(BF16)
     out_ref[...] = summed
     hidden = tokens_ref[...].astype(F32) + summed.astype(F32)
-    normed = (hidden * rms_scale(hidden) * gain_ref[...]).astype(BF16)
-    copies = copies_ref.shape[0]
-    copies_ref[:, :, :width] = jnp.broadcast_to(normed[None], (copies,) + normed.shape)
-    copies_ref[:, :, width:] = routes_ref[...]
-
-
-def join(parts, tokens, gain, routes):
+    normed_ref[...] = (hidden * rms_scale(hidden) * gain_ref[...]).astype(BF16)
+    send_copies(
+        [
+            pltpu.make_async_copy(
+                normed_ref.at[pl.ds(half * each, each), :],
+                copies_refs[half].at[at, :, pl.ds(0, width)],
+                sems.at[half * (copies + 1) + at],
+            )
+            for half in range(halves)
+            for at in range(copies)
+        ]
+    )
+    for copy in extra:
+        copy.wait()
+
+
+def join(parts, tokens, gain, routes, halves):
     copies, rows, extra = routes.shape
-    return pl.pallas_call(
-        join_body,
-        out_shape=[
-            jax.ShapeDtypeStruct(tokens.shape, BF16),
-            jax.ShapeDtypeStruct((copies, rows, tokens.shape[1] + extra), BF16),
+    width = tokens.shape[1]
+    anywhere = pl.BlockSpec(memory_space=pl.ANY)
+    shape = jax.ShapeDtypeStruct((copies, rows // halves, width + extra), BF16)
+    return pl.pallas_call(
+        functools.partial(join_body, halves=halves),
+        in_specs=[resident(), resident(), resident(), anywhere],
+        out_specs=[resident()] + [anywhere] * halves,
+        out_shape=[jax.ShapeDtypeStruct(tokens.shape, BF16)] + [shape] * halves,
+        scratch_shapes=[
+            pltpu.VMEM(tokens.shape, BF16),
+            pltpu.SemaphoreType.DMA((halves * (copies + 1),)),
         ],
         name="join",
     )(near(parts), tokens, gain[None], routes)
@@ -440,19 +471,24 @@
     )(near(x), first[0], first[0], first[1], second[0], second[0], second[1])
 
 
-def total_body(parts_ref, out_ref):
-    total = parts_ref[0].astype(F32)
-    for part in range(1, parts_ref.shape[0]):
-        total = total + parts_ref[part].astype(F32)
-    out_ref[...] = total.astype(BF16)
-
-
-def total_of(parts):
+def total_body(*refs):
+    *parts_refs, out_ref = refs
+    each = parts_refs[0].shape[1]
+    for half, parts_ref in enumerate(parts_refs):
+        total = parts_ref[0].astype(F32)
+        for part in range(1, parts_ref.shape[0]):
+            total = total + parts_ref[part].astype(F32)
+        out_ref[half * each:(half + 1) * each, :] = total.astype(BF16)
+
+
+def total_of(halves):
+    copies, each, width = halves[0].shape
     return pl.pallas_call(
         total_body,
-        out_shape=jax.ShapeDtypeStruct(parts.shape[1:], BF16),
+        in_specs=[resident()] * len(halves),
+        out_shape=jax.ShapeDtypeStruct((len(halves) * each, width), BF16),
         name="total",
-    )(near(parts))
+    )(*[near(parts) for parts in halves])
 
 
 def send_y(value):
@@ -502,28 +538,31 @@
 
     copies = norm_copies(tokens, gain_in, chips)
     mine = exchange(copies, ("x", "y"))
-    theirs = swap_cores(mine)
     pair = jnp.concatenate([w_output, swap_cores(w_output)], axis=0)
-    pair, _ = lax.optimization_barrier((pair, mine))
-    beside = send_y(pair)
-
     scalars = jnp.concatenate([strength_bias, decay_rate, decay_bias])
     w_logit = jnp.pad(w_scalar, ((0, 0), (0, LANES - w_scalar.shape[1])))
-    *parts, maps = block_maps(core[None], scalars, mine, theirs, w_heads, w_logit, dim, ctx_count, PER_STEP)
+    spots = jnp.stack([core, lax.axis_index("y").astype(jnp.int32), place])
+    mine, pair, scalars, w_logit, spots = lax.optimization_barrier(
+        (mine, pair, scalars, w_logit, spots)
+    )
+    theirs = swap_cores(mine)
+    beside = send_y(pair)
+
+    *parts, maps = block_maps(spots, scalars, mine, theirs, w_heads, w_logit, dim, ctx_count, PER_STEP)
     beside, maps, far_gate_up, far_down = lax.optimization_barrier(
         (beside, maps, w_gate_up, w_down)
     )
     across = send_y(beside[:dim])
     all_maps = exchange(maps, "ctx")
-    slope, base, gate = block_reads(core[None], mine, theirs, w_heads, gain_head, parts, dim, PER_STEP)
+    slope, base, gate = block_reads(spots, mine, theirs, w_heads, gain_head, parts, dim, PER_STEP)
     across, slope = lax.optimization_barrier((across, slope))
     w_rows = [pair, beside, across, swap_cores(beside), swap_cores(across)]
     gated = emit(
-        place[None], all_maps, state_init[0], slope, base, gate, x_count, y_count * core_count
+        spots, all_maps, state_init[0], slope, base, gate, x_count, y_count * core_count
     )
     heads = y_count * core_count
     gated = exchange(gated, ("y", "core")).reshape(heads, x_count * tok_dev, dim)
-    partial = project(jnp.stack([core, lax.axis_index("y").astype(jnp.int32)]), gated, w_rows, x_count, 512)
+    partial = project(spots, gated, w_rows, x_count, 512)
 
     other_gate_up = swap_cores(far_gate_up)
     other_down = swap_cores(far_down)
@@ -535,14 +574,18 @@
     routes = jnp.stack(pieces(routes), axis=-1).reshape(chips, tok_dev, -1)
     routes = jnp.pad(routes, ((0, 0), (0, 0), (0, LANES - routes.shape[-1])))
 
-    summed, copies = join(exchange(partial, "x"), tokens, gain_expert, routes)
-    received = exchange(copies, ("x", "y"))
-    outputs = experts_of(received, (w_gate_up, w_down), (other_gate_up, other_down), 2)
-    expert_out = total_of(exchange(outputs, ("x", "y")))
+    summed, *copies = join(exchange(partial, "x"), tokens, gain_expert, routes, HALVES)
+    returned = []
+    for part in copies:
+        received = exchange(part, ("x", "y"))
+        outputs = experts_of(received, (w_gate_up, w_down), (other_gate_up, other_down), 2)
+        returned.append(exchange(outputs, ("x", "y")))
+    expert_out = total_of(returned)
     return (summed, expert_out)
 
 
 PER_STEP = 4
+HALVES = 2
 
 
 def solution(mesh):

time: 199 us -> 200 us (level)
  blocking collectives: 63.7 us -> 39.5 us
  starting transfers between devices: 24.9 us -> 36.5 us
  Pallas kernels: 44.2 us -> 53.7 us
  waiting for transfers between devices: 56.4 us -> 60 us
    all_to_all x2, blocking collectives: 63.7 us -> 39.5 us  [exchange(): return lax.all_to_all(value, axes, split_axis=0, concat_axis=0, tiled=True)]
    all_to_all x4 -> x6, starting transfers between devices: 21.9 us -> 34.5 us  [exchange(): return lax.all_to_all(value, axes, split_axis=0, concat_axis=0, tiled=True)]
    pallas_call x1 -> x2, Pallas kernels: 12 us -> 18.6 us  [experts_of(): pl.pallas_call(functools.partial(experts_body, tiles=tiles), grid=(2 * ti...]
    all_to_all x4 -> x6, waiting for transfers between devices: 49.4 us -> 53.6 us  [exchange(): return lax.all_to_all(value, axes, split_axis=0, concat_axis=0, tiled=True)]
    pallas_call x4, Pallas kernels: 10.5 us -> 13.3 us  [the longest x1 6.93 us: join(): pl.pallas_call(functools.partial(join_body, halves=halves), in_specs=[res...]
  transfers between devices with their start and end apart: 12 -> 14, of which waited for: 6 -> 8; matrix products, arithmetic and copies ran while one was open for 3% -> 3% of each run, Pallas kernels for 15% -> 25%
where the time goes in v4:
time: 200 us; the launch traced here: 199 us
  waiting for transfers between devices  60 us (30%)
  Pallas kernels  53.7 us (27%)
  blocking collectives  39.5 us (20%)
  starting transfers between devices  36.5 us (18%)
  local copies, waits for them, and re-layouts  4.19 us (2%)
  between operations  2.82 us (1%)
  other arithmetic  2.7 us (1%)
    all_to_all x6, waiting for transfers between devices, exchange(): return lax.all_to_all(value, axes, split_axis=0, concat_axis=0, tiled=True)  53.6 us
    all_to_all x2, blocking collectives, exchange(): return lax.all_to_all(value, axes, split_axis=0, concat_axis=0, tiled=True)  39.5 us
    all_to_all x6, starting transfers between devices, exchange(): return lax.all_to_all(value, axes, split_axis=0, concat_axis=0, tiled=True)  34.5 us
    pallas_call x2, Pallas kernels, experts_of(): pl.pallas_call(functools.partial(experts_body, tiles=tiles), grid=(2 * ti...  18.6 us
    pallas_call x1, Pallas kernels, block_maps(): pl.pallas_call(functools.partial(maps_body, per_step=per_step), grid=(spa...  11.5 us
    pallas_call x1, Pallas kernels, join(): pl.pallas_call(functools.partial(join_body, halves=halves), in_specs=[res...  6.93 us
    pallas_call x1, Pallas kernels, block_reads(): pl.pallas_call(functools.partial(reads_body, per_step=per_step), grid=(sp...  5.82 us
    pallas_call x1, Pallas kernels, project(): pl.pallas_call(project_body, grid=(width // tile,), in_specs=[pl.BlockSpe...  4.43 us
  transfers between devices with their start and end apart: 14, of which 8 were waited for; matrix products, arithmetic and copies ran while one was open for 3% of the time, Pallas kernels for 25%

profile of v4, /device:TPU:8, one launch (start us, length us, event | category | flops | bytes accessed | tf_op | source)
XLA Modules:
  0.0 199.4 jit_solution(6223951263860259581)
XLA Ops:
  0.6 2.5 %norm_copies.1 = bf16[16,32,2048]{2,1,0:T(8,128)(2,1)} custom-call(bf16[32,2048]{1,0:T(8,128)(2,1)} %tokens_ref.3, f32[1,2048]{1,0:T(1,128)} %bitcast.23), custom_call_target="tpu_custom_call" | custom-call | tf_op jit(solution)/shard_map/norm_copies/pallas_call | solution.py:259
  3.2 0.0 copy-start.5
  3.2 0.0 copy-start.6
  3.2 7.5 %all-to-all-start = ((bf16[16,32,2048]{2,1,0:T(8,128)(2,1)}), bf16[16,32,2048]{2,1,0:T(8,128)(2,1)S(1)}, u32[]{:S(2)}, u32[]{:S(2)}) async-start(bf16[16,32,2048]{2,1,0:T(8,128)(2,1)} %norm_copies.1), calls=%async_computation | async-start | bytes 4194304 | tf_op jit(solution)/shard_map/all_to_all | solution.py:510
  10.7 0.1 collective-permute-start
  10.8 0.3 copy.29
  13.1 0.9 pad.8.ws_ref
  14.0 0.6 pad_add_fusion.core_ref.place_ref
  14.6 0.6 pad_maximum_fusion.2.scal_ref
  15.2 0.0 collective-permute-done
  15.2 1.3 pad_maximum_fusion.refs_0_
  16.5 23.2 %all-to-all-done.mine_ref = bf16[16,32,2048]{2,1,0:T(8,128)(2,1)S(1)} async-done(((bf16[16,32,2048]{2,1,0:T(8,128)(2,1)}), bf16[16,32,2048]{2,1,0:T(8,128)(2,1)S(1)}, u32[]{:S(2)}, u32[]{:S(2)}) %all-to-all-start) | async-done | bytes 2097184 | tf_op jit(solution)/shard_map/all_to_all | solution.py:510
  39.7 0.0 collective-permute-start.2
  39.7 0.0 collective-permute-start.1
  39.8 4.3 %collective-permute-done.2.theirs_ref = bf16[16,32,2048]{2,1,0:T(8,128)(2,1)} collective-permute-done((bf16[16,32,2048]{2,1,0:T(8,128)(2,1)S(1)}, bf16[16,32,2048]{2,1,0:T(8,128)(2,1)}, u32[]{:S(2)}, u32[]{:S(2)}) %collective-permute-start.2) | collective-permute-done | bytes 2097184 | tf_op jit(solution)/shard_map/ppermute | solution.py:506
  44.0 11.5 %block_maps.1 = (bf16[8,128,128]{2,1,0:T(8,128)(2,1)}, f32[8,128,128]{2,1,0:T(8,128)}, f32[8,128,128]{2,1,0:T(8,128)}, bf16[8,128,256]{2,1,0:T(8,128)(2,1)}, bf1...) custom-call(s32[3]{0:T(128)} %pad_add_fusion.core_ref.place_ref, f32[3]{0:T(128)} %pad_maximum_fusion.2.scal_ref, ...), custom_call_target="tpu_custom_call" | custom-call | tf_op jit(solution)/shard_map/block_maps/pallas_call | solution.py:158
  55.6 0.2 collective-permute-start.6
  55.8 8.5 %all-to-all-start.1 = ((bf16[8,128,256]{2,1,0:T(8,128)(2,1)}), bf16[8,128,256]{2,1,0:T(8,128)(2,1)S(1)}, u32[]{:S(2)}, u32[]{:S(2)}) async-start(bf16[8,128,256]{2,1,0:T(8,128)(2,1)} %get-tuple-element.31), calls=%async_computation.1 | async-start | bytes 1048576 | tf_op jit(solution)/shard_map/all_to_all | solution.py:510
  64.3 1.9 slice.3
  66.2 0.0 collective-permute-start.3
  66.2 1.5 collective-permute-start.4
  67.6 5.8 %block_reads.1 = (bf16[1024,128]{1,0:T(8,128)(2,1)}, f32[1024,128]{1,0:T(8,128)}, f32[1024,128]{1,0:T(8,128)}) custom-call(s32[3]{0:T(128)} %pad_add_fusion.core_ref.place_ref, bf16[16,32,2048]{2,1,0:T(8,128)(2,1)} %copy-done, bf16[16,32,2048]{2,1,0:T(8,128)(2,1)} %collective-permute-done.2.theirs_ref, bf16[2048,512]{1,0:T(8,128)(2,1)} %wg_ref.1, ...), custom_call_target="tpu_custom_call" | custom-call | tf_op jit(solution)/shard_map/block_reads/pallas_call | solution.py:218
  73.5 0.0 copy-start.7
  73.5 0.0 copy-start.8
  73.5 2.1 %collective-permute-done.3.refs_2_ = bf16[128,2048]{1,0:T(8,128)(2,1)S(1)} collective-permute-done((bf16[128,2048]{1,0:T(8,128)(2,1)}, bf16[128,2048]{1,0:T(8,128)(2,1)S(1)}, u32[]{:S(2)}, u32[]{:S(2)}) %collective-permute-start.3) | collective-permute-done | bytes 524320 | tf_op jit(solution)/shard_map/ppermute | solution.py:498
  75.6 6.7 %all-to-all-done.1.maps_ref = bf16[8,128,256]{2,1,0:T(8,128)(2,1)S(1)} async-done(((bf16[8,128,256]{2,1,0:T(8,128)(2,1)}), bf16[8,128,256]{2,1,0:T(8,128)(2,1)S(1)}, u32[]{:S(2)}, u32[]{:S(2)}) %all-to-all-start.1) | async-done | bytes 524320 | tf_op jit(solution)/shard_map/all_to_all | solution.py:510
  82.3 3.0 %emit.1 = bf16[8,4,32,128]{3,2,1,0:T(8,128)(2,1)} custom-call(s32[3]{0:T(128)} %pad_add_fusion.core_ref.place_ref, bf16[8,128,256]{2,1,0:T(8,128)(2,1)S(1)} %all-to-all-done.1.maps_ref, f32[128,128]{1,0:T(8,128)} %bitcast.22, bf16[1024,128]{1,0:T(8,128)(2,1)} %get-tuple-element.39.slope_ref, f32[1024,128]{1,0:T(8,128)} %get-tuple-element.40.base_ref, ...), custom_call_target="tpu_custom_call" | custom-call | tf_op jit(solution)/shard_map/emit/pallas_call | solution.py:305
  85.2 5.0 %all-to-all-start.2 = ((bf16[8,4,32,128]{3,2,1,0:T(8,128)(2,1)}), bf16[8,4,32,128]{3,2,1,0:T(8,128)(2,1)S(1)}, u32[]{:S(2)}, u32[]{:S(2)}) async-start(bf16[8,4,32,128]{3,2,1,0:T(8,128)(2,1)} %emit.1), calls=%async_computation.2 | async-start | bytes 524288 | tf_op jit(solution)/shard_map/all_to_all | solution.py:510
  90.3 0.2 select_reduce_fusion
  90.4 0.1 copy.30
  90.6 0.0 collective-permute-done.4.refs_3_
  90.6 5.8 %all-to-all-done.2 = bf16[8,4,32,128]{3,2,1,0:T(8,128)(2,1)S(1)} async-done(((bf16[8,4,32,128]{3,2,1,0:T(8,128)(2,1)}), bf16[8,4,32,128]{3,2,1,0:T(8,128)(2,1)S(1)}, u32[]{:S(2)}, u32[]{:S(2)}) %all-to-all-start.2) | async-done | bytes 262176 | tf_op jit(solution)/shard_map/all_to_all | solution.py:510
  96.4 4.4 %project.1 = bf16[4,32,2048]{2,1,0:T(8,128)(2,1)} custom-call(s32[3]{0:T(128)} %pad_add_fusion.core_ref.place_ref, bf16[8,128,128]{2,1,0:T(8,128)(2,1)S(1)} %bitcast.18, bf16[256,2048]{1,0:T(8,128)(2,1)} %copy-done.1, bf16[256,2048]{1,0:T(8,128)(2,1)} %collective-permute-done.1.refs_1_, bf16[128,2048]{1,0:T(8,128)(2,1)} %copy-done.3, ...), custom_call_target="tpu_custom_call" | custom-call | tf_op jit(solution)/shard_map/project/pallas_call | solution.py:335
  100.8 3.5 %all-to-all-start.3 = ((bf16[4,32,2048]{2,1,0:T(8,128)(2,1)}), bf16[4,32,2048]{2,1,0:T(8,128)(2,1)S(1)}, u32[]{:S(2)}, u32[]{:S(2)}) async-start(bf16[4,32,2048]{2,1,0:T(8,128)(2,1)} %project.1), calls=%async_computation.3 | async-start | bytes 1048576 | tf_op jit(solution)/shard_map/all_to_all | solution.py:510
  104.3 0.1 collective-permute-start.7
  104.5 0.2 copy.34
  104.7 0.7 pad.9.routes_ref
  105.4 8.2 %all-to-all-done.3.parts_ref = bf16[4,32,2048]{2,1,0:T(8,128)(2,1)S(1)} async-done(((bf16[4,32,2048]{2,1,0:T(8,128)(2,1)}), bf16[4,32,2048]{2,1,0:T(8,128)(2,1)S(1)}, u32[]{:S(2)}, u32[]{:S(2)}) %all-to-all-start.3) | async-done | bytes 524320 | tf_op jit(solution)/shard_map/all_to_all | solution.py:510
  113.7 6.9 %join.1 = (bf16[32,2048]{1,0:T(8,128)(2,1)}, bf16[16,16,2176]{2,1,0:T(8,128)(2,1)}, bf16[16,16,2176]{2,1,0:T(8,128)(2,1)}) custom-call(bf16[4,32,2048]{2,1,0:T(8,128)(2,1)S(1)} %all-to-all-done.3.parts_ref, bf16[32,2048]{1,0:T(8,128)(2,1)} %tokens_ref.3, f32[1,2048]{1,0:T(1,128)} %bitcast.24, bf16[16,32,128]{2,1,0:T(8,128)(2,1)} %pad.9.routes_ref), custom_call_target="tpu_custom_call" | custom-call | tf_op jit(solution)/shard_map/join/pallas_call | solution.py:389
  120.6 20.2 %all_to_all.40.x_ref = bf16[16,16,2176]{2,1,0:T(8,128)(2,1)S(1)} all-to-all(bf16[16,16,2176]{2,1,0:T(8,128)(2,1)} %get-tuple-element.47), channel_id=1, replica_groups=mesh['ctx'=8,'x'=4,'y'=4,'core'=2] {'x','y'}, dimensions={0} | all-to-all | bytes 2228224 | tf_op jit(solution)/shard_map/all_to_all | solution.py:510
  140.8 5.1 %all-to-all-start.4 = ((bf16[16,16,2176]{2,1,0:T(8,128)(2,1)}), bf16[16,16,2176]{2,1,0:T(8,128)(2,1)S(1)}, u32[]{:S(2)}, u32[]{:S(2)}) async-start(bf16[16,16,2176]{2,1,0:T(8,128)(2,1)} %get-tuple-element.44), calls=%async_computation.4 | async-start | bytes 2228224 | tf_op jit(solution)/shard_map/all_to_all | solution.py:510
  146.0 9.4 %experts.3 = bf16[16,16,2048]{2,1,0:T(8,128)(2,1)} custom-call(bf16[16,16,2176]{2,1,0:T(8,128)(2,1)S(1)} %all_to_all.40.x_ref, bf16[1,2048,1024]{2,1,0:T(8,128)(2,1)} %up_a_ref.3, bf16[1,2048,1024]{2,1,0:T(8,128)(2,1)} %up_a_ref.3, bf16[1,512,2048]{2,1,0:T(8,128)(2,1)} %down_a_ref.3, bf16[1,2048,1024]{2,1,0:T(8,128)(2,1)} %collective-permute-done.6.gate_b_ref.up_b_ref, ...), custom_call_target="tpu_custom_call" | custom-call | tf_op jit(solution)/shard_map/experts/pallas_call | solution.py:463
  155.3 5.0 %all-to-all-done.4.x_ref = bf16[16,16,2176]{2,1,0:T(8,128)(2,1)S(1)} async-done(((bf16[16,16,2176]{2,1,0:T(8,128)(2,1)}), bf16[16,16,2176]{2,1,0:T(8,128)(2,1)S(1)}, u32[]{:S(2)}, u32[]{:S(2)}) %all-to-all-start.4) | async-done | bytes 1114144 | tf_op jit(solution)/shard_map/all_to_all | solution.py:510
  160.3 4.9 %all-to-all-start.7 = ((bf16[16,16,2048]{2,1,0:T(8,128)(2,1)}), bf16[16,16,2048]{2,1,0:T(8,128)(2,1)S(1)}, u32[]{:S(2)}, u32[]{:S(2)}) async-start(bf16[16,16,2048]{2,1,0:T(8,128)(2,1)} %experts.3), calls=%async_computation.7 | async-start | bytes 2097152 | tf_op jit(solution)/shard_map/all_to_all | solution.py:510
  165.2 9.2 %experts.2 = bf16[16,16,2048]{2,1,0:T(8,128)(2,1)} custom-call(bf16[16,16,2176]{2,1,0:T(8,128)(2,1)S(1)} %all-to-all-done.4.x_ref, bf16[1,2048,1024]{2,1,0:T(8,128)(2,1)} %up_a_ref.3, bf16[1,2048,1024]{2,1,0:T(8,128)(2,1)} %up_a_ref.3, bf16[1,512,2048]{2,1,0:T(8,128)(2,1)} %down_a_ref.3, bf16[1,2048,1024]{2,1,0:T(8,128)(2,1)} %collective-permute-done.6.gate_b_ref.up_b_ref, ...), custom_call_target="tpu_custom_call" | custom-call | tf_op jit(solution)/shard_map/experts/pallas_call | solution.py:463
  174.5 4.6 %all-to-all-done.7.refs_1_ = bf16[16,16,2048]{2,1,0:T(8,128)(2,1)S(1)} async-done(((bf16[16,16,2048]{2,1,0:T(8,128)(2,1)}), bf16[16,16,2048]{2,1,0:T(8,128)(2,1)S(1)}, u32[]{:S(2)}, u32[]{:S(2)}) %all-to-all-start.7) | async-done | bytes 1048608 | tf_op jit(solution)/shard_map/all_to_all | solution.py:510
  179.1 19.3 %all_to_all.41.refs_0_ = bf16[16,16,2048]{2,1,0:T(8,128)(2,1)S(1)} all-to-all(bf16[16,16,2048]{2,1,0:T(8,128)(2,1)} %experts.2), channel_id=1, replica_groups=mesh['ctx'=8,'x'=4,'y'=4,'core'=2] {'x','y'}, dimensions={0} | all-to-all | bytes 2097152 | tf_op jit(solution)/shard_map/all_to_all | solution.py:510
  198.4 0.9 total.1
  (24 shorter events, 0.2 us)
Async XLA Ops:
  3.2 7.6 %copy-start.5 = (bf16[128,2048]{1,0:T(8,128)(2,1)S(1)}, bf16[128,2048]{1,0:T(8,128)(2,1)}, u32[]{:S(2)}) copy-start(bf16[128,2048]{1,0:T(8,128)(2,1)} %param.24) | copy-start | bytes 1572868
  3.2 7.7 %copy-start.6 = (bf16[2048,2]{0,1:T(2,128)(2,1)S(1)}, bf16[2048,2]{0,1:T(2,128)(2,1)}, u32[]{:S(2)}) copy-start(bf16[2048,2]{0,1:T(2,128)(2,1)} %param.18) | copy-start | bytes 24580
  3.2 36.6 %all-to-all-start = ((bf16[16,32,2048]{2,1,0:T(8,128)(2,1)}), bf16[16,32,2048]{2,1,0:T(8,128)(2,1)S(1)}, u32[]{:S(2)}, u32[]{:S(2)}) async-start(bf16[16,32,2048]{2,1,0:T(8,128)(2,1)} %norm_copies.1), calls=%async_computation | async-start | bytes 4194304 | tf_op jit(solution)/shard_map/all_to_all | solution.py:510
  10.7 4.5 %collective-permute-start = (bf16[128,2048]{1,0:T(8,128)(2,1)S(1)}, bf16[128,2048]{1,0:T(8,128)(2,1)}, u32[]{:S(2)}, u32[]{:S(2)}) collective-permute-start(bf16[128,2048]{1,0:T(8,128)(2,1)S(1)} %copy-done.5), channel_id=1, source_target_pairs={{0,1},{1,0},{2,3},{3,2},{4,5},{5,4},{6,7},{7,6},{8,9},{9,8},{10,11... | collective-permute-start | bytes 1572872 | tf_op jit(solution)/shard_map/ppermute | solution.py:506
  16.5 57.0 %copy-start.1 = (bf16[256,2048]{1,0:T(8,128)(2,1)}, bf16[256,2048]{1,0:T(8,128)(2,1)S(1)}, u32[]{:S(2)}) copy-start(bf16[256,2048]{1,0:T(8,128)(2,1)S(1)} %pad_maximum_fusion.refs_0_) | copy-start | bytes 3145732
  39.7 4.3 %copy-start = (bf16[16,32,2048]{2,1,0:T(8,128)(2,1)}, bf16[16,32,2048]{2,1,0:T(8,128)(2,1)S(1)}, u32[]{:S(2)}) copy-start(bf16[16,32,2048]{2,1,0:T(8,128)(2,1)S(1)} %all-to-all-done.mine_ref) | copy-start | bytes 6291460
  39.7 4.3 %collective-permute-start.2 = (bf16[16,32,2048]{2,1,0:T(8,128)(2,1)S(1)}, bf16[16,32,2048]{2,1,0:T(8,128)(2,1)}, u32[]{:S(2)}, u32[]{:S(2)}) collective-permute-start(bf16[16,32,2048]{2,1,0:T(8,128)(2,1)S(1)} %all-to-all-done.mine_ref), channel_id=1, source_target_pairs={{0,1},{1,0},{2,3},{3,2},{4,5},{5,4},{6,7},{7,6},{8,9},{9,8},{10,11... | collective-permute-start | bytes 6291464 | tf_op jit(solution)/shard_map/ppermute | solution.py:506
  39.7 15.8 %collective-permute-start.1 = (bf16[256,2048]{1,0:T(8,128)(2,1)S(1)}, bf16[256,2048]{1,0:T(8,128)(2,1)}, u32[]{:S(2)}, u32[]{:S(2)}) collective-permute-start(bf16[256,2048]{1,0:T(8,128)(2,1)S(1)} %pad_maximum_fusion.refs_0_), channel_id=1, source_target_pairs={{0,2},{2,4},{4,6},{6,0},{1,7},{3,1},{5,3},{7,5},{8,10},{10,12},{12... | collective-permute-start | bytes 3145736 | tf_op jit(solution)/shard_map/ppermute | solution.py:498
  55.6 90.4 %collective-permute-start.6 = (bf16[1,2048,1024]{2,1,0:T(8,128)(2,1)}, bf16[1,2048,1024]{2,1,0:T(8,128)(2,1)}, u32[]{:S(2)}, u32[]{:S(2)}) collective-permute-start(bf16[1,2048,1024]{2,1,0:T(8,128)(2,1)} %up_a_ref.3), channel_id=1, source_target_pairs={{0,1},{1,0},{2,3},{3,2},{4,5},{5,4},{6,7},{7,6},{8,9},{9,8},{10,11... | collective-permute-start | bytes 12582920 | tf_op jit(solution)/shard_map/ppermute | solution.py:506
  55.8 26.5 %all-to-all-start.1 = ((bf16[8,128,256]{2,1,0:T(8,128)(2,1)}), bf16[8,128,256]{2,1,0:T(8,128)(2,1)S(1)}, u32[]{:S(2)}, u32[]{:S(2)}) async-start(bf16[8,128,256]{2,1,0:T(8,128)(2,1)} %get-tuple-element.31), calls=%async_computation.1 | async-start | bytes 1048576 | tf_op jit(solution)/shard_map/all_to_all | solution.py:510
  66.2 9.4 %collective-permute-start.3 = (bf16[128,2048]{1,0:T(8,128)(2,1)}, bf16[128,2048]{1,0:T(8,128)(2,1)S(1)}, u32[]{:S(2)}, u32[]{:S(2)}) collective-permute-start(bf16[128,2048]{1,0:T(8,128)(2,1)} %slice.3), channel_id=1, source_target_pairs={{0,2},{2,4},{4,6},{6,0},{1,7},{3,1},{5,3},{7,5},{8,10},{10,12},{12... | collective-permute-start | bytes 1572872 | tf_op jit(solution)/shard_map/ppermute | solution.py:498
  66.2 24.4 %collective-permute-start.4 = (bf16[256,2048]{1,0:T(8,128)(2,1)}, bf16[256,2048]{1,0:T(8,128)(2,1)S(1)}, u32[]{:S(2)}, u32[]{:S(2)}) collective-permute-start(bf16[256,2048]{1,0:T(8,128)(2,1)} %collective-permute-done.1.refs_1_), channel_id=1, source_target_pairs={{0,1},{1,0},{2,3},{3,2},{4,5},{5,4},{6,7},{7,6},{8,9},{9,8},{10,11... | collective-permute-start | bytes 3145736 | tf_op jit(solution)/shard_map/ppermute | solution.py:506
  73.5 16.8 %copy-start.7 = (f32[32,10]{0,1:T(8,128)S(1)}, f32[32,10]{0,1:T(8,128)}, u32[]{:S(2)}) copy-start(f32[32,10]{0,1:T(8,128)} %param.27) | copy-start | bytes 3844
  73.5 16.8 %copy-start.8 = (s32[32,10]{0,1:T(8,128)S(1)}, s32[32,10]{0,1:T(8,128)}, u32[]{:S(2)}) copy-start(s32[32,10]{0,1:T(8,128)} %param.26) | copy-start | bytes 3844
  75.5 20.8 %copy-start.3 = (bf16[128,2048]{1,0:T(8,128)(2,1)}, bf16[128,2048]{1,0:T(8,128)(2,1)S(1)}, u32[]{:S(2)}) copy-start(bf16[128,2048]{1,0:T(8,128)(2,1)S(1)} %collective-permute-done.3.refs_2_) | copy-start | bytes 1572868
  75.6 15.0 %collective-permute-start.5 = (bf16[128,2048]{1,0:T(8,128)(2,1)S(1)}, bf16[128,2048]{1,0:T(8,128)(2,1)S(1)}, u32[]{:S(2)}, u32[]{:S(2)}) collective-permute-start(bf16[128,2048]{1,0:T(8,128)(2,1)S(1)} %collective-permute-done.3.refs_2_), channel_id=1, source_target_pairs={{0,1},{1,0},{2,3},{3,2},{4,5},{5,4},{6,7},{7,6},{8,9},{9,8},{10,11... | collective-permute-start | bytes 1572872 | tf_op jit(solution)/shard_map/ppermute | solution.py:506
  85.2 11.2 %all-to-all-start.2 = ((bf16[8,4,32,128]{3,2,1,0:T(8,128)(2,1)}), bf16[8,4,32,128]{3,2,1,0:T(8,128)(2,1)S(1)}, u32[]{:S(2)}, u32[]{:S(2)}) async-start(bf16[8,4,32,128]{3,2,1,0:T(8,128)(2,1)} %emit.1), calls=%async_computation.2 | async-start | bytes 524288 | tf_op jit(solution)/shard_map/all_to_all | solution.py:510
  90.6 5.8 %copy-start.4 = (bf16[128,2048]{1,0:T(8,128)(2,1)}, bf16[128,2048]{1,0:T(8,128)(2,1)S(1)}, u32[]{:S(2)}) copy-start(bf16[128,2048]{1,0:T(8,128)(2,1)S(1)} %collective-permute-done.5.refs_4_) | copy-start | bytes 1572868
  90.6 5.8 %copy-start.2 = (bf16[256,2048]{1,0:T(8,128)(2,1)}, bf16[256,2048]{1,0:T(8,128)(2,1)S(1)}, u32[]{:S(2)}) copy-start(bf16[256,2048]{1,0:T(8,128)(2,1)S(1)} %collective-permute-done.4.refs_3_) | copy-start | bytes 3145732
  100.8 12.8 %all-to-all-start.3 = ((bf16[4,32,2048]{2,1,0:T(8,128)(2,1)}), bf16[4,32,2048]{2,1,0:T(8,128)(2,1)S(1)}, u32[]{:S(2)}, u32[]{:S(2)}) async-start(bf16[4,32,2048]{2,1,0:T(8,128)(2,1)} %project.1), calls=%async_computation.3 | async-start | bytes 1048576 | tf_op jit(solution)/shard_map/all_to_all | solution.py:510
  104.3 41.6 %collective-permute-start.7 = (bf16[1,512,2048]{2,1,0:T(8,128)(2,1)}, bf16[1,512,2048]{2,1,0:T(8,128)(2,1)}, u32[]{:S(2)}, u32[]{:S(2)}) collective-permute-start(bf16[1,512,2048]{2,1,0:T(8,128)(2,1)} %down_a_ref.3), channel_id=1, source_target_pairs={{0,1},{1,0},{2,3},{3,2},{4,5},{5,4},{6,7},{7,6},{8,9},{9,8},{10,11... | collective-permute-start | bytes 6291464 | tf_op jit(solution)/shard_map/ppermute | solution.py:506
  140.8 19.5 %all-to-all-start.4 = ((bf16[16,16,2176]{2,1,0:T(8,128)(2,1)}), bf16[16,16,2176]{2,1,0:T(8,128)(2,1)S(1)}, u32[]{:S(2)}, u32[]{:S(2)}) async-start(bf16[16,16,2176]{2,1,0:T(8,128)(2,1)} %get-tuple-element.44), calls=%async_computation.4 | async-start | bytes 2228224 | tf_op jit(solution)/shard_map/all_to_all | solution.py:510
  160.3 18.8 %all-to-all-start.7 = ((bf16[16,16,2048]{2,1,0:T(8,128)(2,1)}), bf16[16,16,2048]{2,1,0:T(8,128)(2,1)S(1)}, u32[]{:S(2)}, u32[]{:S(2)}) async-start(bf16[16,16,2048]{2,1,0:T(8,128)(2,1)} %experts.3), calls=%async_computation.7 | async-start | bytes 2097152 | tf_op jit(solution)/shard_map/all_to_all | solution.py:510

commit v5 on v4

--- a/solution.py
+++ b/solution.py
@@ -33,6 +33,10 @@
     return slice(n * CHUNK, (n + 1) * CHUNK)
 
 
+def room(mebibytes):
+    return pltpu.CompilerParams(vmem_limit_bytes=mebibytes * 1024 * 1024)
+
+
 def resident():
     return pl.BlockSpec(memory_space=pltpu.VMEM)
 
@@ -41,33 +45,42 @@
     return pl.BlockSpec(shape, lambda i: (0,) * len(shape))
 
 
-def project_rows(core, mine_ref, theirs_ref, w):
-    groups, each, width = mine_ref.shape
-    ours = jnp.dot(mine_ref[...].reshape(groups * each, width), w, preferred_element_type=F32)
-    others = jnp.dot(theirs_ref[...].reshape(groups * each, width), w, preferred_element_type=F32)
+def project_rows(core, mine, theirs, w):
+    groups, each, width = mine.shape
+    ours = jnp.dot(mine.reshape(groups * each, width), w, preferred_element_type=F32)
+    others = jnp.dot(theirs.reshape(groups * each, width), w, preferred_element_type=F32)
     even = jnp.where(core == 0, ours, others)
     odd = jnp.where(core == 0, others, ours)
     rows = []
     for group in range(groups):
         at = slice(group * each, (group + 1) * each)
         rows += [even[at], odd[at]]
-    return jnp.concatenate(rows, axis=0)
+    return rows
 
 
 def maps_body(
-    core_ref, scal_ref, mine_ref, theirs_ref, wk_ref, wv_ref, ws_ref,
-    key_ref, decay_ref, growth_ref, solved_ref, start_ref, maps_ref, carry_ref,
-    *, per_step,
+    core_ref, scal_ref, mine_ref, theirs_ref, w_ref, ws_ref,
+    key_ref, decay_ref, growth_ref, solved_ref, start_ref, maps_ref,
+    mine_buf, theirs_buf, w_buf, ws_buf, sems,
+    *, parts,
 ):
-    dim = wk_ref.shape[1]
-    step = pl.program_id(0)
-
-    @pl.when(step == 0)
-    def _():
-        rows = lax.broadcasted_iota(jnp.int32, (dim, 2 * dim), 0)
-        cols = lax.broadcasted_iota(jnp.int32, (dim, 2 * dim), 1)
-        carry_ref[...] = jnp.where(rows == cols, 1.0, 0.0).astype(F32)
-
+    dim = maps_ref.shape[1]
+    groups = mine_ref.shape[0] // parts
+    w_copies = [
+        pltpu.make_async_copy(w_ref.at[:, pl.ds(dim, 2 * dim)], w_buf, sems.at[0]),
+        pltpu.make_async_copy(ws_ref, ws_buf, sems.at[1]),
+    ]
+    x_copies = []
+    for part in range(parts):
+        at = pl.ds(part * groups, groups)
+        x_copies.append(
+            [
+                pltpu.make_async_copy(mine_ref.at[at], mine_buf.at[at], sems.at[2 + 2 * part]),
+                pltpu.make_async_copy(theirs_ref.at[at], theirs_buf.at[at], sems.at[3 + 2 * part]),
+            ]
+        )
+    for copy in w_copies + [copy for both in x_copies for copy in both]:
+        copy.start()
     lift = scal_ref[0]
     rate = scal_ref[1]
     bias = scal_ref[2]
@@ -78,10 +91,18 @@
     strict = rows > cols
     lower_ones = jnp.where(lower, 1.0, 0.0).astype(BF16)
     eye = jnp.where(rows == cols, 1.0, 0.0).astype(F32)
-    w_all = jnp.concatenate([wk_ref[...], wv_ref[...], ws_ref[...]], axis=1)
-    projected = project_rows(core_ref[0], mine_ref, theirs_ref, w_all)
+    for copy in w_copies:
+        copy.wait()
+    w_all = jnp.concatenate([w_buf[...], ws_buf[...]], axis=1)
+    rows_of = []
+    for part in range(parts):
+        for copy in x_copies[part]:
+            copy.wait()
+        at = slice(part * groups, (part + 1) * groups)
+        rows_of += project_rows(core_ref[0], mine_buf[at], theirs_buf[at], w_all)
+    projected = jnp.concatenate(rows_of, axis=0)
     logits = projected[:, 2 * dim:]
-    every = range(per_step)
+    every = range(projected.shape[0] // CHUNK)
     key_raw = [projected[chunk_of(n), :dim] for n in every]
     value = [projected[chunk_of(n), dim:2 * dim] for n in every]
     strength = [jax.nn.sigmoid(logits[chunk_of(n), 0:1] + lift) for n in every]
@@ -132,45 +153,25 @@
         decay_ref[n] = decay[n]
         growth_ref[n] = growth[n]
         solved_ref[n] = solved[n]
-    carried = carry_ref[...]
+    wide_rows = lax.broadcasted_iota(jnp.int32, (dim, 2 * dim), 0)
+    wide_cols = lax.broadcasted_iota(jnp.int32, (dim, 2 * dim), 1)
+    carried = jnp.where(wide_rows == wide_cols, 1.0, 0.0).astype(F32)
     for n in every:
         start_ref[n] = carried.astype(BF16)
         falls = jnp.concatenate([fall[n], fall[n]], axis=1)
         moved = falls * carried - mm(drive[n][:, dim:], carried)
         carried = jnp.concatenate([moved[:, :dim], moved[:, dim:] + drive[n][:, :dim]], axis=1)
-    carry_ref[...] = carried
-
-    @pl.when(step == pl.num_programs(0) - 1)
-    def _():
-        maps_ref[...] = jnp.broadcast_to(carried.astype(BF16)[None], maps_ref.shape)
-
-
-def block_maps(core, scalars, mine, theirs, w, ws, dim, copies, per_step):
+    maps_ref[...] = jnp.broadcast_to(carried.astype(BF16)[None], maps_ref.shape)
+
+
+def block_maps(core, scalars, mine, theirs, w, ws, dim, copies, parts):
     groups, each, width = mine.shape
-    span = 2 * groups * each
-    rows = per_step * CHUNK
-    x_spec = pl.BlockSpec((rows // (2 * each), each, width), lambda i: (i, 0, 0))
-    count = span // CHUNK
-
-    def stacked(size):
-        return pl.BlockSpec((per_step, CHUNK, size), lambda i: (i, 0, 0))
-
-    return pl.pallas_call(
-        functools.partial(maps_body, per_step=per_step),
-        grid=(span // rows,),
-        in_specs=[
-            pl.BlockSpec(memory_space=pltpu.SMEM),
-            pl.BlockSpec(memory_space=pltpu.SMEM),
-            x_spec,
-            x_spec,
-            pl.BlockSpec((width, dim), lambda i: (0, 1)),
-            pl.BlockSpec((width, dim), lambda i: (0, 2)),
-            whole(ws.shape),
-        ],
-        out_specs=[
-            stacked(CHUNK), stacked(CHUNK), stacked(dim), stacked(2 * dim), stacked(2 * dim),
-            whole((copies, dim, 2 * dim)),
-        ],
+    count = 2 * groups * each // CHUNK
+    scalar = pl.BlockSpec(memory_space=pltpu.SMEM)
+    anywhere = pl.BlockSpec(memory_space=pl.ANY)
+    return pl.pallas_call(
+        functools.partial(maps_body, parts=parts),
+        in_specs=[scalar, scalar] + [anywhere] * 4,
         out_shape=[
             jax.ShapeDtypeStruct((count, dim, CHUNK), BF16),
             jax.ShapeDtypeStruct((count, CHUNK, CHUNK), F32),
@@ -179,9 +180,15 @@
             jax.ShapeDtypeStruct((count, dim, 2 * dim), BF16),
             jax.ShapeDtypeStruct((copies, dim, 2 * dim), BF16),
         ],
-        scratch_shapes=[pltpu.VMEM((dim, 2 * dim), F32)],
+        scratch_shapes=[
+            pltpu.VMEM(mine.shape, BF16),
+            pltpu.VMEM(theirs.shape, BF16),
+            pltpu.VMEM((width, 2 * dim), BF16),
+            pltpu.VMEM(ws.shape, BF16),
+            pltpu.SemaphoreType.DMA((2 + 2 * parts,)),
+        ],
         name="block_maps",
-    )(core, scalars, mine, theirs, w, w, ws)
+    )(core, scalars, mine, theirs, w, ws)
 
 
 def reads_body(
@@ -191,7 +198,9 @@
 ):
     dim = wq_ref.shape[1]
     w_pair = jnp.concatenate([wq_ref[...], wg_ref[...]], axis=1)
-    projected = project_rows(core_ref[0], mine_ref, theirs_ref, w_pair)
+    projected = jnp.concatenate(
+        project_rows(core_ref[0], mine_ref[...], theirs_ref[...], w_pair), axis=0
+    )
     every = range(per_step)
     query = [projected[chunk_of(n), :dim] for n in every]
     scores = [mm(query[n], key_ref[n]) * decay_ref[n] for n in every]
@@ -344,131 +353,78 @@
     )(place, near(gated), *weights)
 
 
-def join_body(parts_ref, tokens_ref, gain_ref, routes_ref, out_ref, *refs, halves):
-    copies_refs, (normed_ref, sems) = refs[:halves], refs[halves:]
-    rows, width = tokens_ref.shape
-    copies = routes_ref.shape[0]
-    each = rows // halves
-    extra = [
-        pltpu.make_async_copy(
-            routes_ref.at[:, pl.ds(half * each, each), :],
-            copies_refs[half].at[:, :, pl.ds(width, routes_ref.shape[2])],
-            sems.at[half * (copies + 1) + copies],
-        )
-        for half in range(halves)
-    ]
-    for copy in extra:
-        copy.start()
+def join_body(parts_ref, tokens_ref, gain_ref, _, out_ref, copies_ref, normed_ref, sems):
+    width = tokens_ref.shape[1]
     total = parts_ref[0].astype(F32)
     for part in range(1, parts_ref.shape[0]):
         total = total + parts_ref[part].astype(F32)
     summed = total.astype(BF16)
-    out_ref[...] = summed
     hidden = tokens_ref[...].astype(F32) + summed.astype(F32)
     normed_ref[...] = (hidden * rms_scale(hidden) * gain_ref[...]).astype(BF16)
-    send_copies(
-        [
-            pltpu.make_async_copy(
-                normed_ref.at[pl.ds(half * each, each), :],
-                copies_refs[half].at[at, :, pl.ds(0, width)],
-                sems.at[half * (copies + 1) + at],
-            )
-            for half in range(halves)
-            for at in range(copies)
-        ]
-    )
-    for copy in extra:
+    copies = [
+        pltpu.make_async_copy(normed_ref, copies_ref.at[at, :, pl.ds(0, width)], sems.at[at])
+        for at in range(copies_ref.shape[0])
+    ]
+    for copy in copies:
+        copy.start()
+    out_ref[...] = summed
+    for copy in copies:
         copy.wait()
 
 
-def join(parts, tokens, gain, routes, halves):
-    copies, rows, extra = routes.shape
-    width = tokens.shape[1]
+def join(parts, tokens, gain, payload):
     anywhere = pl.BlockSpec(memory_space=pl.ANY)
-    shape = jax.ShapeDtypeStruct((copies, rows // halves, width + extra), BF16)
-    return pl.pallas_call(
-        functools.partial(join_body, halves=halves),
+    return pl.pallas_call(
+        join_body,
         in_specs=[resident(), resident(), resident(), anywhere],
-        out_specs=[resident()] + [anywhere] * halves,
-        out_shape=[jax.ShapeDtypeStruct(tokens.shape, BF16)] + [shape] * halves,
+        out_specs=[resident(), anywhere],
+        out_shape=[
+            jax.ShapeDtypeStruct(tokens.shape, BF16),
+            jax.ShapeDtypeStruct(payload.shape, BF16),
+        ],
+        input_output_aliases={3: 1},
         scratch_shapes=[
             pltpu.VMEM(tokens.shape, BF16),
-            pltpu.SemaphoreType.DMA((halves * (copies + 1),)),
+            pltpu.SemaphoreType.DMA((payload.shape[0],)),
         ],
         name="join",
-    )(near(parts), tokens, gain[None], routes)
-
-
-def experts_body(
-    x_ref, gate_a_ref, up_a_ref, down_a_ref, gate_b_ref, up_b_ref, down_b_ref, out_ref,
-    rows_ref, total_ref,
-    *, tiles,
-):
-    step = pl.program_id(0)
+    )(near(parts), tokens, gain[None], payload)
+
+
+def experts_body(x_ref, up_a_ref, down_a_ref, up_b_ref, down_b_ref, out_ref, *, tiles):
     groups, each, width = out_ref.shape
     count = groups * each
-
-    def tile(gate_ref, up_ref, down_ref):
-        x = x_ref[:, :, :width].reshape(count, width)
-        gate = jnp.dot(x, gate_ref[0], preferred_element_type=F32)
-        up = jnp.dot(x, up_ref[0], preferred_element_type=F32)
-        activated = (gate * jax.nn.sigmoid(gate) * up).astype(BF16)
-        return jnp.dot(activated, down_ref[0], preferred_element_type=F32)
-
-    def weight(which):
-        extra = x_ref[:, :, width:].astype(F32).reshape(count, -1)
+    hidden_units = down_a_ref.shape[1]
+    tile = hidden_units // tiles
+    x = x_ref[:, :, :width].reshape(count, width)
+    extra = x_ref[:, :, width:].astype(F32).reshape(count, -1)
+    total = None
+    for which, (up_ref, down_ref) in enumerate(((up_a_ref, down_a_ref), (up_b_ref, down_b_ref))):
+        pre = jnp.dot(x, up_ref[0], preferred_element_type=F32)
+        gate = pre[:, :hidden_units]
+        activated = (gate * jax.nn.sigmoid(gate) * pre[:, hidden_units:]).astype(BF16)
+        rows = jnp.dot(activated, down_ref[0], preferred_element_type=F32)
         first = 3 * which
-        return (
+        weight = (
             extra[:, first:first + 1]
             + extra[:, first + 1:first + 2]
             + extra[:, first + 2:first + 3]
         )
-
-    for which, refs in enumerate(
-        ((gate_a_ref, up_a_ref, down_a_ref), (gate_b_ref, up_b_ref, down_b_ref))
-    ):
-        for part in range(tiles):
-
-            @pl.when(step == which * tiles + part)
-            def _(refs=refs, which=which, part=part):
-                rows = tile(*refs)
-                if part > 0:
-                    rows = rows_ref[...] + rows
-                if part < tiles - 1:
-                    rows_ref[...] = rows
-                else:
-                    scaled = rows.astype(BF16).astype(F32) * weight(which)
-                    if which == 0:
-                        total_ref[...] = scaled
-                    else:
-                        out_ref[...] = (total_ref[...] + scaled).astype(BF16).reshape(out_ref.shape)
+        scaled = rows.astype(BF16).astype(F32) * weight
+        total = scaled if total is None else total + scaled
+    out_ref[...] = total.astype(BF16).reshape(out_ref.shape)
 
 
 def experts_of(x, first, second, tiles):
-    groups, each, wide = x.shape
-    rows = groups * each
-    hidden_units, width = first[1].shape[1:]
-    tile = hidden_units // tiles
-
-    def specs(start):
-        def at(i):
-            return jnp.clip(i - start, 0, tiles - 1)
-
-        return [
-            pl.BlockSpec((1, width, tile), lambda i: (0, 0, at(i))),
-            pl.BlockSpec((1, width, tile), lambda i: (0, 0, tiles + at(i))),
-            pl.BlockSpec((1, tile, width), lambda i: (0, at(i), 0)),
-        ]
-
+    groups, each, _ = x.shape
+    width = first[1].shape[2]
     return pl.pallas_call(
         functools.partial(experts_body, tiles=tiles),
-        grid=(2 * tiles,),
-        in_specs=[resident()] + specs(0) + specs(tiles),
-        out_specs=resident(),
+        in_specs=[resident()] * 5,
         out_shape=jax.ShapeDtypeStruct((groups, each, width), BF16),
-        scratch_shapes=[pltpu.VMEM((rows, width), F32), pltpu.VMEM((rows, width), F32)],
+        compiler_params=room(28),
         name="experts",
-    )(near(x), first[0], first[0], first[1], second[0], second[0], second[1])
+    )(near(x), *[near(part) for part in first + second])
 
 
 def total_body(*refs):
@@ -548,10 +504,8 @@
     theirs = swap_cores(mine)
     beside = send_y(pair)
 
-    *parts, maps = block_maps(spots, scalars, mine, theirs, w_heads, w_logit, dim, ctx_count, PER_STEP)
-    beside, maps, far_gate_up, far_down = lax.optimization_barrier(
-        (beside, maps, w_gate_up, w_down)
-    )
+    *parts, maps = block_maps(spots, scalars, mine, theirs, w_heads, w_logit, dim, ctx_count, 4)
+    beside, maps = lax.optimization_barrier((beside, maps))
     across = send_y(beside[:dim])
     all_maps = exchange(maps, "ctx")
     slope, base, gate = block_reads(spots, mine, theirs, w_heads, gain_head, parts, dim, PER_STEP)
@@ -562,30 +516,26 @@
     )
     heads = y_count * core_count
     gated = exchange(gated, ("y", "core")).reshape(heads, x_count * tok_dev, dim)
-    partial = project(spots, gated, w_rows, x_count, 512)
-
-    other_gate_up = swap_cores(far_gate_up)
-    other_down = swap_cores(far_down)
+    partial = project(spots, gated, w_rows, x_count, 1024)
+
     numbers = jnp.arange(expert_total, dtype=jnp.int32)
     named = expert_ids[:, :, None] == numbers[None, None, :]
     routes = jnp.sum(jnp.where(named, gate_weights[:, :, None], 0.0), axis=1)
     routes = routes.reshape(tok_dev, chips, core_count).transpose(1, 0, 2)
     routes = jnp.where(core == 0, routes, routes[:, :, ::-1])
     routes = jnp.stack(pieces(routes), axis=-1).reshape(chips, tok_dev, -1)
-    routes = jnp.pad(routes, ((0, 0), (0, 0), (0, LANES - routes.shape[-1])))
-
-    summed, *copies = join(exchange(partial, "x"), tokens, gain_expert, routes, HALVES)
-    returned = []
-    for part in copies:
-        received = exchange(part, ("x", "y"))
-        outputs = experts_of(received, (w_gate_up, w_down), (other_gate_up, other_down), 2)
-        returned.append(exchange(outputs, ("x", "y")))
-    expert_out = total_of(returned)
+    payload = jnp.pad(routes, ((0, 0), (0, 0), (width, LANES - routes.shape[-1])))
+
+    summed, copies = join(exchange(partial, "x"), tokens, gain_expert, payload)
+    far_gate_up, far_down, summed = lax.optimization_barrier((w_gate_up, w_down, summed))
+    swapped = (swap_cores(far_gate_up), swap_cores(far_down))
+    received = exchange(copies, ("x", "y"))
+    outputs = experts_of(received, (w_gate_up, w_down), swapped, 2)
+    expert_out = total_of([exchange(outputs, ("x", "y"))])
     return (summed, expert_out)
 
 
 PER_STEP = 4
-HALVES = 2
 
 
 def solution(mesh):

time: 200 us -> 188 us (0.940)
  blocking collectives: 39.5 us -> 65.3 us
  Pallas kernels: 53.7 us -> 35.4 us
  starting transfers between devices: 36.5 us -> 25.5 us
  waiting for transfers between devices: 60 us -> 50.6 us
    all_to_all x2, blocking collectives: 39.5 us -> 65.3 us  [exchange(): return lax.all_to_all(value, axes, split_axis=0, concat_axis=0, tiled=True)]
    pallas_call x4 -> x3, Pallas kernels: 37 us -> 19.8 us  [the longest x1 9.81 us: block_maps(): pl.pallas_call(functools.partial(maps_body, parts=parts), in_specs=[scala...]
    all_to_all x6 -> x4, waiting for transfers between devices: 53.6 us -> 41.9 us  [exchange(): return lax.all_to_all(value, axes, split_axis=0, concat_axis=0, tiled=True)]
    all_to_all x6 -> x4, starting transfers between devices: 34.5 us -> 24.2 us  [exchange(): return lax.all_to_all(value, axes, split_axis=0, concat_axis=0, tiled=True)]
    ppermute x2, waiting for transfers between devices: 2.06 us -> 4.42 us  [send_y(): return lax.ppermute(value, ('y', 'core'), up + down)]
  transfers between devices with their start and end apart: 14 -> 12, of which waited for: 8 -> 7; matrix products, arithmetic and copies ran while one was open for 3% -> 4% of each run, Pallas kernels for 25% -> 10%
where the time goes in v5:
time: 188 us; the launch traced here: 187 us
  blocking collectives  65.3 us (35%)
  waiting for transfers between devices  50.6 us (27%)
  Pallas kernels  35.4 us (19%)
  starting transfers between devices  25.5 us (14%)
  local copies, waits for them, and re-layouts  5.06 us (3%)
  between operations  2.82 us (2%)
  other arithmetic  2.68 us (1%)
    all_to_all x2, blocking collectives, exchange(): return lax.all_to_all(value, axes, split_axis=0, concat_axis=0, tiled=True)  65.3 us
    all_to_all x4, waiting for transfers between devices, exchange(): return lax.all_to_all(value, axes, split_axis=0, concat_axis=0, tiled=True)  41.9 us
    all_to_all x4, starting transfers between devices, exchange(): return lax.all_to_all(value, axes, split_axis=0, concat_axis=0, tiled=True)  24.2 us
    pallas_call x1, Pallas kernels, block_maps(): pl.pallas_call(functools.partial(maps_body, parts=parts), in_specs=[scala...  9.81 us
    pallas_call x1, Pallas kernels, experts_of(): pl.pallas_call(functools.partial(experts_body, tiles=tiles), in_specs=[re...  6.73 us
    pallas_call x1, Pallas kernels, block_reads(): pl.pallas_call(functools.partial(reads_body, per_step=per_step), grid=(sp...  5.83 us
    ppermute x2, waiting for transfers between devices, send_y(): return lax.ppermute(value, ('y', 'core'), up + down)  4.42 us
    ppermute x6, waiting for transfers between devices, swap_cores(): return lax.ppermute(value, 'core', [(0, 1), (1, 0)])  4.3 us
  transfers between devices with their start and end apart: 12, of which 7 were waited for; matrix products, arithmetic and copies ran while one was open for 4% of the time, Pallas kernels for 10%

profile of v5, /device:TPU:8, one launch (start us, length us, event | category | flops | bytes accessed | tf_op | source)
XLA Modules:
  0.0 187.3 jit_solution(15429676123491160360)
XLA Ops:
  0.6 2.5 %norm_copies.1 = bf16[16,32,2048]{2,1,0:T(8,128)(2,1)} custom-call(bf16[32,2048]{1,0:T(8,128)(2,1)} %tokens_ref.3, f32[1,2048]{1,0:T(1,128)} %bitcast.23), custom_call_target="tpu_custom_call" | custom-call | tf_op jit(solution)/shard_map/norm_copies/pallas_call | solution.py:268
  3.2 0.0 copy-start.7
  3.2 0.0 copy-start.8
  3.2 7.5 %all-to-all-start = ((bf16[16,32,2048]{2,1,0:T(8,128)(2,1)}), bf16[16,32,2048]{2,1,0:T(8,128)(2,1)S(1)}, u32[]{:S(2)}, u32[]{:S(2)}) async-start(bf16[16,32,2048]{2,1,0:T(8,128)(2,1)} %norm_copies.1), calls=%async_computation | async-start | bytes 4194304 | tf_op jit(solution)/shard_map/all_to_all | solution.py:466
  10.7 0.1 collective-permute-start
  10.8 0.3 copy.30
  13.1 0.9 pad.8.ws_ref
  14.0 0.6 pad_add_fusion.core_ref.place_ref
  14.6 0.6 pad_maximum_fusion.2.scal_ref
  15.2 0.0 collective-permute-done
  15.2 1.3 pad_maximum_fusion.refs_0_
  16.5 23.3 %all-to-all-done.mine_ref = bf16[16,32,2048]{2,1,0:T(8,128)(2,1)S(1)} async-done(((bf16[16,32,2048]{2,1,0:T(8,128)(2,1)}), bf16[16,32,2048]{2,1,0:T(8,128)(2,1)S(1)}, u32[]{:S(2)}, u32[]{:S(2)}) %all-to-all-start) | async-done | bytes 2097184 | tf_op jit(solution)/shard_map/all_to_all | solution.py:466
  39.7 0.0 collective-permute-start.2
  39.7 0.0 collective-permute-start.1
  39.7 4.3 %collective-permute-done.2.theirs_ref = bf16[16,32,2048]{2,1,0:T(8,128)(2,1)} collective-permute-done((bf16[16,32,2048]{2,1,0:T(8,128)(2,1)S(1)}, bf16[16,32,2048]{2,1,0:T(8,128)(2,1)}, u32[]{:S(2)}, u32[]{:S(2)}) %collective-permute-start.2) | collective-permute-done | bytes 2097184 | tf_op jit(solution)/shard_map/ppermute | solution.py:462
  44.0 9.8 %block_maps.1 = (bf16[8,128,128]{2,1,0:T(8,128)(2,1)}, f32[8,128,128]{2,1,0:T(8,128)}, f32[8,128,128]{2,1,0:T(8,128)}, bf16[8,128,256]{2,1,0:T(8,128)(2,1)}, bf1...) custom-call(s32[3]{0:T(128)} %pad_add_fusion.core_ref.place_ref, f32[3]{0:T(128)} %pad_maximum_fusion.2.scal_ref, ...), custom_call_target="tpu_custom_call" | custom-call | tf_op jit(solution)/shard_map/block_maps/pallas_call | solution.py:172
  53.8 0.8 collective-permute-done.1.refs_1_
  54.6 8.5 %all-to-all-start.1 = ((bf16[8,128,256]{2,1,0:T(8,128)(2,1)}), bf16[8,128,256]{2,1,0:T(8,128)(2,1)S(1)}, u32[]{:S(2)}, u32[]{:S(2)}) async-start(bf16[8,128,256]{2,1,0:T(8,128)(2,1)} %get-tuple-element.31), calls=%async_computation.1 | async-start | bytes 1048576 | tf_op jit(solution)/shard_map/all_to_all | solution.py:466
  63.1 1.9 %slice.3 = bf16[128,2048]{1,0:T(8,128)(2,1)} slice(bf16[256,2048]{1,0:T(8,128)(2,1)} %collective-permute-done.1.refs_1_), slice={[0:128], [0:2048]} | slice | bytes 1048576 | tf_op jit(solution)/shard_map/slice | solution.py:509
  65.0 0.0 collective-permute-start.3
  65.0 0.6 collective-permute-start.4
  65.6 5.8 %block_reads.1 = (bf16[1024,128]{1,0:T(8,128)(2,1)}, f32[1024,128]{1,0:T(8,128)}, f32[1024,128]{1,0:T(8,128)}) custom-call(s32[3]{0:T(128)} %pad_add_fusion.core_ref.place_ref, bf16[16,32,2048]{2,1,0:T(8,128)(2,1)} %copy-done.2, bf16[16,32,2048]{2,1,0:T(8,128)(2,1)} %collective-permute-done.2.theirs_ref, bf16[2048,512]{1,0:T(8,128)(2,1)} %wg_ref.1, ...), custom_call_target="tpu_custom_call" | custom-call | tf_op jit(solution)/shard_map/block_reads/pallas_call | solution.py:227
  71.4 0.0 copy-start.9
  71.4 0.0 copy-start.10
  71.4 3.6 %collective-permute-done.3.refs_2_ = bf16[128,2048]{1,0:T(8,128)(2,1)S(1)} collective-permute-done((bf16[128,2048]{1,0:T(8,128)(2,1)}, bf16[128,2048]{1,0:T(8,128)(2,1)S(1)}, u32[]{:S(2)}, u32[]{:S(2)}) %collective-permute-start.3) | collective-permute-done | bytes 524320 | tf_op jit(solution)/shard_map/ppermute | solution.py:454
  75.1 0.0 collective-permute-start.5
  75.1 5.4 %all-to-all-done.1.maps_ref = bf16[8,128,256]{2,1,0:T(8,128)(2,1)S(1)} async-done(((bf16[8,128,256]{2,1,0:T(8,128)(2,1)}), bf16[8,128,256]{2,1,0:T(8,128)(2,1)S(1)}, u32[]{:S(2)}, u32[]{:S(2)}) %all-to-all-start.1) | async-done | bytes 524320 | tf_op jit(solution)/shard_map/all_to_all | solution.py:466
  80.4 2.9 %emit.1 = bf16[8,4,32,128]{3,2,1,0:T(8,128)(2,1)} custom-call(s32[3]{0:T(128)} %pad_add_fusion.core_ref.place_ref, bf16[8,128,256]{2,1,0:T(8,128)(2,1)S(1)} %all-to-all-done.1.maps_ref, f32[128,128]{1,0:T(8,128)} %bitcast.22, bf16[1024,128]{1,0:T(8,128)(2,1)} %get-tuple-element.39.slope_ref, f32[1024,128]{1,0:T(8,128)} %get-tuple-element.40.base_ref, ...), custom_call_target="tpu_custom_call" | custom-call | tf_op jit(solution)/shard_map/emit/pallas_call | solution.py:314
  83.4 4.8 %all-to-all-start.2 = ((bf16[8,4,32,128]{3,2,1,0:T(8,128)(2,1)}), bf16[8,4,32,128]{3,2,1,0:T(8,128)(2,1)S(1)}, u32[]{:S(2)}, u32[]{:S(2)}) async-start(bf16[8,4,32,128]{3,2,1,0:T(8,128)(2,1)} %emit.1), calls=%async_computation.2 | async-start | bytes 524288 | tf_op jit(solution)/shard_map/all_to_all | solution.py:466
  88.2 0.2 select_reduce_fusion
  88.3 0.1 copy.31
  88.4 0.0 collective-permute-done.5.refs_4_
  88.5 0.0 collective-permute-done.4.refs_3_
  88.5 5.8 %all-to-all-done.2 = bf16[8,4,32,128]{3,2,1,0:T(8,128)(2,1)S(1)} async-done(((bf16[8,4,32,128]{3,2,1,0:T(8,128)(2,1)}), bf16[8,4,32,128]{3,2,1,0:T(8,128)(2,1)S(1)}, u32[]{:S(2)}, u32[]{:S(2)}) %all-to-all-start.2) | async-done | bytes 262176 | tf_op jit(solution)/shard_map/all_to_all | solution.py:466
  94.3 3.4 %project.1 = bf16[4,32,2048]{2,1,0:T(8,128)(2,1)} custom-call(s32[3]{0:T(128)} %pad_add_fusion.core_ref.place_ref, bf16[8,128,128]{2,1,0:T(8,128)(2,1)S(1)} %bitcast.18, bf16[256,2048]{1,0:T(8,128)(2,1)} %copy-done.3, bf16[256,2048]{1,0:T(8,128)(2,1)} %collective-permute-done.1.refs_1_, bf16[128,2048]{1,0:T(8,128)(2,1)} %copy-done.5, ...), custom_call_target="tpu_custom_call" | custom-call | tf_op jit(solution)/shard_map/project/pallas_call | solution.py:344
  97.6 3.5 %all-to-all-start.3 = ((bf16[4,32,2048]{2,1,0:T(8,128)(2,1)}), bf16[4,32,2048]{2,1,0:T(8,128)(2,1)S(1)}, u32[]{:S(2)}, u32[]{:S(2)}) async-start(bf16[4,32,2048]{2,1,0:T(8,128)(2,1)} %project.1), calls=%async_computation.3 | async-start | bytes 1048576 | tf_op jit(solution)/shard_map/all_to_all | solution.py:466
  101.2 0.2 copy.35
  101.4 1.5 pad.9._
  103.0 7.5 %all-to-all-done.3.parts_ref = bf16[4,32,2048]{2,1,0:T(8,128)(2,1)S(1)} async-done(((bf16[4,32,2048]{2,1,0:T(8,128)(2,1)}), bf16[4,32,2048]{2,1,0:T(8,128)(2,1)S(1)}, u32[]{:S(2)}, u32[]{:S(2)}) %all-to-all-start.3) | async-done | bytes 524320 | tf_op jit(solution)/shard_map/all_to_all | solution.py:466
  110.5 3.3 %join.1 = (bf16[32,2048]{1,0:T(8,128)(2,1)}, bf16[16,32,2176]{2,1,0:T(8,128)(2,1)}) custom-call(bf16[4,32,2048]{2,1,0:T(8,128)(2,1)S(1)} %all-to-all-done.3.parts_ref, bf16[32,2048]{1,0:T(8,128)(2,1)} %tokens_ref.3, f32[1,2048]{1,0:T(1,128)} %bitcast.24, bf16[16,32,2176]{2,1,0:T(8,128)(2,1)} %pad.9._), custom_call_target="tpu_custom_call", output_to_operand_aliasing={{1}: (3, {})} | custom-call | tf_op jit(solution)/shard_map/join/pallas_call | solution.py:377
  113.7 0.1 collective-permute-start.6
  113.8 0.5 collective-permute-start.7
  114.3 34.0 %all_to_all.30.x_ref = bf16[16,32,2176]{2,1,0:T(8,128)(2,1)S(1)} all-to-all(bf16[16,32,2176]{2,1,0:T(8,128)(2,1)} %get-tuple-element.45), channel_id=1, replica_groups=mesh['ctx'=8,'x'=4,'y'=4,'core'=2] {'x','y'}, dimensions={0} | all-to-all | bytes 4456448 | tf_op jit(solution)/shard_map/all_to_all | solution.py:466
  148.3 0.0 collective-permute-done.7.down_b_ref
  148.3 0.0 collective-permute-done.6.up_b_ref
  148.3 6.7 %experts.1 = bf16[16,32,2048]{2,1,0:T(8,128)(2,1)S(1)} custom-call(bf16[16,32,2176]{2,1,0:T(8,128)(2,1)S(1)} %all_to_all.30.x_ref, bf16[1,2048,1024]{2,1,0:T(8,128)(2,1)S(1)} %copy-done, bf16[1,512,2048]{2,1,0:T(8,128)(2,1)S(1)} %copy-done.1, bf16[1,2048,1024]{2,1,0:T(8,128)(2,1)S(1)} %collective-permute-done.6.up_b_ref, ...), custom_call_target="tpu_custom_call" | custom-call | tf_op jit(solution)/shard_map/experts/pallas_call | solution.py:421
  155.1 31.3 %all_to_all.31.refs_0_ = bf16[16,32,2048]{2,1,0:T(8,128)(2,1)S(1)} all-to-all(bf16[16,32,2048]{2,1,0:T(8,128)(2,1)S(1)} %experts.1), channel_id=1, replica_groups=mesh['ctx'=8,'x'=4,'y'=4,'core'=2] {'x','y'}, dimensions={0} | all-to-all | bytes 4194304 | tf_op jit(solution)/shard_map/all_to_all | solution.py:466
  186.4 0.9 total.1
  (23 shorter events, 0.2 us)
Async XLA Ops:
  3.2 7.6 %copy-start.7 = (bf16[128,2048]{1,0:T(8,128)(2,1)S(1)}, bf16[128,2048]{1,0:T(8,128)(2,1)}, u32[]{:S(2)}) copy-start(bf16[128,2048]{1,0:T(8,128)(2,1)} %param.24) | copy-start | bytes 1572868
  3.2 7.7 %copy-start.8 = (bf16[2048,2]{0,1:T(2,128)(2,1)S(1)}, bf16[2048,2]{0,1:T(2,128)(2,1)}, u32[]{:S(2)}) copy-start(bf16[2048,2]{0,1:T(2,128)(2,1)} %param.18) | copy-start | bytes 24580
  3.2 36.6 %all-to-all-start = ((bf16[16,32,2048]{2,1,0:T(8,128)(2,1)}), bf16[16,32,2048]{2,1,0:T(8,128)(2,1)S(1)}, u32[]{:S(2)}, u32[]{:S(2)}) async-start(bf16[16,32,2048]{2,1,0:T(8,128)(2,1)} %norm_copies.1), calls=%async_computation | async-start | bytes 4194304 | tf_op jit(solution)/shard_map/all_to_all | solution.py:466
  10.7 4.5 %collective-permute-start = (bf16[128,2048]{1,0:T(8,128)(2,1)S(1)}, bf16[128,2048]{1,0:T(8,128)(2,1)}, u32[]{:S(2)}, u32[]{:S(2)}) collective-permute-start(bf16[128,2048]{1,0:T(8,128)(2,1)S(1)} %copy-done.7), channel_id=1, source_target_pairs={{0,1},{1,0},{2,3},{3,2},{4,5},{5,4},{6,7},{7,6},{8,9},{9,8},{10,11... | collective-permute-start | bytes 1572872 | tf_op jit(solution)/shard_map/ppermute | solution.py:462
  16.5 54.9 %copy-start.3 = (bf16[256,2048]{1,0:T(8,128)(2,1)}, bf16[256,2048]{1,0:T(8,128)(2,1)S(1)}, u32[]{:S(2)}) copy-start(bf16[256,2048]{1,0:T(8,128)(2,1)S(1)} %pad_maximum_fusion.refs_0_) | copy-start | bytes 3145732
  39.7 4.3 %copy-start.2 = (bf16[16,32,2048]{2,1,0:T(8,128)(2,1)}, bf16[16,32,2048]{2,1,0:T(8,128)(2,1)S(1)}, u32[]{:S(2)}) copy-start(bf16[16,32,2048]{2,1,0:T(8,128)(2,1)S(1)} %all-to-all-done.mine_ref) | copy-start | bytes 6291460
  39.7 4.3 %collective-permute-start.2 = (bf16[16,32,2048]{2,1,0:T(8,128)(2,1)S(1)}, bf16[16,32,2048]{2,1,0:T(8,128)(2,1)}, u32[]{:S(2)}, u32[]{:S(2)}) collective-permute-start(bf16[16,32,2048]{2,1,0:T(8,128)(2,1)S(1)} %all-to-all-done.mine_ref), channel_id=1, source_target_pairs={{0,1},{1,0},{2,3},{3,2},{4,5},{5,4},{6,7},{7,6},{8,9},{9,8},{10,11... | collective-permute-start | bytes 6291464 | tf_op jit(solution)/shard_map/ppermute | solution.py:462
  39.7 14.9 %collective-permute-start.1 = (bf16[256,2048]{1,0:T(8,128)(2,1)S(1)}, bf16[256,2048]{1,0:T(8,128)(2,1)}, u32[]{:S(2)}, u32[]{:S(2)}) collective-permute-start(bf16[256,2048]{1,0:T(8,128)(2,1)S(1)} %pad_maximum_fusion.refs_0_), channel_id=1, source_target_pairs={{0,2},{2,4},{4,6},{6,0},{1,7},{3,1},{5,3},{7,5},{8,10},{10,12},{12... | collective-permute-start | bytes 3145736 | tf_op jit(solution)/shard_map/ppermute | solution.py:454
  54.6 25.8 %all-to-all-start.1 = ((bf16[8,128,256]{2,1,0:T(8,128)(2,1)}), bf16[8,128,256]{2,1,0:T(8,128)(2,1)S(1)}, u32[]{:S(2)}, u32[]{:S(2)}) async-start(bf16[8,128,256]{2,1,0:T(8,128)(2,1)} %get-tuple-element.31), calls=%async_computation.1 | async-start | bytes 1048576 | tf_op jit(solution)/shard_map/all_to_all | solution.py:466
  65.0 10.0 %collective-permute-start.3 = (bf16[128,2048]{1,0:T(8,128)(2,1)}, bf16[128,2048]{1,0:T(8,128)(2,1)S(1)}, u32[]{:S(2)}, u32[]{:S(2)}) collective-permute-start(bf16[128,2048]{1,0:T(8,128)(2,1)} %slice.3), channel_id=1, source_target_pairs={{0,2},{2,4},{4,6},{6,0},{1,7},{3,1},{5,3},{7,5},{8,10},{10,12},{12... | collective-permute-start | bytes 1572872 | tf_op jit(solution)/shard_map/ppermute | solution.py:454
  65.0 23.4 %collective-permute-start.4 = (bf16[256,2048]{1,0:T(8,128)(2,1)}, bf16[256,2048]{1,0:T(8,128)(2,1)S(1)}, u32[]{:S(2)}, u32[]{:S(2)}) collective-permute-start(bf16[256,2048]{1,0:T(8,128)(2,1)} %collective-permute-done.1.refs_1_), channel_id=1, source_target_pairs={{0,1},{1,0},{2,3},{3,2},{4,5},{5,4},{6,7},{7,6},{8,9},{9,8},{10,11... | collective-permute-start | bytes 3145736 | tf_op jit(solution)/shard_map/ppermute | solution.py:462
  71.4 16.7 %copy-start.9 = (f32[32,10]{0,1:T(8,128)S(1)}, f32[32,10]{0,1:T(8,128)}, u32[]{:S(2)}) copy-start(f32[32,10]{0,1:T(8,128)} %param.27) | copy-start | bytes 3844
  71.4 16.7 %copy-start.10 = (s32[32,10]{0,1:T(8,128)S(1)}, s32[32,10]{0,1:T(8,128)}, u32[]{:S(2)}) copy-start(s32[32,10]{0,1:T(8,128)} %param.26) | copy-start | bytes 3844
  75.1 19.2 %copy-start.5 = (bf16[128,2048]{1,0:T(8,128)(2,1)}, bf16[128,2048]{1,0:T(8,128)(2,1)S(1)}, u32[]{:S(2)}) copy-start(bf16[128,2048]{1,0:T(8,128)(2,1)S(1)} %collective-permute-done.3.refs_2_) | copy-start | bytes 1572868
  75.1 13.4 %collective-permute-start.5 = (bf16[128,2048]{1,0:T(8,128)(2,1)S(1)}, bf16[128,2048]{1,0:T(8,128)(2,1)S(1)}, u32[]{:S(2)}, u32[]{:S(2)}) collective-permute-start(bf16[128,2048]{1,0:T(8,128)(2,1)S(1)} %collective-permute-done.3.refs_2_), channel_id=1, source_target_pairs={{0,1},{1,0},{2,3},{3,2},{4,5},{5,4},{6,7},{7,6},{8,9},{9,8},{10,11... | collective-permute-start | bytes 1572872 | tf_op jit(solution)/shard_map/ppermute | solution.py:462
  83.4 10.9 %all-to-all-start.2 = ((bf16[8,4,32,128]{3,2,1,0:T(8,128)(2,1)}), bf16[8,4,32,128]{3,2,1,0:T(8,128)(2,1)S(1)}, u32[]{:S(2)}, u32[]{:S(2)}) async-start(bf16[8,4,32,128]{3,2,1,0:T(8,128)(2,1)} %emit.1), calls=%async_computation.2 | async-start | bytes 524288 | tf_op jit(solution)/shard_map/all_to_all | solution.py:466
  88.4 5.8 %copy-start.6 = (bf16[128,2048]{1,0:T(8,128)(2,1)}, bf16[128,2048]{1,0:T(8,128)(2,1)S(1)}, u32[]{:S(2)}) copy-start(bf16[128,2048]{1,0:T(8,128)(2,1)S(1)} %collective-permute-done.5.refs_4_) | copy-start | bytes 1572868
  88.5 5.8 %copy-start.4 = (bf16[256,2048]{1,0:T(8,128)(2,1)}, bf16[256,2048]{1,0:T(8,128)(2,1)S(1)}, u32[]{:S(2)}) copy-start(bf16[256,2048]{1,0:T(8,128)(2,1)S(1)} %collective-permute-done.4.refs_3_) | copy-start | bytes 3145732
  97.6 12.8 %all-to-all-start.3 = ((bf16[4,32,2048]{2,1,0:T(8,128)(2,1)}), bf16[4,32,2048]{2,1,0:T(8,128)(2,1)S(1)}, u32[]{:S(2)}, u32[]{:S(2)}) async-start(bf16[4,32,2048]{2,1,0:T(8,128)(2,1)} %project.1), calls=%async_computation.3 | async-start | bytes 1048576 | tf_op jit(solution)/shard_map/all_to_all | solution.py:466
  101.4 12.4 %copy-start.1 = (bf16[1,512,2048]{2,1,0:T(8,128)(2,1)S(1)}, bf16[1,512,2048]{2,1,0:T(8,128)(2,1)}, u32[]{:S(2)}) copy-start(bf16[1,512,2048]{2,1,0:T(8,128)(2,1)} %down_a_ref.1) | copy-start | bytes 6291460
  113.7 34.6 %collective-permute-start.6 = (bf16[1,2048,1024]{2,1,0:T(8,128)(2,1)}, bf16[1,2048,1024]{2,1,0:T(8,128)(2,1)S(1)}, u32[]{:S(2)}, u32[]{:S(2)}) collective-permute-start(bf16[1,2048,1024]{2,1,0:T(8,128)(2,1)} %up_a_ref.1), channel_id=1, source_target_pairs={{0,1},{1,0},{2,3},{3,2},{4,5},{5,4},{6,7},{7,6},{8,9},{9,8},{10,11... | collective-permute-start | bytes 12582920 | tf_op jit(solution)/shard_map/ppermute | solution.py:462
  113.8 34.5 %collective-permute-start.7 = (bf16[1,512,2048]{2,1,0:T(8,128)(2,1)S(1)}, bf16[1,512,2048]{2,1,0:T(8,128)(2,1)S(1)}, u32[]{:S(2)}, u32[]{:S(2)}) collective-permute-start(bf16[1,512,2048]{2,1,0:T(8,128)(2,1)S(1)} %copy-done.1), channel_id=1, source_target_pairs={{0,1},{1,0},{2,3},{3,2},{4,5},{5,4},{6,7},{7,6},{8,9},{9,8},{10,11... | collective-permute-start | bytes 6291464 | tf_op jit(solution)/shard_map/ppermute | solution.py:462
  114.3 34.0 %copy-start = (bf16[1,2048,1024]{2,1,0:T(8,128)(2,1)S(1)}, bf16[1,2048,1024]{2,1,0:T(8,128)(2,1)}, u32[]{:S(2)}) copy-start(bf16[1,2048,1024]{2,1,0:T(8,128)(2,1)} %up_a_ref.1) | copy-start | bytes 12582916

commit v6 on v5

--- a/solution.py
+++ b/solution.py
@@ -274,7 +274,18 @@
     )(tokens, gain[None])
 
 
-def emit_body(place_ref, maps_ref, init_ref, slope_ref, base_ref, gate_ref, out_ref):
+def emit_body(
+    place_ref, maps_ref, init_ref, slope_ref, base_ref, gate_ref, out_ref,
+    slope_buf, base_buf, gate_buf, sems,
+):
+    moves = [
+        pltpu.make_async_copy(source, target, sems.at[at])
+        for at, (source, target) in enumerate(
+            ((slope_ref, slope_buf), (base_ref, base_buf), (gate_ref, gate_buf))
+        )
+    ]
+    for move in moves:
+        move.start()
     dim = init_ref.shape[0]
     place = place_ref[2]
     rows = lax.broadcasted_iota(jnp.int32, (dim, 2 * dim), 0)
@@ -300,11 +311,13 @@
         if steps and not odd:
             state = mm(steps[0][:, :dim], state) + steps[0][:, dim:]
             steps = steps[1:]
+    for move in moves:
+        move.wait()
     inner, outer, each, _ = out_ref.shape
     for part in range(outer):
         at = slice(part * inner * each, (part + 1) * inner * each)
-        head_raw = mm(slope_ref[at, :], state) + base_ref[at, :]
-        gated = head_raw * rms_scale(head_raw) * gate_ref[at, :]
+        head_raw = mm(slope_buf[at, :], state) + base_buf[at, :]
+        gated = head_raw * rms_scale(head_raw) * gate_buf[at, :]
         out_ref[:, part] = gated.astype(BF16).reshape(inner, each, dim)
 
 
@@ -313,42 +326,72 @@
     each = span // (outer * inner)
     return pl.pallas_call(
         emit_body,
-        in_specs=[pl.BlockSpec(memory_space=pltpu.SMEM)] + [resident()] * 5,
+        in_specs=[pl.BlockSpec(memory_space=pltpu.SMEM)]
+        + [resident()] * 2
+        + [pl.BlockSpec(memory_space=pl.ANY)] * 3,
         out_specs=resident(),
         out_shape=jax.ShapeDtypeStruct((inner, outer, each, dim), BF16),
+        scratch_shapes=[
+            pltpu.VMEM(slope.shape, slope.dtype),
+            pltpu.VMEM(base.shape, base.dtype),
+            pltpu.VMEM(gate.shape, gate.dtype),
+            pltpu.SemaphoreType.DMA((3,)),
+        ],
         name="emit",
     )(place, near(maps), init, slope, base, gate)
 
 
-def project_body(place_ref, gated_ref, *refs):
-    *w_refs, out_ref = refs
+def project_body(place_ref, gated_ref, *refs, tiles):
+    *w_refs, out_ref, w_buf, sems = refs
+    heads, rows, dim = gated_ref.shape
+    width = out_ref.shape[-1]
+    tile = width // tiles
+    moves = []
+    for part in range(tiles):
+        cols = pl.ds(part * tile, tile)
+        moves.append(
+            [
+                pltpu.make_async_copy(
+                    w_ref.at[:, cols],
+                    w_buf.at[pl.ds(at * dim, dim), cols],
+                    sems.at[part * heads + at],
+                )
+                for at, w_ref in enumerate(w_refs)
+            ]
+        )
+    for move in [move for group in moves for move in group]:
+        move.start()
     core = place_ref[0]
     row = place_ref[1]
-    count = gated_ref.shape[0] // 2
+    count = heads // 2
     step = 2 * core - 1 + count
-    rows = [row, row, row + step, row + step, row + 2, row + count - step + count,
-            row + count - step + count, row + 2]
-    cores = [core, 1 - core, core, 1 - core, core, 1 - core, core, 1 - core]
-    left = [gated_ref[2 * lax.rem(at, count) + side] for at, side in zip(rows, cores)]
-    total = jnp.dot(
-        jnp.concatenate(left, axis=1),
-        jnp.concatenate([ref[...] for ref in w_refs], axis=0),
-        preferred_element_type=F32,
+    back = row + 2 * count - step
+    spots = [row, row, row + step, row + step, row + 2, back, back, row + 2]
+    sides = [core, 1 - core, core, 1 - core, core, 1 - core, core, 1 - core]
+    left = jnp.concatenate(
+        [gated_ref[2 * lax.rem(at, count) + side] for at, side in zip(spots, sides)], axis=1
     )
-    out_ref[...] = total.astype(BF16).reshape(out_ref.shape)
-
-
-def project(place, gated, weights, parts, tile):
+    for part in range(tiles):
+        for move in moves[part]:
+            move.wait()
+        cols = slice(part * tile, (part + 1) * tile)
+        total = jnp.dot(left, w_buf[:, cols], preferred_element_type=F32)
+        out_ref[:, :, cols] = total.astype(BF16).reshape(out_ref.shape[:2] + (tile,))
+
+
+def project(place, gated, weights, parts, tiles):
     heads, rows, dim = gated.shape
     width = weights[0].shape[1]
     return pl.pallas_call(
-        project_body,
-        grid=(width // tile,),
-        in_specs=[pl.BlockSpec(memory_space=pltpu.SMEM), resident()] + [
-            pl.BlockSpec((rows.shape[0], tile), lambda i: (0, i)) for rows in weights
-        ],
-        out_specs=pl.BlockSpec((parts, rows // parts, tile), lambda i: (0, 0, i)),
+        functools.partial(project_body, tiles=tiles),
+        in_specs=[pl.BlockSpec(memory_space=pltpu.SMEM), resident()]
+        + [pl.BlockSpec(memory_space=pl.ANY)] * heads,
+        out_specs=resident(),
         out_shape=jax.ShapeDtypeStruct((parts, rows // parts, width), BF16),
+        scratch_shapes=[
+            pltpu.VMEM((heads * dim, width), BF16),
+            pltpu.SemaphoreType.DMA((tiles * heads,)),
+        ],
         name="project",
     )(place, near(gated), *weights)
 
@@ -388,7 +431,7 @@
             pltpu.SemaphoreType.DMA((payload.shape[0],)),
         ],
         name="join",
-    )(near(parts), tokens, gain[None], payload)
+    )(near(parts), near(tokens), gain[None], payload)
 
 
 def experts_body(x_ref, up_a_ref, down_a_ref, up_b_ref, down_b_ref, out_ref, *, tiles):
@@ -494,30 +537,10 @@
 
     copies = norm_copies(tokens, gain_in, chips)
     mine = exchange(copies, ("x", "y"))
-    pair = jnp.concatenate([w_output, swap_cores(w_output)], axis=0)
+    w_pair = (w_output, swap_cores(w_output))
     scalars = jnp.concatenate([strength_bias, decay_rate, decay_bias])
     w_logit = jnp.pad(w_scalar, ((0, 0), (0, LANES - w_scalar.shape[1])))
     spots = jnp.stack([core, lax.axis_index("y").astype(jnp.int32), place])
-    mine, pair, scalars, w_logit, spots = lax.optimization_barrier(
-        (mine, pair, scalars, w_logit, spots)
-    )
-    theirs = swap_cores(mine)
-    beside = send_y(pair)
-
-    *parts, maps = block_maps(spots, scalars, mine, theirs, w_heads, w_logit, dim, ctx_count, 4)
-    beside, maps = lax.optimization_barrier((beside, maps))
-    across = send_y(beside[:dim])
-    all_maps = exchange(maps, "ctx")
-    slope, base, gate = block_reads(spots, mine, theirs, w_heads, gain_head, parts, dim, PER_STEP)
-    across, slope = lax.optimization_barrier((across, slope))
-    w_rows = [pair, beside, across, swap_cores(beside), swap_cores(across)]
-    gated = emit(
-        spots, all_maps, state_init[0], slope, base, gate, x_count, y_count * core_count
-    )
-    heads = y_count * core_count
-    gated = exchange(gated, ("y", "core")).reshape(heads, x_count * tok_dev, dim)
-    partial = project(spots, gated, w_rows, x_count, 1024)
-
     numbers = jnp.arange(expert_total, dtype=jnp.int32)
     named = expert_ids[:, :, None] == numbers[None, None, :]
     routes = jnp.sum(jnp.where(named, gate_weights[:, :, None], 0.0), axis=1)
@@ -525,6 +548,26 @@
     routes = jnp.where(core == 0, routes, routes[:, :, ::-1])
     routes = jnp.stack(pieces(routes), axis=-1).reshape(chips, tok_dev, -1)
     payload = jnp.pad(routes, ((0, 0), (0, 0), (width, LANES - routes.shape[-1])))
+
+    mine, w_pair, scalars, w_logit, spots, payload = lax.optimization_barrier(
+        (mine, w_pair, scalars, w_logit, spots, payload)
+    )
+    theirs = swap_cores(mine)
+    beside = tuple(send_y(rows) for rows in w_pair)
+
+    *parts, maps = block_maps(spots, scalars, mine, theirs, w_heads, w_logit, dim, ctx_count, 4)
+    beside, maps = lax.optimization_barrier((beside, maps))
+    across = send_y(beside[0])
+    all_maps = exchange(maps, "ctx")
+    slope, base, gate = block_reads(spots, mine, theirs, w_heads, gain_head, parts, dim, PER_STEP)
+    across, slope = lax.optimization_barrier((across, slope))
+    w_rows = [*w_pair, *beside, across, *[swap_cores(rows) for rows in (*beside, across)]]
+    gated = emit(
+        spots, all_maps, state_init[0], slope, base, gate, x_count, y_count * core_count
+    )
+    heads = y_count * core_count
+    gated = exchange(gated, ("y", "core")).reshape(heads, x_count * tok_dev, dim)
+    partial = project(spots, gated, w_rows, x_count, 4)
 
     summed, copies = join(exchange(partial, "x"), tokens, gain_expert, payload)
     far_gate_up, far_down, summed = lax.optimization_barrier((w_gate_up, w_down, summed))

time: 188 us -> 190 us (1.011)
  blocking collectives: 65.3 us -> 78.2 us
  waiting for transfers between devices: 50.6 us -> 43.3 us
  starting transfers between devices: 25.5 us -> 22.9 us
    all_to_all x2 -> x3, blocking collectives: 65.3 us -> 78.2 us  [exchange(): return lax.all_to_all(value, axes, split_axis=0, concat_axis=0, tiled=True)]
    all_to_all x4 -> x3, waiting for transfers between devices: 41.9 us -> 35.8 us  [exchange(): return lax.all_to_all(value, axes, split_axis=0, concat_axis=0, tiled=True)]
    all_to_all x4 -> x3, starting transfers between devices: 24.2 us -> 20.8 us  [exchange(): return lax.all_to_all(value, axes, split_axis=0, concat_axis=0, tiled=True)]
    slice x1 -> x0, local copies, waits for them, and re-layouts: 1.91 us -> none  [shards(): across = send_y(beside[:dim])]
    ppermute x6 -> x7, waiting for transfers between devices: 4.3 us -> 3.46 us  [swap_cores(): return lax.ppermute(value, 'core', [(0, 1), (1, 0)])]
    ppermute x2 -> x3, waiting for transfers between devices: 4.42 us -> 4.02 us  [send_y(): return lax.ppermute(value, ('y', 'core'), up + down)]
  transfers between devices with their start and end apart: 12 -> 13, of which waited for: 7 -> 6; matrix products, arithmetic and copies ran while one was open for 4% -> 2% of each run, Pallas kernels for 10% -> 10%
where the time goes in v6:
time: 190 us; the launch traced here: 189 us
  blocking collectives  78.2 us (41%)
  waiting for transfers between devices  43.3 us (23%)
  Pallas kernels  37 us (19%)
  starting transfers between devices  22.9 us (12%)
  local copies, waits for them, and re-layouts  3.21 us (2%)
  between operations  2.87 us (2%)
    all_to_all x3, blocking collectives, exchange(): return lax.all_to_all(value, axes, split_axis=0, concat_axis=0, tiled=True)  78.2 us
    all_to_all x3, waiting for transfers between devices, exchange(): return lax.all_to_all(value, axes, split_axis=0, concat_axis=0, tiled=True)  35.8 us
    all_to_all x3, starting transfers between devices, exchange(): return lax.all_to_all(value, axes, split_axis=0, concat_axis=0, tiled=True)  20.8 us
    pallas_call x1, Pallas kernels, block_maps(): pl.pallas_call(functools.partial(maps_body, parts=parts), in_specs=[scala...  9.84 us
    pallas_call x1, Pallas kernels, experts_of(): pl.pallas_call(functools.partial(experts_body, tiles=tiles), in_specs=[re...  6.73 us
    pallas_call x1, Pallas kernels, block_reads(): pl.pallas_call(functools.partial(reads_body, per_step=per_step), grid=(sp...  5.94 us
    pallas_call x1, Pallas kernels, project(): pl.pallas_call(functools.partial(project_body, tiles=tiles), in_specs=[pl...  4.45 us
    ppermute x3, waiting for transfers between devices, send_y(): return lax.ppermute(value, ('y', 'core'), up + down)  4.02 us
  transfers between devices with their start and end apart: 13, of which 6 were waited for; matrix products, arithmetic and copies ran while one was open for 2% of the time, Pallas kernels for 10%

profile of v6, /device:TPU:8, one launch (start us, length us, event | category | flops | bytes accessed | tf_op | source)
XLA Modules:
  0.0 189.0 jit_solution(10513293527436602447)
XLA Ops:
  0.6 2.5 %norm_copies.1 = bf16[16,32,2048]{2,1,0:T(8,128)(2,1)} custom-call(bf16[32,2048]{1,0:T(8,128)(2,1)} %tokens_ref.3, f32[1,2048]{1,0:T(1,128)} %bitcast.23), custom_call_target="tpu_custom_call" | custom-call | tf_op jit(solution)/shard_map/norm_copies/pallas_call | solution.py:268
  3.1 0.0 copy-start.4
  3.2 0.0 copy-start.11
  3.2 0.0 copy-start.12
  3.2 0.0 copy-start.10
  3.2 7.5 %all-to-all-start = ((bf16[16,32,2048]{2,1,0:T(8,128)(2,1)}), bf16[16,32,2048]{2,1,0:T(8,128)(2,1)S(1)}, u32[]{:S(2)}, u32[]{:S(2)}) async-start(bf16[16,32,2048]{2,1,0:T(8,128)(2,1)} %norm_copies.1), calls=%async_computation | async-start | bytes 4194304 | tf_op jit(solution)/shard_map/all_to_all | solution.py:509
  10.7 0.1 collective-permute-start
  10.9 0.2 select_reduce_fusion
  11.0 0.1 copy.31
  11.3 0.2 copy.35
  11.5 0.3 copy.30
  11.8 1.6 pad.9._
  13.3 0.9 pad.8.ws_ref
  16.2 0.6 pad_add_fusion.core_ref.place_ref
  16.9 0.6 pad_maximum_fusion.1.scal_ref
  17.4 0.0 collective-permute-done.refs_1_
  17.4 22.3 %all-to-all-done.mine_ref = bf16[16,32,2048]{2,1,0:T(8,128)(2,1)S(1)} async-done(((bf16[16,32,2048]{2,1,0:T(8,128)(2,1)}), bf16[16,32,2048]{2,1,0:T(8,128)(2,1)S(1)}, u32[]{:S(2)}, u32[]{:S(2)}) %all-to-all-start) | async-done | bytes 2097184 | tf_op jit(solution)/shard_map/all_to_all | solution.py:509
  39.7 0.0 collective-permute-start.3
  39.7 0.0 collective-permute-start.1
  39.8 0.8 collective-permute-start.2
  40.6 3.4 %collective-permute-done.3.theirs_ref = bf16[16,32,2048]{2,1,0:T(8,128)(2,1)} collective-permute-done((bf16[16,32,2048]{2,1,0:T(8,128)(2,1)S(1)}, bf16[16,32,2048]{2,1,0:T(8,128)(2,1)}, u32[]{:S(2)}, u32[]{:S(2)}) %collective-permute-start.3) | collective-permute-done | bytes 2097184 | tf_op jit(solution)/shard_map/ppermute | solution.py:505
  44.0 9.8 %block_maps.1 = (bf16[8,128,128]{2,1,0:T(8,128)(2,1)}, f32[8,128,128]{2,1,0:T(8,128)}, f32[8,128,128]{2,1,0:T(8,128)}, bf16[8,128,256]{2,1,0:T(8,128)(2,1)}, bf1...) custom-call(s32[3]{0:T(128)} %pad_add_fusion.core_ref.place_ref, f32[3]{0:T(128)} %pad_maximum_fusion.1.scal_ref, ...), custom_call_target="tpu_custom_call" | custom-call | tf_op jit(solution)/shard_map/block_maps/pallas_call | solution.py:172
  53.9 0.0 collective-permute-done.1.refs_2_
  53.9 0.7 collective-permute-done.2.refs_3_
  54.7 8.5 %all-to-all-start.1 = ((bf16[8,128,256]{2,1,0:T(8,128)(2,1)}), bf16[8,128,256]{2,1,0:T(8,128)(2,1)S(1)}, u32[]{:S(2)}, u32[]{:S(2)}) async-start(bf16[8,128,256]{2,1,0:T(8,128)(2,1)} %get-tuple-element.35), calls=%async_computation.1 | async-start | bytes 1048576 | tf_op jit(solution)/shard_map/all_to_all | solution.py:509
  63.1 0.0 collective-permute-start.4
  63.1 0.5 collective-permute-start.5
  63.7 0.1 collective-permute-start.6
  63.7 5.9 %block_reads.1 = (bf16[1024,128]{1,0:T(8,128)(2,1)}, f32[1024,128]{1,0:T(8,128)}, f32[1024,128]{1,0:T(8,128)}) custom-call(s32[3]{0:T(128)} %pad_add_fusion.core_ref.place_ref, bf16[16,32,2048]{2,1,0:T(8,128)(2,1)} %copy-done.3, bf16[16,32,2048]{2,1,0:T(8,128)(2,1)} %collective-permute-done.3.theirs_ref, bf16[2048,512]{1,0:T(8,128)(2,1)} %wg_ref.1, ...), custom_call_target="tpu_custom_call" | custom-call | tf_op jit(solution)/shard_map/block_reads/pallas_call | solution.py:227
  69.7 3.3 %collective-permute-done.4.refs_4_ = bf16[128,2048]{1,0:T(8,128)(2,1)S(1)} collective-permute-done((bf16[128,2048]{1,0:T(8,128)(2,1)S(1)}, bf16[128,2048]{1,0:T(8,128)(2,1)S(1)}, u32[]{:S(2)}, u32[]{:S(2)}) %collective-permute-start.4) | collective-permute-done | bytes 524320 | tf_op jit(solution)/shard_map/ppermute | solution.py:497
  73.0 7.5 %all-to-all-done.1.maps_ref = bf16[8,128,256]{2,1,0:T(8,128)(2,1)S(1)} async-done(((bf16[8,128,256]{2,1,0:T(8,128)(2,1)}), bf16[8,128,256]{2,1,0:T(8,128)(2,1)S(1)}, u32[]{:S(2)}, u32[]{:S(2)}) %all-to-all-start.1) | async-done | bytes 524320 | tf_op jit(solution)/shard_map/all_to_all | solution.py:509
  80.4 3.6 %emit.1 = bf16[8,4,32,128]{3,2,1,0:T(8,128)(2,1)} custom-call(s32[3]{0:T(128)} %pad_add_fusion.core_ref.place_ref, bf16[8,128,256]{2,1,0:T(8,128)(2,1)S(1)} %all-to-all-done.1.maps_ref, f32[128,128]{1,0:T(8,128)} %bitcast.22, bf16[1024,128]{1,0:T(8,128)(2,1)} %get-tuple-element.43.slope_ref, f32[1024,128]{1,0:T(8,128)} %get-tuple-element.44.base_ref, ...), custom_call_target="tpu_custom_call" | custom-call | tf_op jit(solution)/shard_map/emit/pallas_call | solution.py:327
  84.0 4.8 %all-to-all-start.2 = ((bf16[8,4,32,128]{3,2,1,0:T(8,128)(2,1)}), bf16[8,4,32,128]{3,2,1,0:T(8,128)(2,1)S(1)}, u32[]{:S(2)}, u32[]{:S(2)}) async-start(bf16[8,4,32,128]{3,2,1,0:T(8,128)(2,1)} %emit.1), calls=%async_computation.2 | async-start | bytes 524288 | tf_op jit(solution)/shard_map/all_to_all | solution.py:509
  88.8 0.0 collective-permute-done.5.refs_5_
  88.8 0.0 collective-permute-done.7.refs_7_
  88.9 6.1 %all-to-all-done.2 = bf16[8,4,32,128]{3,2,1,0:T(8,128)(2,1)S(1)} async-done(((bf16[8,4,32,128]{3,2,1,0:T(8,128)(2,1)}), bf16[8,4,32,128]{3,2,1,0:T(8,128)(2,1)S(1)}, u32[]{:S(2)}, u32[]{:S(2)}) %all-to-all-start.2) | async-done | bytes 262176 | tf_op jit(solution)/shard_map/all_to_all | solution.py:509
  94.9 0.0 copy-start.2
  94.9 4.4 %project.1 = bf16[4,32,2048]{2,1,0:T(8,128)(2,1)} custom-call(s32[3]{0:T(128)} %pad_add_fusion.core_ref.place_ref, bf16[8,128,128]{2,1,0:T(8,128)(2,1)S(1)} %bitcast.18, bf16[128,2048]{1,0:T(8,128)(2,1)} %refs_0_, bf16[128,2048]{1,0:T(8,128)(2,1)} %collective-permute-done.refs_1_, bf16[128,2048]{1,0:T(8,128)(2,1)} %copy-done.5, ...), custom_call_target="tpu_custom_call" | custom-call | tf_op jit(solution)/shard_map/project/pallas_call | solution.py:385
  99.4 0.0 copy-start.1
  99.4 13.0 %all_to_all.30.parts_ref = bf16[4,32,2048]{2,1,0:T(8,128)(2,1)S(1)} all-to-all(bf16[4,32,2048]{2,1,0:T(8,128)(2,1)} %project.1), channel_id=1, replica_groups=mesh['ctx'=8,'x'=4,'y'=4,'core'=2] {'x'}, dimensions={0} | all-to-all | bytes 1048576 | tf_op jit(solution)/shard_map/all_to_all | solution.py:509
  112.4 3.1 %join.1 = (bf16[32,2048]{1,0:T(8,128)(2,1)}, bf16[16,32,2176]{2,1,0:T(8,128)(2,1)}) custom-call(bf16[4,32,2048]{2,1,0:T(8,128)(2,1)S(1)} %all_to_all.30.parts_ref, bf16[32,2048]{1,0:T(8,128)(2,1)S(1)} %copy-done.2, f32[1,2048]{1,0:T(1,128)} %bitcast.24, bf16[16,32,2176]{2,1,0:T(8,128)(2,1)} %pad.9._), custom_call_target="tpu_custom_call", output_to_operand_aliasing={{1}: (3, {})} | custom-call | tf_op jit(solution)/shard_map/join/pallas_call | solution.py:420
  115.5 0.1 collective-permute-start.8
  115.6 0.5 collective-permute-start.9
  116.1 34.0 %all_to_all.31.x_ref = bf16[16,32,2176]{2,1,0:T(8,128)(2,1)S(1)} all-to-all(bf16[16,32,2176]{2,1,0:T(8,128)(2,1)} %get-tuple-element.51), channel_id=1, replica_groups=mesh['ctx'=8,'x'=4,'y'=4,'core'=2] {'x','y'}, dimensions={0} | all-to-all | bytes 4456448 | tf_op jit(solution)/shard_map/all_to_all | solution.py:509
  150.0 0.0 collective-permute-done.9.down_b_ref
  150.1 6.7 %experts.1 = bf16[16,32,2048]{2,1,0:T(8,128)(2,1)S(1)} custom-call(bf16[16,32,2176]{2,1,0:T(8,128)(2,1)S(1)} %all_to_all.31.x_ref, bf16[1,2048,1024]{2,1,0:T(8,128)(2,1)S(1)} %copy-done, bf16[1,512,2048]{2,1,0:T(8,128)(2,1)S(1)} %copy-done.1, bf16[1,2048,1024]{2,1,0:T(8,128)(2,1)S(1)} %collective-permute-done.8.up_b_ref, ...), custom_call_target="tpu_custom_call" | custom-call | tf_op jit(solution)/shard_map/experts/pallas_call | solution.py:464
  156.8 31.3 %all_to_all.32.refs_0_ = bf16[16,32,2048]{2,1,0:T(8,128)(2,1)S(1)} all-to-all(bf16[16,32,2048]{2,1,0:T(8,128)(2,1)S(1)} %experts.1), channel_id=1, replica_groups=mesh['ctx'=8,'x'=4,'y'=4,'core'=2] {'x','y'}, dimensions={0} | all-to-all | bytes 4194304 | tf_op jit(solution)/shard_map/all_to_all | solution.py:509
  188.1 0.9 total.1
  (28 shorter events, 0.2 us)
Async XLA Ops:
  3.1 7.6 %copy-start.4 = (bf16[128,2048]{1,0:T(8,128)(2,1)S(1)}, bf16[128,2048]{1,0:T(8,128)(2,1)}, u32[]{:S(2)}) copy-start(bf16[128,2048]{1,0:T(8,128)(2,1)} %refs_0_) | copy-start | bytes 1572868
  3.2 7.7 %copy-start.11 = (f32[32,10]{0,1:T(8,128)S(1)}, f32[32,10]{0,1:T(8,128)}, u32[]{:S(2)}) copy-start(f32[32,10]{0,1:T(8,128)} %param.27) | copy-start | bytes 3844
  3.2 7.7 %copy-start.12 = (s32[32,10]{0,1:T(8,128)S(1)}, s32[32,10]{0,1:T(8,128)}, u32[]{:S(2)}) copy-start(s32[32,10]{0,1:T(8,128)} %param.26) | copy-start | bytes 3844
  3.2 8.3 %copy-start.10 = (bf16[2048,2]{0,1:T(2,128)(2,1)S(1)}, bf16[2048,2]{0,1:T(2,128)(2,1)}, u32[]{:S(2)}) copy-start(bf16[2048,2]{0,1:T(2,128)(2,1)} %param.18) | copy-start | bytes 24580
  3.2 36.6 %all-to-all-start = ((bf16[16,32,2048]{2,1,0:T(8,128)(2,1)}), bf16[16,32,2048]{2,1,0:T(8,128)(2,1)S(1)}, u32[]{:S(2)}, u32[]{:S(2)}) async-start(bf16[16,32,2048]{2,1,0:T(8,128)(2,1)} %norm_copies.1), calls=%async_computation | async-start | bytes 4194304 | tf_op jit(solution)/shard_map/all_to_all | solution.py:509
  10.7 6.7 %collective-permute-start = (bf16[128,2048]{1,0:T(8,128)(2,1)S(1)}, bf16[128,2048]{1,0:T(8,128)(2,1)}, u32[]{:S(2)}, u32[]{:S(2)}) collective-permute-start(bf16[128,2048]{1,0:T(8,128)(2,1)S(1)} %copy-done.4), channel_id=1, source_target_pairs={{0,1},{1,0},{2,3},{3,2},{4,5},{5,4},{6,7},{7,6},{8,9},{9,8},{10,11... | collective-permute-start | bytes 1572872 | tf_op jit(solution)/shard_map/ppermute | solution.py:505
  39.7 4.3 %copy-start.3 = (bf16[16,32,2048]{2,1,0:T(8,128)(2,1)}, bf16[16,32,2048]{2,1,0:T(8,128)(2,1)S(1)}, u32[]{:S(2)}) copy-start(bf16[16,32,2048]{2,1,0:T(8,128)(2,1)S(1)} %all-to-all-done.mine_ref) | copy-start | bytes 6291460
  39.7 4.3 %collective-permute-start.3 = (bf16[16,32,2048]{2,1,0:T(8,128)(2,1)S(1)}, bf16[16,32,2048]{2,1,0:T(8,128)(2,1)}, u32[]{:S(2)}, u32[]{:S(2)}) collective-permute-start(bf16[16,32,2048]{2,1,0:T(8,128)(2,1)S(1)} %all-to-all-done.mine_ref), channel_id=1, source_target_pairs={{0,1},{1,0},{2,3},{3,2},{4,5},{5,4},{6,7},{7,6},{8,9},{9,8},{10,11... | collective-permute-start | bytes 6291464 | tf_op jit(solution)/shard_map/ppermute | solution.py:505
  39.7 14.1 %collective-permute-start.1 = (bf16[128,2048]{1,0:T(8,128)(2,1)S(1)}, bf16[128,2048]{1,0:T(8,128)(2,1)S(1)}, u32[]{:S(2)}, u32[]{:S(2)}) collective-permute-start(bf16[128,2048]{1,0:T(8,128)(2,1)S(1)} %copy-done.4), channel_id=1, source_target_pairs={{0,2},{2,4},{4,6},{6,0},{1,7},{3,1},{5,3},{7,5},{8,10},{10,12},{12... | collective-permute-start | bytes 1572872 | tf_op jit(solution)/shard_map/ppermute | solution.py:497
  39.8 14.9 %collective-permute-start.2 = (bf16[128,2048]{1,0:T(8,128)(2,1)}, bf16[128,2048]{1,0:T(8,128)(2,1)}, u32[]{:S(2)}, u32[]{:S(2)}) collective-permute-start(bf16[128,2048]{1,0:T(8,128)(2,1)} %collective-permute-done.refs_1_), channel_id=1, source_target_pairs={{0,2},{2,4},{4,6},{6,0},{1,7},{3,1},{5,3},{7,5},{8,10},{10,12},{12... | collective-permute-start | bytes 1572872 | tf_op jit(solution)/shard_map/ppermute | solution.py:497
  53.9 15.8 %copy-start.5 = (bf16[128,2048]{1,0:T(8,128)(2,1)}, bf16[128,2048]{1,0:T(8,128)(2,1)S(1)}, u32[]{:S(2)}) copy-start(bf16[128,2048]{1,0:T(8,128)(2,1)S(1)} %collective-permute-done.1.refs_2_) | copy-start | bytes 1572868
  54.7 25.8 %all-to-all-start.1 = ((bf16[8,128,256]{2,1,0:T(8,128)(2,1)}), bf16[8,128,256]{2,1,0:T(8,128)(2,1)S(1)}, u32[]{:S(2)}, u32[]{:S(2)}) async-start(bf16[8,128,256]{2,1,0:T(8,128)(2,1)} %get-tuple-element.35), calls=%async_computation.1 | async-start | bytes 1048576 | tf_op jit(solution)/shard_map/all_to_all | solution.py:509
  63.1 9.8 %collective-permute-start.4 = (bf16[128,2048]{1,0:T(8,128)(2,1)S(1)}, bf16[128,2048]{1,0:T(8,128)(2,1)S(1)}, u32[]{:S(2)}, u32[]{:S(2)}) collective-permute-start(bf16[128,2048]{1,0:T(8,128)(2,1)S(1)} %collective-permute-done.1.refs_2_), channel_id=1, source_target_pairs={{0,2},{2,4},{4,6},{6,0},{1,7},{3,1},{5,3},{7,5},{8,10},{10,12},{12... | collective-permute-start | bytes 1572872 | tf_op jit(solution)/shard_map/ppermute | solution.py:497
  63.1 25.7 %collective-permute-start.5 = (bf16[128,2048]{1,0:T(8,128)(2,1)S(1)}, bf16[128,2048]{1,0:T(8,128)(2,1)S(1)}, u32[]{:S(2)}, u32[]{:S(2)}) collective-permute-start(bf16[128,2048]{1,0:T(8,128)(2,1)S(1)} %collective-permute-done.1.refs_2_), channel_id=1, source_target_pairs={{0,1},{1,0},{2,3},{3,2},{4,5},{5,4},{6,7},{7,6},{8,9},{9,8},{10,11... | collective-permute-start | bytes 1572872 | tf_op jit(solution)/shard_map/ppermute | solution.py:505
  63.7 25.1 %collective-permute-start.6 = (bf16[128,2048]{1,0:T(8,128)(2,1)}, bf16[128,2048]{1,0:T(8,128)(2,1)S(1)}, u32[]{:S(2)}, u32[]{:S(2)}) collective-permute-start(bf16[128,2048]{1,0:T(8,128)(2,1)} %collective-permute-done.2.refs_3_), channel_id=1, source_target_pairs={{0,1},{1,0},{2,3},{3,2},{4,5},{5,4},{6,7},{7,6},{8,9},{9,8},{10,11... | collective-permute-start | bytes 1572872 | tf_op jit(solution)/shard_map/ppermute | solution.py:505
  73.0 22.0 %copy-start.6 = (bf16[128,2048]{1,0:T(8,128)(2,1)}, bf16[128,2048]{1,0:T(8,128)(2,1)S(1)}, u32[]{:S(2)}) copy-start(bf16[128,2048]{1,0:T(8,128)(2,1)S(1)} %collective-permute-done.4.refs_4_) | copy-start | bytes 1572868
  73.0 15.9 %collective-permute-start.7 = (bf16[128,2048]{1,0:T(8,128)(2,1)S(1)}, bf16[128,2048]{1,0:T(8,128)(2,1)S(1)}, u32[]{:S(2)}, u32[]{:S(2)}) collective-permute-start(bf16[128,2048]{1,0:T(8,128)(2,1)S(1)} %collective-permute-done.4.refs_4_), channel_id=1, source_target_pairs={{0,1},{1,0},{2,3},{3,2},{4,5},{5,4},{6,7},{7,6},{8,9},{9,8},{10,11... | collective-permute-start | bytes 1572872 | tf_op jit(solution)/shard_map/ppermute | solution.py:505
  84.0 10.9 %all-to-all-start.2 = ((bf16[8,4,32,128]{3,2,1,0:T(8,128)(2,1)}), bf16[8,4,32,128]{3,2,1,0:T(8,128)(2,1)S(1)}, u32[]{:S(2)}, u32[]{:S(2)}) async-start(bf16[8,4,32,128]{3,2,1,0:T(8,128)(2,1)} %emit.1), calls=%async_computation.2 | async-start | bytes 524288 | tf_op jit(solution)/shard_map/all_to_all | solution.py:509
  88.8 6.1 %copy-start.7 = (bf16[128,2048]{1,0:T(8,128)(2,1)}, bf16[128,2048]{1,0:T(8,128)(2,1)S(1)}, u32[]{:S(2)}) copy-start(bf16[128,2048]{1,0:T(8,128)(2,1)S(1)} %collective-permute-done.5.refs_5_) | copy-start | bytes 1572868
  88.8 6.1 %copy-start.8 = (bf16[128,2048]{1,0:T(8,128)(2,1)}, bf16[128,2048]{1,0:T(8,128)(2,1)S(1)}, u32[]{:S(2)}) copy-start(bf16[128,2048]{1,0:T(8,128)(2,1)S(1)} %collective-permute-done.6.refs_6_) | copy-start | bytes 1572868
  88.8 6.1 %copy-start.9 = (bf16[128,2048]{1,0:T(8,128)(2,1)}, bf16[128,2048]{1,0:T(8,128)(2,1)S(1)}, u32[]{:S(2)}) copy-start(bf16[128,2048]{1,0:T(8,128)(2,1)S(1)} %collective-permute-done.7.refs_7_) | copy-start | bytes 1572868
  94.9 17.5 %copy-start.2 = (bf16[32,2048]{1,0:T(8,128)(2,1)S(1)}, bf16[32,2048]{1,0:T(8,128)(2,1)}, u32[]{:S(2)}) copy-start(bf16[32,2048]{1,0:T(8,128)(2,1)} %tokens_ref.3) | copy-start | bytes 393220
  99.4 16.2 %copy-start.1 = (bf16[1,512,2048]{2,1,0:T(8,128)(2,1)S(1)}, bf16[1,512,2048]{2,1,0:T(8,128)(2,1)}, u32[]{:S(2)}) copy-start(bf16[1,512,2048]{2,1,0:T(8,128)(2,1)} %down_a_ref.1) | copy-start | bytes 6291460
  115.5 34.6 %collective-permute-start.8 = (bf16[1,2048,1024]{2,1,0:T(8,128)(2,1)}, bf16[1,2048,1024]{2,1,0:T(8,128)(2,1)S(1)}, u32[]{:S(2)}, u32[]{:S(2)}) collective-permute-start(bf16[1,2048,1024]{2,1,0:T(8,128)(2,1)} %up_a_ref.1), channel_id=1, source_target_pairs={{0,1},{1,0},{2,3},{3,2},{4,5},{5,4},{6,7},{7,6},{8,9},{9,8},{10,11... | collective-permute-start | bytes 12582920 | tf_op jit(solution)/shard_map/ppermute | solution.py:505
  115.6 34.5 %collective-permute-start.9 = (bf16[1,512,2048]{2,1,0:T(8,128)(2,1)S(1)}, bf16[1,512,2048]{2,1,0:T(8,128)(2,1)S(1)}, u32[]{:S(2)}, u32[]{:S(2)}) collective-permute-start(bf16[1,512,2048]{2,1,0:T(8,128)(2,1)S(1)} %copy-done.1), channel_id=1, source_target_pairs={{0,1},{1,0},{2,3},{3,2},{4,5},{5,4},{6,7},{7,6},{8,9},{9,8},{10,11... | collective-permute-start | bytes 6291464 | tf_op jit(solution)/shard_map/ppermute | solution.py:505
  116.1 34.0 %copy-start = (bf16[1,2048,1024]{2,1,0:T(8,128)(2,1)S(1)}, bf16[1,2048,1024]{2,1,0:T(8,128)(2,1)}, u32[]{:S(2)}) copy-start(bf16[1,2048,1024]{2,1,0:T(8,128)(2,1)} %up_a_ref.1) | copy-start | bytes 12582916

commit v7 on v5

--- a/solution.py
+++ b/solution.py
@@ -353,8 +353,7 @@
     )(place, near(gated), *weights)
 
 
-def join_body(parts_ref, tokens_ref, gain_ref, _, out_ref, copies_ref, normed_ref, sems):
-    width = tokens_ref.shape[1]
+def join_body(parts_ref, tokens_ref, gain_ref, out_ref, copies_ref, normed_ref, sems):
     total = parts_ref[0].astype(F32)
     for part in range(1, parts_ref.shape[0]):
         total = total + parts_ref[part].astype(F32)
@@ -362,7 +361,7 @@
     hidden = tokens_ref[...].astype(F32) + summed.astype(F32)
     normed_ref[...] = (hidden * rms_scale(hidden) * gain_ref[...]).astype(BF16)
     copies = [
-        pltpu.make_async_copy(normed_ref, copies_ref.at[at, :, pl.ds(0, width)], sems.at[at])
+        pltpu.make_async_copy(normed_ref, copies_ref.at[at], sems.at[at])
         for at in range(copies_ref.shape[0])
     ]
     for copy in copies:
@@ -372,59 +371,55 @@
         copy.wait()
 
 
-def join(parts, tokens, gain, payload):
-    anywhere = pl.BlockSpec(memory_space=pl.ANY)
+def join(parts, tokens, gain, copies):
     return pl.pallas_call(
         join_body,
-        in_specs=[resident(), resident(), resident(), anywhere],
-        out_specs=[resident(), anywhere],
+        in_specs=[resident()] * 3,
+        out_specs=[resident(), pl.BlockSpec(memory_space=pl.ANY)],
         out_shape=[
             jax.ShapeDtypeStruct(tokens.shape, BF16),
-            jax.ShapeDtypeStruct(payload.shape, BF16),
+            jax.ShapeDtypeStruct((copies,) + tokens.shape, BF16),
         ],
-        input_output_aliases={3: 1},
-        scratch_shapes=[
-            pltpu.VMEM(tokens.shape, BF16),
-            pltpu.SemaphoreType.DMA((payload.shape[0],)),
-        ],
+        scratch_shapes=[pltpu.VMEM(tokens.shape, BF16), pltpu.SemaphoreType.DMA((copies,))],
         name="join",
-    )(near(parts), tokens, gain[None], payload)
-
-
-def experts_body(x_ref, up_a_ref, down_a_ref, up_b_ref, down_b_ref, out_ref, *, tiles):
+    )(near(parts), near(tokens), gain[None])
+
+
+def experts_body(
+    place_ref, gates_ref, x_ref, up_a_ref, down_a_ref, up_b_ref, down_b_ref, out_ref,
+    *, x_count,
+):
     groups, each, width = out_ref.shape
     count = groups * each
     hidden_units = down_a_ref.shape[1]
-    tile = hidden_units // tiles
-    x = x_ref[:, :, :width].reshape(count, width)
-    extra = x_ref[:, :, width:].astype(F32).reshape(count, -1)
+    y_count = groups // x_count
+    blocks = []
+    for group in range(groups):
+        by_x = lax.rem(place_ref[3] + x_count - group // y_count, x_count)
+        by_y = lax.rem(place_ref[1] + y_count - group % y_count, y_count)
+        blocks.append(gates_ref[by_y * x_count + by_x])
+    gates = jnp.concatenate(blocks, axis=0)
+    x = x_ref[...].reshape(count, width)
     total = None
     for which, (up_ref, down_ref) in enumerate(((up_a_ref, down_a_ref), (up_b_ref, down_b_ref))):
         pre = jnp.dot(x, up_ref[0], preferred_element_type=F32)
         gate = pre[:, :hidden_units]
         activated = (gate * jax.nn.sigmoid(gate) * pre[:, hidden_units:]).astype(BF16)
         rows = jnp.dot(activated, down_ref[0], preferred_element_type=F32)
-        first = 3 * which
-        weight = (
-            extra[:, first:first + 1]
-            + extra[:, first + 1:first + 2]
-            + extra[:, first + 2:first + 3]
-        )
+        weight = gates[:, which:which + 1]
         scaled = rows.astype(BF16).astype(F32) * weight
         total = scaled if total is None else total + scaled
     out_ref[...] = total.astype(BF16).reshape(out_ref.shape)
 
 
-def experts_of(x, first, second, tiles):
-    groups, each, _ = x.shape
-    width = first[1].shape[2]
-    return pl.pallas_call(
-        functools.partial(experts_body, tiles=tiles),
-        in_specs=[resident()] * 5,
-        out_shape=jax.ShapeDtypeStruct((groups, each, width), BF16),
+def experts_of(place, gates, x, first, second, x_count):
+    return pl.pallas_call(
+        functools.partial(experts_body, x_count=x_count),
+        in_specs=[pl.BlockSpec(memory_space=pltpu.SMEM)] + [resident()] * 6,
+        out_shape=jax.ShapeDtypeStruct(x.shape, BF16),
         compiler_params=room(28),
         name="experts",
-    )(near(x), *[near(part) for part in first + second])
+    )(place, gates, near(x), *[near(part) for part in first + second])
 
 
 def total_body(*refs):
@@ -445,6 +440,13 @@
         out_shape=jax.ShapeDtypeStruct((len(halves) * each, width), BF16),
         name="total",
     )(*[near(parts) for parts in halves])
+
+
+def shift(value, axis, steps):
+    count = lax.axis_size(axis)
+    if steps == 0:
+        return value
+    return lax.ppermute(value, axis, [(at, (at + steps) % count) for at in range(count)])
 
 
 def send_y(value):
@@ -494,23 +496,35 @@
 
     copies = norm_copies(tokens, gain_in, chips)
     mine = exchange(copies, ("x", "y"))
-    pair = jnp.concatenate([w_output, swap_cores(w_output)], axis=0)
+    w_pair = (w_output, swap_cores(w_output))
     scalars = jnp.concatenate([strength_bias, decay_rate, decay_bias])
     w_logit = jnp.pad(w_scalar, ((0, 0), (0, LANES - w_scalar.shape[1])))
-    spots = jnp.stack([core, lax.axis_index("y").astype(jnp.int32), place])
-    mine, pair, scalars, w_logit, spots = lax.optimization_barrier(
-        (mine, pair, scalars, w_logit, spots)
+    row = lax.axis_index("y").astype(jnp.int32)
+    spots = jnp.stack([core, row, place, lax.axis_index("x").astype(jnp.int32)])
+    numbers = jnp.arange(expert_total, dtype=jnp.int32)
+    named = expert_ids[:, :, None] == numbers[None, None, :]
+    routes = jnp.sum(jnp.where(named, gate_weights[:, :, None], 0.0), axis=1)
+    routes = jnp.concatenate([shift(routes, "x", by) for by in range(x_count)], axis=1)
+    routes = jnp.stack([shift(routes, "y", by) for by in range(y_count)])
+    routes = routes.reshape(y_count, tok_dev, x_count, expert_total).transpose(0, 2, 1, 3)
+    chip = spots[3] * y_count + row
+    ours = jnp.stack([numbers == 2 * chip + core, numbers == 2 * chip + 1 - core], axis=1)
+    gates = jnp.sum(
+        jnp.where(ours[None, None, None], routes[..., None], 0.0), axis=-2
+    ).reshape(chips, tok_dev, core_count)
+    mine, w_pair, scalars, w_logit, spots, gates = lax.optimization_barrier(
+        (mine, w_pair, scalars, w_logit, spots, gates)
     )
     theirs = swap_cores(mine)
-    beside = send_y(pair)
+    beside = tuple(send_y(rows) for rows in w_pair)
 
     *parts, maps = block_maps(spots, scalars, mine, theirs, w_heads, w_logit, dim, ctx_count, 4)
     beside, maps = lax.optimization_barrier((beside, maps))
-    across = send_y(beside[:dim])
+    across = send_y(beside[0])
     all_maps = exchange(maps, "ctx")
     slope, base, gate = block_reads(spots, mine, theirs, w_heads, gain_head, parts, dim, PER_STEP)
     across, slope = lax.optimization_barrier((across, slope))
-    w_rows = [pair, beside, across, swap_cores(beside), swap_cores(across)]
+    w_rows = [*w_pair, *beside, across, *[swap_cores(rows) for rows in (*beside, across)]]
     gated = emit(
         spots, all_maps, state_init[0], slope, base, gate, x_count, y_count * core_count
     )
@@ -518,19 +532,11 @@
     gated = exchange(gated, ("y", "core")).reshape(heads, x_count * tok_dev, dim)
     partial = project(spots, gated, w_rows, x_count, 1024)
 
-    numbers = jnp.arange(expert_total, dtype=jnp.int32)
-    named = expert_ids[:, :, None] == numbers[None, None, :]
-    routes = jnp.sum(jnp.where(named, gate_weights[:, :, None], 0.0), axis=1)
-    routes = routes.reshape(tok_dev, chips, core_count).transpose(1, 0, 2)
-    routes = jnp.where(core == 0, routes, routes[:, :, ::-1])
-    routes = jnp.stack(pieces(routes), axis=-1).reshape(chips, tok_dev, -1)
-    payload = jnp.pad(routes, ((0, 0), (0, 0), (width, LANES - routes.shape[-1])))
-
-    summed, copies = join(exchange(partial, "x"), tokens, gain_expert, payload)
+    summed, copies = join(exchange(partial, "x"), tokens, gain_expert, chips)
     far_gate_up, far_down, summed = lax.optimization_barrier((w_gate_up, w_down, summed))
     swapped = (swap_cores(far_gate_up), swap_cores(far_down))
     received = exchange(copies, ("x", "y"))
-    outputs = experts_of(received, (w_gate_up, w_down), swapped, 2)
+    outputs = experts_of(spots, gates, received, (w_gate_up, w_down), swapped, x_count)
     expert_out = total_of([exchange(outputs, ("x", "y"))])
     return (summed, expert_out)
 

time: 188 us -> 193 us (1.027)
  waiting for transfers between devices: 50.6 us -> 37.7 us
  blocking collectives: 65.3 us -> 76.7 us
  starting transfers between devices: 25.5 us -> 35.9 us
  local copies, waits for them, and re-layouts: 5.06 us -> 1.86 us
    all_to_all x4 -> x3, waiting for transfers between devices: 41.9 us -> 12.7 us  [exchange(): return lax.all_to_all(value, axes, split_axis=0, concat_axis=0, tiled=True)]
    ppermute x0 -> x6, waiting for transfers between devices: none -> 19.4 us  [shift(): lax.ppermute(value, axis, [(at, (at + steps) % count) for at in range(cou...]
    all_to_all x2 -> x3, blocking collectives: 65.3 us -> 76.7 us  [exchange(): return lax.all_to_all(value, axes, split_axis=0, concat_axis=0, tiled=True)]
    ppermute x0 -> x6, starting transfers between devices: none -> 9.64 us  [shift(): lax.ppermute(value, axis, [(at, (at + steps) % count) for at in range(cou...]
    ppermute x2 -> x3, starting transfers between devices: 0.01 us -> 3.84 us  [send_y(): return lax.ppermute(value, ('y', 'core'), up + down)]
    all_to_all x4 -> x3, starting transfers between devices: 24.2 us -> 21.3 us  [exchange(): return lax.all_to_all(value, axes, split_axis=0, concat_axis=0, tiled=True)]
    ppermute x6 -> x7, waiting for transfers between devices: 4.3 us -> 2.2 us  [swap_cores(): return lax.ppermute(value, 'core', [(0, 1), (1, 0)])]
    ppermute x2 -> x3, waiting for transfers between devices: 4.42 us -> 3.36 us  [send_y(): return lax.ppermute(value, ('y', 'core'), up + down)]
  transfers between devices with their start and end apart: 12 -> 19, of which waited for: 7 -> 7; matrix products, arithmetic and copies ran while one was open for 4% -> 2% of each run, Pallas kernels for 10% -> 10%
where the time goes in v7:
time: 193 us
  blocking collectives  76.7 us (40%)
  waiting for transfers between devices  37.7 us (20%)
  Pallas kernels  35.9 us (19%)
  starting transfers between devices  35.9 us (19%)
  between operations  2.9 us (2%)
    all_to_all x3, blocking collectives, exchange(): return lax.all_to_all(value, axes, split_axis=0, concat_axis=0, tiled=True)  76.7 us
    all_to_all x3, starting transfers between devices, exchange(): return lax.all_to_all(value, axes, split_axis=0, concat_axis=0, tiled=True)  21.3 us
    ppermute x6, waiting for transfers between devices, shift(): lax.ppermute(value, axis, [(at, (at + steps) % count) for at in range(cou...  19.4 us
    all_to_all x3, waiting for transfers between devices, exchange(): return lax.all_to_all(value, axes, split_axis=0, concat_axis=0, tiled=True)  12.7 us
    pallas_call x1, Pallas kernels, block_maps(): pl.pallas_call(functools.partial(maps_body, parts=parts), in_specs=[scala...  9.8 us
    ppermute x6, starting transfers between devices, shift(): lax.ppermute(value, axis, [(at, (at + steps) % count) for at in range(cou...  9.64 us
    pallas_call x1, Pallas kernels, experts_of(): pl.pallas_call(functools.partial(experts_body, x_count=x_count), in_specs...  7.28 us
    pallas_call x1, Pallas kernels, block_reads(): pl.pallas_call(functools.partial(reads_body, per_step=per_step), grid=(sp...  5.81 us
  transfers between devices with their start and end apart: 19, of which 7 were waited for; matrix products, arithmetic and copies ran while one was open for 2% of the time, Pallas kernels for 10%

profile of v7, /device:TPU:8, one launch (start us, length us, event | category | flops | bytes accessed | tf_op | source)
XLA Modules:
  0.0 192.8 jit_solution(9154957876949597547)
XLA Ops:
  0.6 2.5 %norm_copies.1 = bf16[16,32,2048]{2,1,0:T(8,128)(2,1)} custom-call(bf16[32,2048]{1,0:T(8,128)(2,1)} %tokens_ref.3, f32[1,2048]{1,0:T(1,128)} %bitcast.15), custom_call_target="tpu_custom_call" | custom-call | tf_op jit(solution)/shard_map/norm_copies/pallas_call | solution.py:268
  3.2 0.0 copy-start.5
  3.2 7.5 %all-to-all-start = ((bf16[16,32,2048]{2,1,0:T(8,128)(2,1)}), bf16[16,32,2048]{2,1,0:T(8,128)(2,1)S(1)}, u32[]{:S(2)}, u32[]{:S(2)}) async-start(bf16[16,32,2048]{2,1,0:T(8,128)(2,1)} %norm_copies.1), calls=%async_computation | async-start | bytes 4194304 | tf_op jit(solution)/shard_map/all_to_all | solution.py:468
  10.8 0.2 select_reduce_fusion.1
  10.9 2.8 %collective-permute-start.3 = (f32[32,32]{1,0:T(8,128)S(1)}, f32[32,32]{1,0:T(8,128)S(1)}, u32[]{:S(2)}, u32[]{:S(2)}) collective-permute-start(f32[32,32]{1,0:T(8,128)S(1)} %select_reduce_fusion.1), channel_id=1, source_target_pairs={{0,24},{8,0},{16,8},{24,16},{1,25},{9,1},{17,9},{25,17},{2,26},{10... | collective-permute-start | bytes 12296 | tf_op jit(solution)/shard_map/ppermute | solution.py:449
  13.7 0.9 collective-permute-start.2
  14.5 0.9 collective-permute-start.1
  17.4 0.6 pad_maximum_fusion.1.scal_ref
  18.0 17.6 %collective-permute-done.3 = f32[32,32]{1,0:T(8,128)S(1)} collective-permute-done((f32[32,32]{1,0:T(8,128)S(1)}, f32[32,32]{1,0:T(8,128)S(1)}, u32[]{:S(2)}, u32[]{:S(2)}) %collective-permute-start.3) | collective-permute-done | bytes 4128 | tf_op jit(solution)/shard_map/ppermute | solution.py:449
  35.6 1.8 collective-permute-done.2
  37.4 0.1 pad_maximum_fusion
  37.4 0.6 collective-permute-start.6
  38.0 2.8 %collective-permute-start.5 = (f32[32,128]{1,0:T(8,128)S(1)}, f32[32,128]{1,0:T(8,128)S(1)}, u32[]{:S(2)}, u32[]{:S(2)}) collective-permute-start(f32[32,128]{1,0:T(8,128)S(1)} %pad_maximum_fusion), channel_id=1, source_target_pairs={{0,4},{2,6},{4,0},{6,2},{1,5},{3,7},{5,1},{7,3},{8,12},{10,14},{12... | collective-permute-start | bytes 49160 | tf_op jit(solution)/shard_map/ppermute | solution.py:449
  40.8 1.8 collective-permute-start.4
  42.6 0.6 pad_add_fusion.1.core_ref.place_ref
  43.3 0.3 copy.29
  43.6 0.9 pad.4.ws_ref
  44.5 0.1 stack.41
  44.6 0.1 stack.42
  44.7 0.1 stack.43
  44.8 0.1 stack.44
  44.9 0.1 maximum_bitcast_fusion
  45.0 0.2 select_reduce_fusion
  45.3 0.2 copy.31
  45.5 0.1 collective-permute-start.9
  45.6 1.8 collective-permute-start.7
  47.4 0.3 collective-permute-start.8
  47.7 2.2 %collective-permute-done.9.theirs_ref = bf16[16,32,2048]{2,1,0:T(8,128)(2,1)} collective-permute-done((bf16[16,32,2048]{2,1,0:T(8,128)(2,1)S(1)}, bf16[16,32,2048]{2,1,0:T(8,128)(2,1)}, u32[]{:S(2)}, u32[]{:S(2)}) %collective-permute-start.9) | collective-permute-done | bytes 2097184 | tf_op jit(solution)/shard_map/ppermute | solution.py:464
  49.9 9.8 %block_maps.1 = (bf16[8,128,128]{2,1,0:T(8,128)(2,1)}, f32[8,128,128]{2,1,0:T(8,128)}, f32[8,128,128]{2,1,0:T(8,128)}, bf16[8,128,256]{2,1,0:T(8,128)(2,1)}, bf1...) custom-call(s32[4]{0:T(128)} %pad_add_fusion.1.core_ref.place_ref, f32[3]{0:T(128)} %pad_maximum_fusion.1.scal_ref, ...), custom_call_target="tpu_custom_call" | custom-call | tf_op jit(solution)/shard_map/block_maps/pallas_call | solution.py:172
  59.7 0.9 collective-permute-done.8.refs_3_
  60.6 8.5 %all-to-all-start.1 = ((bf16[8,128,256]{2,1,0:T(8,128)(2,1)}), bf16[8,128,256]{2,1,0:T(8,128)(2,1)S(1)}, u32[]{:S(2)}, u32[]{:S(2)}) async-start(bf16[8,128,256]{2,1,0:T(8,128)(2,1)} %get-tuple-element.35), calls=%async_computation.1 | async-start | bytes 1048576 | tf_op jit(solution)/shard_map/all_to_all | solution.py:468
  69.0 1.7 collective-permute-start.10
  70.8 0.5 collective-permute-start.12
  71.3 5.8 %block_reads.1 = (bf16[1024,128]{1,0:T(8,128)(2,1)}, f32[1024,128]{1,0:T(8,128)}, f32[1024,128]{1,0:T(8,128)}) custom-call(s32[4]{0:T(128)} %pad_add_fusion.1.core_ref.place_ref, bf16[16,32,2048]{2,1,0:T(8,128)(2,1)} %copy-done.4, bf16[16,32,2048]{2,1,0:T(8,128)(2,1)} %collective-permute-done.9.theirs_ref, bf16[2048,512]{1,0:T(8,128)(2,1)} %wg_ref.1, ...), custom_call_target="tpu_custom_call" | custom-call | tf_op jit(solution)/shard_map/block_reads/pallas_call | solution.py:227
  77.1 2.5 %collective-permute-done.10.refs_4_ = bf16[128,2048]{1,0:T(8,128)(2,1)S(1)} collective-permute-done((bf16[128,2048]{1,0:T(8,128)(2,1)}, bf16[128,2048]{1,0:T(8,128)(2,1)S(1)}, u32[]{:S(2)}, u32[]{:S(2)}) %collective-permute-start.10) | collective-permute-done | bytes 524320 | tf_op jit(solution)/shard_map/ppermute | solution.py:456
  79.6 6.7 %all-to-all-done.1.maps_ref = bf16[8,128,256]{2,1,0:T(8,128)(2,1)S(1)} async-done(((bf16[8,128,256]{2,1,0:T(8,128)(2,1)}), bf16[8,128,256]{2,1,0:T(8,128)(2,1)S(1)}, u32[]{:S(2)}, u32[]{:S(2)}) %all-to-all-start.1) | async-done | bytes 524320 | tf_op jit(solution)/shard_map/all_to_all | solution.py:468
  86.3 3.0 %emit.1 = bf16[8,4,32,128]{3,2,1,0:T(8,128)(2,1)} custom-call(s32[4]{0:T(128)} %pad_add_fusion.1.core_ref.place_ref, bf16[8,128,256]{2,1,0:T(8,128)(2,1)S(1)} %all-to-all-done.1.maps_ref, f32[128,128]{1,0:T(8,128)} %bitcast.14, bf16[1024,128]{1,0:T(8,128)(2,1)} %get-tuple-element.43.slope_ref, f32[1024,128]{1,0:T(8,128)} %get-tuple-element.44.base_ref, ...), custom_call_target="tpu_custom_call" | custom-call | tf_op jit(solution)/shard_map/emit/pallas_call | solution.py:314
  89.2 5.3 %all-to-all-start.2 = ((bf16[8,4,32,128]{3,2,1,0:T(8,128)(2,1)}), bf16[8,4,32,128]{3,2,1,0:T(8,128)(2,1)S(1)}, u32[]{:S(2)}, u32[]{:S(2)}) async-start(bf16[8,4,32,128]{3,2,1,0:T(8,128)(2,1)} %emit.1), calls=%async_computation.2 | async-start | bytes 524288 | tf_op jit(solution)/shard_map/all_to_all | solution.py:468
  94.5 6.1 %all-to-all-done.2 = bf16[8,4,32,128]{3,2,1,0:T(8,128)(2,1)S(1)} async-done(((bf16[8,4,32,128]{3,2,1,0:T(8,128)(2,1)}), bf16[8,4,32,128]{3,2,1,0:T(8,128)(2,1)S(1)}, u32[]{:S(2)}, u32[]{:S(2)}) %all-to-all-start.2) | async-done | bytes 262176 | tf_op jit(solution)/shard_map/all_to_all | solution.py:468
  100.7 3.5 %project.1 = bf16[4,32,2048]{2,1,0:T(8,128)(2,1)} custom-call(s32[4]{0:T(128)} %pad_add_fusion.1.core_ref.place_ref, bf16[8,128,128]{2,1,0:T(8,128)(2,1)S(1)} %bitcast.13, bf16[128,2048]{1,0:T(8,128)(2,1)} %refs_0_, bf16[128,2048]{1,0:T(8,128)(2,1)} %collective-permute-done.refs_1_, bf16[128,2048]{1,0:T(8,128)(2,1)} %collective-permute-done.7.refs_2_, ...), custom_call_target="tpu_custom_call" | custom-call | tf_op jit(solution)/shard_map/project/pallas_call | solution.py:344
  104.2 12.8 %all_to_all.30.parts_ref = bf16[4,32,2048]{2,1,0:T(8,128)(2,1)S(1)} all-to-all(bf16[4,32,2048]{2,1,0:T(8,128)(2,1)} %project.1), channel_id=1, replica_groups=mesh['ctx'=8,'x'=4,'y'=4,'core'=2] {'x'}, dimensions={0} | all-to-all | bytes 1048576 | tf_op jit(solution)/shard_map/all_to_all | solution.py:468
  117.0 3.1 %join.1 = (bf16[32,2048]{1,0:T(8,128)(2,1)}, bf16[16,32,2048]{2,1,0:T(8,128)(2,1)}) custom-call(bf16[4,32,2048]{2,1,0:T(8,128)(2,1)S(1)} %all_to_all.30.parts_ref, bf16[32,2048]{1,0:T(8,128)(2,1)S(1)} %copy-done.2, f32[1,2048]{1,0:T(1,128)} %bitcast.16), custom_call_target="tpu_custom_call" | custom-call | tf_op jit(solution)/shard_map/join/pallas_call | solution.py:375
  120.1 0.1 collective-permute-start.14
  120.2 0.5 collective-permute-start.15
  120.7 32.8 %all_to_all.31.x_ref = bf16[16,32,2048]{2,1,0:T(8,128)(2,1)S(1)} all-to-all(bf16[16,32,2048]{2,1,0:T(8,128)(2,1)} %get-tuple-element.51), channel_id=1, replica_groups=mesh['ctx'=8,'x'=4,'y'=4,'core'=2] {'x','y'}, dimensions={0} | all-to-all | bytes 4194304 | tf_op jit(solution)/shard_map/all_to_all | solution.py:468
  153.5 7.3 %experts.1 = bf16[16,32,2048]{2,1,0:T(8,128)(2,1)S(1)} custom-call(s32[4]{0:T(128)S(1)} %copy-done.3, f32[16,32,2]{2,1,0:T(8,128)S(1)} %bitcast.12, bf16[16,32,2048]{2,1,0:T(8,128)(2,1)S(1)} %all_to_all.31.x_ref, bf16[1,2048,1024]{2,1,0:T(8,128)(2,1)S(1)} %copy-done, bf16[1,512,2048]{2,1,0:T(8,128)(2,1)S(1)} %copy-done.1, ...), custom_call_target="tpu_custom_call" | custom-call | tf_op jit(solution)/shard_map/experts/pallas_call | solution.py:416
  160.8 31.0 %all_to_all.32.refs_0_ = bf16[16,32,2048]{2,1,0:T(8,128)(2,1)S(1)} all-to-all(bf16[16,32,2048]{2,1,0:T(8,128)(2,1)S(1)} %experts.1), channel_id=1, replica_groups=mesh['ctx'=8,'x'=4,'y'=4,'core'=2] {'x','y'}, dimensions={0} | all-to-all | bytes 4194304 | tf_op jit(solution)/shard_map/all_to_all | solution.py:468
  191.8 0.9 total.1
  (43 shorter events, 0.1 us)
Async XLA Ops:
  3.2 7.6 %copy-start.11 = (f32[32,10]{0,1:T(8,128)S(1)}, f32[32,10]{0,1:T(8,128)}, u32[]{:S(2)}) copy-start(f32[32,10]{0,1:T(8,128)} %param.27) | copy-start | bytes 3844
  3.2 7.6 %copy-start.12 = (s32[32,10]{0,1:T(8,128)S(1)}, s32[32,10]{0,1:T(8,128)}, u32[]{:S(2)}) copy-start(s32[32,10]{0,1:T(8,128)} %param.26) | copy-start | bytes 3844
  3.2 12.2 %copy-start.5 = (bf16[128,2048]{1,0:T(8,128)(2,1)S(1)}, bf16[128,2048]{1,0:T(8,128)(2,1)}, u32[]{:S(2)}) copy-start(bf16[128,2048]{1,0:T(8,128)(2,1)} %refs_0_) | copy-start | bytes 1572868
  3.2 40.1 %copy-start.10 = (bf16[2048,2]{0,1:T(2,128)(2,1)S(1)}, bf16[2048,2]{0,1:T(2,128)(2,1)}, u32[]{:S(2)}) copy-start(bf16[2048,2]{0,1:T(2,128)(2,1)} %param.18) | copy-start | bytes 24580
  3.2 42.2 %all-to-all-start = ((bf16[16,32,2048]{2,1,0:T(8,128)(2,1)}), bf16[16,32,2048]{2,1,0:T(8,128)(2,1)S(1)}, u32[]{:S(2)}, u32[]{:S(2)}) async-start(bf16[16,32,2048]{2,1,0:T(8,128)(2,1)} %norm_copies.1), calls=%async_computation | async-start | bytes 4194304 | tf_op jit(solution)/shard_map/all_to_all | solution.py:468
  10.9 24.7 %collective-permute-start.3 = (f32[32,32]{1,0:T(8,128)S(1)}, f32[32,32]{1,0:T(8,128)S(1)}, u32[]{:S(2)}, u32[]{:S(2)}) collective-permute-start(f32[32,32]{1,0:T(8,128)S(1)} %select_reduce_fusion.1), channel_id=1, source_target_pairs={{0,24},{8,0},{16,8},{24,16},{1,25},{9,1},{17,9},{25,17},{2,26},{10... | collective-permute-start | bytes 12296 | tf_op jit(solution)/shard_map/ppermute | solution.py:449
  13.7 23.7 %collective-permute-start.2 = (f32[32,32]{1,0:T(8,128)S(1)}, f32[32,32]{1,0:T(8,128)S(1)}, u32[]{:S(2)}, u32[]{:S(2)}) collective-permute-start(f32[32,32]{1,0:T(8,128)S(1)} %select_reduce_fusion.1), channel_id=1, source_target_pairs={{0,16},{8,24},{16,0},{24,8},{1,17},{9,25},{17,1},{25,9},{2,18},{10... | collective-permute-start | bytes 12296 | tf_op jit(solution)/shard_map/ppermute | solution.py:449
  14.5 22.8 %collective-permute-start.1 = (f32[32,32]{1,0:T(8,128)S(1)}, f32[32,32]{1,0:T(8,128)S(1)}, u32[]{:S(2)}, u32[]{:S(2)}) collective-permute-start(f32[32,32]{1,0:T(8,128)S(1)} %select_reduce_fusion.1), channel_id=1, source_target_pairs={{0,8},{8,16},{16,24},{24,0},{1,9},{9,17},{17,25},{25,1},{2,10},{10... | collective-permute-start | bytes 12296 | tf_op jit(solution)/shard_map/ppermute | solution.py:449
  15.4 30.1 %collective-permute-start = (bf16[128,2048]{1,0:T(8,128)(2,1)S(1)}, bf16[128,2048]{1,0:T(8,128)(2,1)}, u32[]{:S(2)}, u32[]{:S(2)}) collective-permute-start(bf16[128,2048]{1,0:T(8,128)(2,1)S(1)} %copy-done.5), channel_id=1, source_target_pairs={{0,1},{1,0},{2,3},{3,2},{4,5},{5,4},{6,7},{7,6},{8,9},{9,8},{10,11... | collective-permute-start | bytes 1572872 | tf_op jit(solution)/shard_map/ppermute | solution.py:464
  37.4 7.4 %collective-permute-start.6 = (f32[32,128]{1,0:T(8,128)S(1)}, f32[32,128]{1,0:T(8,128)S(1)}, u32[]{:S(2)}, u32[]{:S(2)}) collective-permute-start(f32[32,128]{1,0:T(8,128)S(1)} %pad_maximum_fusion), channel_id=1, source_target_pairs={{0,6},{2,0},{4,2},{6,4},{1,7},{3,1},{5,3},{7,5},{8,14},{10,8},{12,... | collective-permute-start | bytes 49160 | tf_op jit(solution)/shard_map/ppermute | solution.py:449
  38.0 6.7 %collective-permute-start.5 = (f32[32,128]{1,0:T(8,128)S(1)}, f32[32,128]{1,0:T(8,128)S(1)}, u32[]{:S(2)}, u32[]{:S(2)}) collective-permute-start(f32[32,128]{1,0:T(8,128)S(1)} %pad_maximum_fusion), channel_id=1, source_target_pairs={{0,4},{2,6},{4,0},{6,2},{1,5},{3,7},{5,1},{7,3},{8,12},{10,14},{12... | collective-permute-start | bytes 49160 | tf_op jit(solution)/shard_map/ppermute | solution.py:449
  40.8 3.8 %collective-permute-start.4 = (f32[32,128]{1,0:T(8,128)S(1)}, f32[32,128]{1,0:T(8,128)S(1)}, u32[]{:S(2)}, u32[]{:S(2)}) collective-permute-start(f32[32,128]{1,0:T(8,128)S(1)} %pad_maximum_fusion), channel_id=1, source_target_pairs={{0,2},{2,4},{4,6},{6,0},{1,3},{3,5},{5,7},{7,1},{8,10},{10,12},{12... | collective-permute-start | bytes 49160 | tf_op jit(solution)/shard_map/ppermute | solution.py:449
  45.5 4.4 %copy-start.4 = (bf16[16,32,2048]{2,1,0:T(8,128)(2,1)}, bf16[16,32,2048]{2,1,0:T(8,128)(2,1)S(1)}, u32[]{:S(2)}) copy-start(bf16[16,32,2048]{2,1,0:T(8,128)(2,1)S(1)} %all-to-all-done.mine_ref) | copy-start | bytes 6291460
  45.5 4.4 %collective-permute-start.9 = (bf16[16,32,2048]{2,1,0:T(8,128)(2,1)S(1)}, bf16[16,32,2048]{2,1,0:T(8,128)(2,1)}, u32[]{:S(2)}, u32[]{:S(2)}) collective-permute-start(bf16[16,32,2048]{2,1,0:T(8,128)(2,1)S(1)} %all-to-all-done.mine_ref), channel_id=1, source_target_pairs={{0,1},{1,0},{2,3},{3,2},{4,5},{5,4},{6,7},{7,6},{8,9},{9,8},{10,11... | collective-permute-start | bytes 6291464 | tf_op jit(solution)/shard_map/ppermute | solution.py:464
  45.6 14.1 %collective-permute-start.7 = (bf16[128,2048]{1,0:T(8,128)(2,1)S(1)}, bf16[128,2048]{1,0:T(8,128)(2,1)}, u32[]{:S(2)}, u32[]{:S(2)}) collective-permute-start(bf16[128,2048]{1,0:T(8,128)(2,1)S(1)} %copy-done.5), channel_id=1, source_target_pairs={{0,2},{2,4},{4,6},{6,0},{1,7},{3,1},{5,3},{7,5},{8,10},{10,12},{12... | collective-permute-start | bytes 1572872 | tf_op jit(solution)/shard_map/ppermute | solution.py:456
  47.4 13.2 %collective-permute-start.8 = (bf16[128,2048]{1,0:T(8,128)(2,1)}, bf16[128,2048]{1,0:T(8,128)(2,1)}, u32[]{:S(2)}, u32[]{:S(2)}) collective-permute-start(bf16[128,2048]{1,0:T(8,128)(2,1)} %collective-permute-done.refs_1_), channel_id=1, source_target_pairs={{0,2},{2,4},{4,6},{6,0},{1,7},{3,1},{5,3},{7,5},{8,10},{10,12},{12... | collective-permute-start | bytes 1572872 | tf_op jit(solution)/shard_map/ppermute | solution.py:456
  60.6 25.7 %all-to-all-start.1 = ((bf16[8,128,256]{2,1,0:T(8,128)(2,1)}), bf16[8,128,256]{2,1,0:T(8,128)(2,1)S(1)}, u32[]{:S(2)}, u32[]{:S(2)}) async-start(bf16[8,128,256]{2,1,0:T(8,128)(2,1)} %get-tuple-element.35), calls=%async_computation.1 | async-start | bytes 1048576 | tf_op jit(solution)/shard_map/all_to_all | solution.py:468
  69.0 10.5 %collective-permute-start.10 = (bf16[128,2048]{1,0:T(8,128)(2,1)}, bf16[128,2048]{1,0:T(8,128)(2,1)S(1)}, u32[]{:S(2)}, u32[]{:S(2)}) collective-permute-start(bf16[128,2048]{1,0:T(8,128)(2,1)} %collective-permute-done.7.refs_2_), channel_id=1, source_target_pairs={{0,2},{2,4},{4,6},{6,0},{1,7},{3,1},{5,3},{7,5},{8,10},{10,12},{12... | collective-permute-start | bytes 1572872 | tf_op jit(solution)/shard_map/ppermute | solution.py:456
  70.8 23.7 %collective-permute-start.11 = (bf16[128,2048]{1,0:T(8,128)(2,1)}, bf16[128,2048]{1,0:T(8,128)(2,1)S(1)}, u32[]{:S(2)}, u32[]{:S(2)}) collective-permute-start(bf16[128,2048]{1,0:T(8,128)(2,1)} %collective-permute-done.7.refs_2_), channel_id=1, source_target_pairs={{0,1},{1,0},{2,3},{3,2},{4,5},{5,4},{6,7},{7,6},{8,9},{9,8},{10,11... | collective-permute-start | bytes 1572872 | tf_op jit(solution)/shard_map/ppermute | solution.py:464
  70.8 23.7 %collective-permute-start.12 = (bf16[128,2048]{1,0:T(8,128)(2,1)}, bf16[128,2048]{1,0:T(8,128)(2,1)S(1)}, u32[]{:S(2)}, u32[]{:S(2)}) collective-permute-start(bf16[128,2048]{1,0:T(8,128)(2,1)} %collective-permute-done.8.refs_3_), channel_id=1, source_target_pairs={{0,1},{1,0},{2,3},{3,2},{4,5},{5,4},{6,7},{7,6},{8,9},{9,8},{10,11... | collective-permute-start | bytes 1572872 | tf_op jit(solution)/shard_map/ppermute | solution.py:464
  79.6 21.1 %copy-start.6 = (bf16[128,2048]{1,0:T(8,128)(2,1)}, bf16[128,2048]{1,0:T(8,128)(2,1)S(1)}, u32[]{:S(2)}) copy-start(bf16[128,2048]{1,0:T(8,128)(2,1)S(1)} %collective-permute-done.10.refs_4_) | copy-start | bytes 1572868
  79.6 15.0 %collective-permute-start.13 = (bf16[128,2048]{1,0:T(8,128)(2,1)S(1)}, bf16[128,2048]{1,0:T(8,128)(2,1)S(1)}, u32[]{:S(2)}, u32[]{:S(2)}) collective-permute-start(bf16[128,2048]{1,0:T(8,128)(2,1)S(1)} %collective-permute-done.10.refs_4_), channel_id=1, source_target_pairs={{0,1},{1,0},{2,3},{3,2},{4,5},{5,4},{6,7},{7,6},{8,9},{9,8},{10,11... | collective-permute-start | bytes 1572872 | tf_op jit(solution)/shard_map/ppermute | solution.py:464
  89.2 11.4 %all-to-all-start.2 = ((bf16[8,4,32,128]{3,2,1,0:T(8,128)(2,1)}), bf16[8,4,32,128]{3,2,1,0:T(8,128)(2,1)S(1)}, u32[]{:S(2)}, u32[]{:S(2)}) async-start(bf16[8,4,32,128]{3,2,1,0:T(8,128)(2,1)} %emit.1), calls=%async_computation.2 | async-start | bytes 524288 | tf_op jit(solution)/shard_map/all_to_all | solution.py:468
  94.5 6.1 %copy-start.8 = (bf16[128,2048]{1,0:T(8,128)(2,1)}, bf16[128,2048]{1,0:T(8,128)(2,1)S(1)}, u32[]{:S(2)}) copy-start(bf16[128,2048]{1,0:T(8,128)(2,1)S(1)} %collective-permute-done.12.refs_6_) | copy-start | bytes 1572868
  94.5 6.1 %copy-start.7 = (bf16[128,2048]{1,0:T(8,128)(2,1)}, bf16[128,2048]{1,0:T(8,128)(2,1)S(1)}, u32[]{:S(2)}) copy-start(bf16[128,2048]{1,0:T(8,128)(2,1)S(1)} %collective-permute-done.11.refs_5_) | copy-start | bytes 1572868
  94.5 6.1 %copy-start.9 = (bf16[128,2048]{1,0:T(8,128)(2,1)}, bf16[128,2048]{1,0:T(8,128)(2,1)S(1)}, u32[]{:S(2)}) copy-start(bf16[128,2048]{1,0:T(8,128)(2,1)S(1)} %collective-permute-done.13.refs_7_) | copy-start | bytes 1572868
  100.6 16.4 %copy-start.2 = (bf16[32,2048]{1,0:T(8,128)(2,1)S(1)}, bf16[32,2048]{1,0:T(8,128)(2,1)}, u32[]{:S(2)}) copy-start(bf16[32,2048]{1,0:T(8,128)(2,1)} %tokens_ref.3) | copy-start | bytes 393220
  100.6 19.5 %copy-start.1 = (bf16[1,512,2048]{2,1,0:T(8,128)(2,1)S(1)}, bf16[1,512,2048]{2,1,0:T(8,128)(2,1)}, u32[]{:S(2)}) copy-start(bf16[1,512,2048]{2,1,0:T(8,128)(2,1)} %down_a_ref.1) | copy-start | bytes 6291460
  117.0 36.5 %copy-start.3 = (s32[4]{0:T(128)S(1)}, s32[4]{0:T(128)}, u32[]{:S(2)}) copy-start(s32[4]{0:T(128)} %pad_add_fusion.1.core_ref.place_ref) | copy-start | bytes 52
  120.1 33.4 %collective-permute-start.14 = (bf16[1,2048,1024]{2,1,0:T(8,128)(2,1)}, bf16[1,2048,1024]{2,1,0:T(8,128)(2,1)S(1)}, u32[]{:S(2)}, u32[]{:S(2)}) collective-permute-start(bf16[1,2048,1024]{2,1,0:T(8,128)(2,1)} %up_a_ref.1), channel_id=1, source_target_pairs={{0,1},{1,0},{2,3},{3,2},{4,5},{5,4},{6,7},{7,6},{8,9},{9,8},{10,11... | collective-permute-start | bytes 12582920 | tf_op jit(solution)/shard_map/ppermute | solution.py:464
  120.2 33.3 %collective-permute-start.15 = (bf16[1,512,2048]{2,1,0:T(8,128)(2,1)S(1)}, bf16[1,512,2048]{2,1,0:T(8,128)(2,1)S(1)}, u32[]{:S(2)}, u32[]{:S(2)}) collective-permute-start(bf16[1,512,2048]{2,1,0:T(8,128)(2,1)S(1)} %copy-done.1), channel_id=1, source_target_pairs={{0,1},{1,0},{2,3},{3,2},{4,5},{5,4},{6,7},{7,6},{8,9},{9,8},{10,11... | collective-permute-start | bytes 6291464 | tf_op jit(solution)/shard_map/ppermute | solution.py:464
  120.7 32.8 %copy-start = (bf16[1,2048,1024]{2,1,0:T(8,128)(2,1)S(1)}, bf16[1,2048,1024]{2,1,0:T(8,128)(2,1)}, u32[]{:S(2)}) copy-start(bf16[1,2048,1024]{2,1,0:T(8,128)(2,1)} %up_a_ref.1) | copy-start | bytes 12582916

commit v8 on v5

--- a/solution.py
+++ b/solution.py
@@ -58,6 +58,40 @@
     return rows
 
 
+def ours_body(mine_ref, wk_ref, wv_ref, ws_ref, out_ref):
+    groups, each, width = mine_ref.shape
+    w_all = jnp.concatenate([wk_ref[...], wv_ref[...], ws_ref[...]], axis=1)
+    x = mine_ref[...].reshape(groups * each, width)
+    out_ref[...] = jnp.dot(x, w_all, preferred_element_type=F32).reshape(out_ref.shape)
+
+
+def project_ours(mine, w, ws, dim, steps):
+    groups, each, width = mine.shape
+    total = 2 * dim + ws.shape[1]
+    return pl.pallas_call(
+        ours_body,
+        grid=(steps,),
+        in_specs=[
+            pl.BlockSpec((groups // steps, each, width), lambda i: (i, 0, 0)),
+            pl.BlockSpec((width, dim), lambda i: (0, 1)),
+            pl.BlockSpec((width, dim), lambda i: (0, 2)),
+            whole(ws.shape),
+        ],
+        out_specs=pl.BlockSpec((groups // steps, each, total), lambda i: (i, 0, 0)),
+        out_shape=jax.ShapeDtypeStruct((groups, each, total), F32),
+        name="project_ours",
+    )(mine, w, w, ws)
+
+
+def interleave(core, ours, others, each):
+    even = jnp.where(core == 0, ours, others)
+    odd = jnp.where(core == 0, others, ours)
+    rows = []
+    for at in range(0, ours.shape[0], each):
+        rows += [even[at:at + each], odd[at:at + each]]
+    return rows
+
+
 def maps_body(
     core_ref, scal_ref, mine_ref, theirs_ref, w_ref, ws_ref,
     key_ref, decay_ref, growth_ref, solved_ref, start_ref, maps_ref,
@@ -65,7 +99,8 @@
     *, parts,
 ):
     dim = maps_ref.shape[1]
-    groups = mine_ref.shape[0] // parts
+    groups = theirs_ref.shape[0] // parts
+    each, width = theirs_ref.shape[1:]
     w_copies = [
         pltpu.make_async_copy(w_ref.at[:, pl.ds(dim, 2 * dim)], w_buf, sems.at[0]),
         pltpu.make_async_copy(ws_ref, ws_buf, sems.at[1]),
@@ -99,7 +134,10 @@
         for copy in x_copies[part]:
             copy.wait()
         at = slice(part * groups, (part + 1) * groups)
-        rows_of += project_rows(core_ref[0], mine_buf[at], theirs_buf[at], w_all)
+        x = theirs_buf[at].reshape(groups * each, width)
+        others = jnp.dot(x, w_all, preferred_element_type=F32)
+        ours = mine_buf[at].reshape(groups * each, -1)
+        rows_of += interleave(core_ref[0], ours, others, each)
     projected = jnp.concatenate(rows_of, axis=0)
     logits = projected[:, 2 * dim:]
     every = range(projected.shape[0] // CHUNK)
@@ -132,13 +170,13 @@
         jnp.where(strict, gram[n] * decay[n] * beta[n], 0.0) for n in every
     ]
     inverse = [eye - jnp.where(differ < 2, b, 0.0) for b in below]
-    width = 2
-    while width < CHUNK:
-        ring = (differ >= width) & (differ < 2 * width)
+    span = 2
+    while span < CHUNK:
+        ring = (differ >= span) & (differ < 2 * span)
         corner = [jnp.where(ring, b, 0.0) for b in below]
         half = [mm(inverse[n], corner[n]) for n in every]
         inverse = [inverse[n] - mm(half[n], inverse[n]) for n in every]
-        width *= 2
+        span *= 2
     solved = [
         mm(
             inverse[n],
@@ -165,7 +203,7 @@
 
 
 def block_maps(core, scalars, mine, theirs, w, ws, dim, copies, parts):
-    groups, each, width = mine.shape
+    groups, each, width = theirs.shape
     count = 2 * groups * each // CHUNK
     scalar = pl.BlockSpec(memory_space=pltpu.SMEM)
     anywhere = pl.BlockSpec(memory_space=pl.ANY)
@@ -181,7 +219,7 @@
             jax.ShapeDtypeStruct((copies, dim, 2 * dim), BF16),
         ],
         scratch_shapes=[
-            pltpu.VMEM(mine.shape, BF16),
+            pltpu.VMEM(mine.shape, F32),
             pltpu.VMEM(theirs.shape, BF16),
             pltpu.VMEM((width, 2 * dim), BF16),
             pltpu.VMEM(ws.shape, BF16),
@@ -388,7 +426,7 @@
             pltpu.SemaphoreType.DMA((payload.shape[0],)),
         ],
         name="join",
-    )(near(parts), tokens, gain[None], payload)
+    )(near(parts), near(tokens), gain[None], payload)
 
 
 def experts_body(x_ref, up_a_ref, down_a_ref, up_b_ref, down_b_ref, out_ref, *, tiles):
@@ -494,30 +532,10 @@
 
     copies = norm_copies(tokens, gain_in, chips)
     mine = exchange(copies, ("x", "y"))
-    pair = jnp.concatenate([w_output, swap_cores(w_output)], axis=0)
+    w_pair = (w_output, swap_cores(w_output))
     scalars = jnp.concatenate([strength_bias, decay_rate, decay_bias])
     w_logit = jnp.pad(w_scalar, ((0, 0), (0, LANES - w_scalar.shape[1])))
     spots = jnp.stack([core, lax.axis_index("y").astype(jnp.int32), place])
-    mine, pair, scalars, w_logit, spots = lax.optimization_barrier(
-        (mine, pair, scalars, w_logit, spots)
-    )
-    theirs = swap_cores(mine)
-    beside = send_y(pair)
-
-    *parts, maps = block_maps(spots, scalars, mine, theirs, w_heads, w_logit, dim, ctx_count, 4)
-    beside, maps = lax.optimization_barrier((beside, maps))
-    across = send_y(beside[:dim])
-    all_maps = exchange(maps, "ctx")
-    slope, base, gate = block_reads(spots, mine, theirs, w_heads, gain_head, parts, dim, PER_STEP)
-    across, slope = lax.optimization_barrier((across, slope))
-    w_rows = [pair, beside, across, swap_cores(beside), swap_cores(across)]
-    gated = emit(
-        spots, all_maps, state_init[0], slope, base, gate, x_count, y_count * core_count
-    )
-    heads = y_count * core_count
-    gated = exchange(gated, ("y", "core")).reshape(heads, x_count * tok_dev, dim)
-    partial = project(spots, gated, w_rows, x_count, 1024)
-
     numbers = jnp.arange(expert_total, dtype=jnp.int32)
     named = expert_ids[:, :, None] == numbers[None, None, :]
     routes = jnp.sum(jnp.where(named, gate_weights[:, :, None], 0.0), axis=1)
@@ -525,6 +543,27 @@
     routes = jnp.where(core == 0, routes, routes[:, :, ::-1])
     routes = jnp.stack(pieces(routes), axis=-1).reshape(chips, tok_dev, -1)
     payload = jnp.pad(routes, ((0, 0), (0, 0), (width, LANES - routes.shape[-1])))
+
+    mine, w_pair, scalars, w_logit, spots, payload = lax.optimization_barrier(
+        (mine, w_pair, scalars, w_logit, spots, payload)
+    )
+    theirs = swap_cores(mine)
+    beside = tuple(send_y(rows) for rows in w_pair)
+
+    ours = project_ours(mine, w_heads, w_logit, dim, 2)
+    *parts, maps = block_maps(spots, scalars, ours, theirs, w_heads, w_logit, dim, ctx_count, 4)
+    beside, maps = lax.optimization_barrier((beside, maps))
+    across = send_y(beside[0])
+    all_maps = exchange(maps, "ctx")
+    slope, base, gate = block_reads(spots, mine, theirs, w_heads, gain_head, parts, dim, PER_STEP)
+    across, slope = lax.optimization_barrier((across, slope))
+    w_rows = [*w_pair, *beside, across, *[swap_cores(rows) for rows in (*beside, across)]]
+    gated = emit(
+        spots, all_maps, state_init[0], slope, base, gate, x_count, y_count * core_count
+    )
+    heads = y_count * core_count
+    gated = exchange(gated, ("y", "core")).reshape(heads, x_count * tok_dev, dim)
+    partial = project(spots, gated, w_rows, x_count, 1024)
 
     summed, copies = join(exchange(partial, "x"), tokens, gain_expert, payload)
     far_gate_up, far_down, summed = lax.optimization_barrier((w_gate_up, w_down, summed))

time: 188 us -> 188 us (level)
  blocking collectives: 65.3 us -> 78.2 us
  waiting for transfers between devices: 50.6 us -> 38.8 us
  Pallas kernels: 35.4 us -> 37.8 us
    all_to_all x2 -> x3, blocking collectives: 65.3 us -> 78.2 us  [exchange(): return lax.all_to_all(value, axes, split_axis=0, concat_axis=0, tiled=True)]
    all_to_all x4 -> x3, waiting for transfers between devices: 41.9 us -> 35.9 us  [exchange(): return lax.all_to_all(value, axes, split_axis=0, concat_axis=0, tiled=True)]
    ppermute x6 -> x7, waiting for transfers between devices: 4.3 us -> 0.02 us  [swap_cores(): return lax.ppermute(value, 'core', [(0, 1), (1, 0)])]
    pallas_call x0 -> x1, Pallas kernels: none -> 3.87 us  [project_ours(): pl.pallas_call(ours_body, grid=(steps,), in_specs=[pl.BlockSpec((groups /...]
    all_to_all x4 -> x3, starting transfers between devices: 24.2 us -> 20.8 us  [exchange(): return lax.all_to_all(value, axes, split_axis=0, concat_axis=0, tiled=True)]
    ppermute x2 -> x3, starting transfers between devices: 0.01 us -> 2.52 us  [send_y(): return lax.ppermute(value, ('y', 'core'), up + down)]
    slice x1 -> x0, local copies, waits for them, and re-layouts: 1.91 us -> none  [shards(): across = send_y(beside[:dim])]
    ppermute x2 -> x3, waiting for transfers between devices: 4.42 us -> 2.93 us  [send_y(): return lax.ppermute(value, ('y', 'core'), up + down)]
  transfers between devices with their start and end apart: 12 -> 13, of which waited for: 7 -> 5; matrix products, arithmetic and copies ran while one was open for 4% -> 2% of each run, Pallas kernels for 10% -> 11%
where the time goes in v8:
time: 188 us; the launch traced here: 187 us
  blocking collectives  78.2 us (42%)
  waiting for transfers between devices  38.8 us (21%)
  Pallas kernels  37.8 us (20%)
  starting transfers between devices  24.5 us (13%)
  local copies, waits for them, and re-layouts  3.65 us (2%)
  between operations  2.84 us (2%)
    all_to_all x3, blocking collectives, exchange(): return lax.all_to_all(value, axes, split_axis=0, concat_axis=0, tiled=True)  78.2 us
    all_to_all x3, waiting for transfers between devices, exchange(): return lax.all_to_all(value, axes, split_axis=0, concat_axis=0, tiled=True)  35.9 us
    all_to_all x3, starting transfers between devices, exchange(): return lax.all_to_all(value, axes, split_axis=0, concat_axis=0, tiled=True)  20.8 us
    pallas_call x1, Pallas kernels, block_maps(): pl.pallas_call(functools.partial(maps_body, parts=parts), in_specs=[scala...  8.56 us
    pallas_call x1, Pallas kernels, experts_of(): pl.pallas_call(functools.partial(experts_body, tiles=tiles), in_specs=[re...  6.73 us
    pallas_call x1, Pallas kernels, block_reads(): pl.pallas_call(functools.partial(reads_body, per_step=per_step), grid=(sp...  5.83 us
    pallas_call x1, Pallas kernels, project_ours(): pl.pallas_call(ours_body, grid=(steps,), in_specs=[pl.BlockSpec((groups /...  3.87 us
  transfers between devices with their start and end apart: 13, of which 5 were waited for; matrix products, arithmetic and copies ran while one was open for 2% of the time, Pallas kernels for 11%

profile of v8, /device:TPU:8, one launch (start us, length us, event | category | flops | bytes accessed | tf_op | source)
XLA Modules:
  0.0 187.3 jit_solution(3419046346925489483)
XLA Ops:
  0.6 2.5 %norm_copies.1 = bf16[16,32,2048]{2,1,0:T(8,128)(2,1)} custom-call(bf16[32,2048]{1,0:T(8,128)(2,1)} %tokens_ref.3, f32[1,2048]{1,0:T(1,128)} %bitcast.23), custom_call_target="tpu_custom_call" | custom-call | tf_op jit(solution)/shard_map/norm_copies/pallas_call | solution.py:306
  3.1 0.0 copy-start.4
  3.2 0.0 copy-start.11
  3.2 0.0 copy-start.12
  3.2 0.0 copy-start.10
  3.2 7.5 %all-to-all-start = ((bf16[16,32,2048]{2,1,0:T(8,128)(2,1)}), bf16[16,32,2048]{2,1,0:T(8,128)(2,1)S(1)}, u32[]{:S(2)}, u32[]{:S(2)}) async-start(bf16[16,32,2048]{2,1,0:T(8,128)(2,1)} %norm_copies.1), calls=%async_computation | async-start | bytes 4194304 | tf_op jit(solution)/shard_map/all_to_all | solution.py:504
  10.7 0.1 collective-permute-start
  10.9 0.2 select_reduce_fusion
  11.0 0.1 copy.31
  11.3 0.2 copy.35
  11.5 0.3 copy.30
  11.8 1.6 pad.9._
  13.3 0.9 pad.8.ws_ref
  16.2 0.6 pad_add_fusion.core_ref.place_ref
  16.8 0.6 pad_maximum_fusion.1.scal_ref
  17.4 0.0 collective-permute-done.refs_1_
  17.4 22.3 %all-to-all-done.mine_ref = bf16[16,32,2048]{2,1,0:T(8,128)(2,1)S(1)} async-done(((bf16[16,32,2048]{2,1,0:T(8,128)(2,1)}), bf16[16,32,2048]{2,1,0:T(8,128)(2,1)S(1)}, u32[]{:S(2)}, u32[]{:S(2)}) %all-to-all-start) | async-done | bytes 2097184 | tf_op jit(solution)/shard_map/all_to_all | solution.py:504
  39.7 0.0 collective-permute-start.3
  39.7 0.0 collective-permute-start.1
  39.8 0.8 collective-permute-start.2
  40.6 0.5 copy-done.3
  41.1 3.9 %project_ours.1.mine_ref = f32[16,32,384]{2,1,0:T(8,128)} custom-call(bf16[16,32,2048]{2,1,0:T(8,128)(2,1)} %copy-done.3, bf16[2048,512]{1,0:T(8,128)(2,1)} %wg_ref.1, bf16[2048,512]{1,0:T(8,128)(2,1)} %wg_ref.1, bf16[2048,128]{1,0:T(8,128)(2,1)} %pad.8.ws_ref), custom_call_target="tpu_custom_call" | custom-call | tf_op jit(solution)/shard_map/project_ours/pallas_call | solution.py:71
  44.9 0.0 collective-permute-done.3.theirs_ref
  44.9 8.6 %block_maps.1 = (bf16[8,128,128]{2,1,0:T(8,128)(2,1)}, f32[8,128,128]{2,1,0:T(8,128)}, f32[8,128,128]{2,1,0:T(8,128)}, bf16[8,128,256]{2,1,0:T(8,128)(2,1)}, bf1...) custom-call(s32[3]{0:T(128)} %pad_add_fusion.core_ref.place_ref, f32[3]{0:T(128)} %pad_maximum_fusion.1.scal_ref, ...), custom_call_target="tpu_custom_call" | custom-call | tf_op jit(solution)/shard_map/block_maps/pallas_call | solution.py:210
  53.5 0.0 collective-permute-done.1.refs_2_
  53.5 1.1 collective-permute-done.2.refs_3_
  54.7 8.5 %all-to-all-start.1 = ((bf16[8,128,256]{2,1,0:T(8,128)(2,1)}), bf16[8,128,256]{2,1,0:T(8,128)(2,1)S(1)}, u32[]{:S(2)}, u32[]{:S(2)}) async-start(bf16[8,128,256]{2,1,0:T(8,128)(2,1)} %get-tuple-element.35), calls=%async_computation.1 | async-start | bytes 1048576 | tf_op jit(solution)/shard_map/all_to_all | solution.py:504
  63.1 1.7 collective-permute-start.4
  64.8 0.0 collective-permute-start.5
  64.8 0.5 collective-permute-start.6
  65.3 5.8 %block_reads.1 = (bf16[1024,128]{1,0:T(8,128)(2,1)}, f32[1024,128]{1,0:T(8,128)}, f32[1024,128]{1,0:T(8,128)}) custom-call(s32[3]{0:T(128)} %pad_add_fusion.core_ref.place_ref, bf16[16,32,2048]{2,1,0:T(8,128)(2,1)} %copy-done.3, bf16[16,32,2048]{2,1,0:T(8,128)(2,1)} %collective-permute-done.3.theirs_ref, bf16[2048,512]{1,0:T(8,128)(2,1)} %wg_ref.1, ...), custom_call_target="tpu_custom_call" | custom-call | tf_op jit(solution)/shard_map/block_reads/pallas_call | solution.py:265
  71.1 1.8 collective-permute-done.4.refs_4_
  73.0 0.0 collective-permute-start.7
  73.0 7.5 %all-to-all-done.1.maps_ref = bf16[8,128,256]{2,1,0:T(8,128)(2,1)S(1)} async-done(((bf16[8,128,256]{2,1,0:T(8,128)(2,1)}), bf16[8,128,256]{2,1,0:T(8,128)(2,1)S(1)}, u32[]{:S(2)}, u32[]{:S(2)}) %all-to-all-start.1) | async-done | bytes 524320 | tf_op jit(solution)/shard_map/all_to_all | solution.py:504
  80.4 2.9 %emit.1 = bf16[8,4,32,128]{3,2,1,0:T(8,128)(2,1)} custom-call(s32[3]{0:T(128)} %pad_add_fusion.core_ref.place_ref, bf16[8,128,256]{2,1,0:T(8,128)(2,1)S(1)} %all-to-all-done.1.maps_ref, f32[128,128]{1,0:T(8,128)} %bitcast.22, bf16[1024,128]{1,0:T(8,128)(2,1)} %get-tuple-element.43.slope_ref, f32[1024,128]{1,0:T(8,128)} %get-tuple-element.44.base_ref, ...), custom_call_target="tpu_custom_call" | custom-call | tf_op jit(solution)/shard_map/emit/pallas_call | solution.py:352
  83.4 4.8 %all-to-all-start.2 = ((bf16[8,4,32,128]{3,2,1,0:T(8,128)(2,1)}), bf16[8,4,32,128]{3,2,1,0:T(8,128)(2,1)S(1)}, u32[]{:S(2)}, u32[]{:S(2)}) async-start(bf16[8,4,32,128]{3,2,1,0:T(8,128)(2,1)} %emit.1), calls=%async_computation.2 | async-start | bytes 524288 | tf_op jit(solution)/shard_map/all_to_all | solution.py:504
  88.2 6.1 %all-to-all-done.2 = bf16[8,4,32,128]{3,2,1,0:T(8,128)(2,1)S(1)} async-done(((bf16[8,4,32,128]{3,2,1,0:T(8,128)(2,1)}), bf16[8,4,32,128]{3,2,1,0:T(8,128)(2,1)S(1)}, u32[]{:S(2)}, u32[]{:S(2)}) %all-to-all-start.2) | async-done | bytes 262176 | tf_op jit(solution)/shard_map/all_to_all | solution.py:504
  94.3 0.0 copy-start.2
  94.3 3.4 %project.1 = bf16[4,32,2048]{2,1,0:T(8,128)(2,1)} custom-call(s32[3]{0:T(128)} %pad_add_fusion.core_ref.place_ref, bf16[8,128,128]{2,1,0:T(8,128)(2,1)S(1)} %bitcast.18, bf16[128,2048]{1,0:T(8,128)(2,1)} %refs_0_, bf16[128,2048]{1,0:T(8,128)(2,1)} %collective-permute-done.refs_1_, bf16[128,2048]{1,0:T(8,128)(2,1)} %copy-done.5, ...), custom_call_target="tpu_custom_call" | custom-call | tf_op jit(solution)/shard_map/project/pallas_call | solution.py:382
  97.7 13.0 %all_to_all.30.parts_ref = bf16[4,32,2048]{2,1,0:T(8,128)(2,1)S(1)} all-to-all(bf16[4,32,2048]{2,1,0:T(8,128)(2,1)} %project.1), channel_id=1, replica_groups=mesh['ctx'=8,'x'=4,'y'=4,'core'=2] {'x'}, dimensions={0} | all-to-all | bytes 1048576 | tf_op jit(solution)/shard_map/all_to_all | solution.py:504
  110.6 3.1 %join.1 = (bf16[32,2048]{1,0:T(8,128)(2,1)}, bf16[16,32,2176]{2,1,0:T(8,128)(2,1)}) custom-call(bf16[4,32,2048]{2,1,0:T(8,128)(2,1)S(1)} %all_to_all.30.parts_ref, bf16[32,2048]{1,0:T(8,128)(2,1)S(1)} %copy-done.2, f32[1,2048]{1,0:T(1,128)} %bitcast.24, bf16[16,32,2176]{2,1,0:T(8,128)(2,1)} %pad.9._), custom_call_target="tpu_custom_call", output_to_operand_aliasing={{1}: (3, {})} | custom-call | tf_op jit(solution)/shard_map/join/pallas_call | solution.py:415
  113.7 0.1 collective-permute-start.8
  113.8 0.5 collective-permute-start.9
  114.3 34.0 %all_to_all.31.x_ref = bf16[16,32,2176]{2,1,0:T(8,128)(2,1)S(1)} all-to-all(bf16[16,32,2176]{2,1,0:T(8,128)(2,1)} %get-tuple-element.51), channel_id=1, replica_groups=mesh['ctx'=8,'x'=4,'y'=4,'core'=2] {'x','y'}, dimensions={0} | all-to-all | bytes 4456448 | tf_op jit(solution)/shard_map/all_to_all | solution.py:504
  148.3 0.0 collective-permute-done.8.up_b_ref
  148.3 6.7 %experts.1 = bf16[16,32,2048]{2,1,0:T(8,128)(2,1)S(1)} custom-call(bf16[16,32,2176]{2,1,0:T(8,128)(2,1)S(1)} %all_to_all.31.x_ref, bf16[1,2048,1024]{2,1,0:T(8,128)(2,1)S(1)} %copy-done, bf16[1,512,2048]{2,1,0:T(8,128)(2,1)S(1)} %copy-done.1, bf16[1,2048,1024]{2,1,0:T(8,128)(2,1)S(1)} %collective-permute-done.8.up_b_ref, ...), custom_call_target="tpu_custom_call" | custom-call | tf_op jit(solution)/shard_map/experts/pallas_call | solution.py:459
  155.1 31.3 %all_to_all.32.refs_0_ = bf16[16,32,2048]{2,1,0:T(8,128)(2,1)S(1)} all-to-all(bf16[16,32,2048]{2,1,0:T(8,128)(2,1)S(1)} %experts.1), channel_id=1, replica_groups=mesh['ctx'=8,'x'=4,'y'=4,'core'=2] {'x','y'}, dimensions={0} | all-to-all | bytes 4194304 | tf_op jit(solution)/shard_map/all_to_all | solution.py:504
  186.3 0.9 total.1
  (29 shorter events, 0.2 us)
Async XLA Ops:
  3.1 7.6 %copy-start.4 = (bf16[128,2048]{1,0:T(8,128)(2,1)S(1)}, bf16[128,2048]{1,0:T(8,128)(2,1)}, u32[]{:S(2)}) copy-start(bf16[128,2048]{1,0:T(8,128)(2,1)} %refs_0_) | copy-start | bytes 1572868
  3.2 7.7 %copy-start.11 = (f32[32,10]{0,1:T(8,128)S(1)}, f32[32,10]{0,1:T(8,128)}, u32[]{:S(2)}) copy-start(f32[32,10]{0,1:T(8,128)} %param.27) | copy-start | bytes 3844
  3.2 7.7 %copy-start.12 = (s32[32,10]{0,1:T(8,128)S(1)}, s32[32,10]{0,1:T(8,128)}, u32[]{:S(2)}) copy-start(s32[32,10]{0,1:T(8,128)} %param.26) | copy-start | bytes 3844
  3.2 8.3 %copy-start.10 = (bf16[2048,2]{0,1:T(2,128)(2,1)S(1)}, bf16[2048,2]{0,1:T(2,128)(2,1)}, u32[]{:S(2)}) copy-start(bf16[2048,2]{0,1:T(2,128)(2,1)} %param.18) | copy-start | bytes 24580
  3.2 36.6 %all-to-all-start = ((bf16[16,32,2048]{2,1,0:T(8,128)(2,1)}), bf16[16,32,2048]{2,1,0:T(8,128)(2,1)S(1)}, u32[]{:S(2)}, u32[]{:S(2)}) async-start(bf16[16,32,2048]{2,1,0:T(8,128)(2,1)} %norm_copies.1), calls=%async_computation | async-start | bytes 4194304 | tf_op jit(solution)/shard_map/all_to_all | solution.py:504
  10.7 6.7 %collective-permute-start = (bf16[128,2048]{1,0:T(8,128)(2,1)S(1)}, bf16[128,2048]{1,0:T(8,128)(2,1)}, u32[]{:S(2)}, u32[]{:S(2)}) collective-permute-start(bf16[128,2048]{1,0:T(8,128)(2,1)S(1)} %copy-done.4), channel_id=1, source_target_pairs={{0,1},{1,0},{2,3},{3,2},{4,5},{5,4},{6,7},{7,6},{8,9},{9,8},{10,11... | collective-permute-start | bytes 1572872 | tf_op jit(solution)/shard_map/ppermute | solution.py:500
  39.7 1.3 copy-start.3
  39.7 5.2 %collective-permute-start.3 = (bf16[16,32,2048]{2,1,0:T(8,128)(2,1)S(1)}, bf16[16,32,2048]{2,1,0:T(8,128)(2,1)}, u32[]{:S(2)}, u32[]{:S(2)}) collective-permute-start(bf16[16,32,2048]{2,1,0:T(8,128)(2,1)S(1)} %all-to-all-done.mine_ref), channel_id=1, source_target_pairs={{0,1},{1,0},{2,3},{3,2},{4,5},{5,4},{6,7},{7,6},{8,9},{9,8},{10,11... | collective-permute-start | bytes 6291464 | tf_op jit(solution)/shard_map/ppermute | solution.py:500
  39.7 13.8 %collective-permute-start.1 = (bf16[128,2048]{1,0:T(8,128)(2,1)S(1)}, bf16[128,2048]{1,0:T(8,128)(2,1)S(1)}, u32[]{:S(2)}, u32[]{:S(2)}) collective-permute-start(bf16[128,2048]{1,0:T(8,128)(2,1)S(1)} %copy-done.4), channel_id=1, source_target_pairs={{0,2},{2,4},{4,6},{6,0},{1,7},{3,1},{5,3},{7,5},{8,10},{10,12},{12... | collective-permute-start | bytes 1572872 | tf_op jit(solution)/shard_map/ppermute | solution.py:492
  39.8 14.9 %collective-permute-start.2 = (bf16[128,2048]{1,0:T(8,128)(2,1)}, bf16[128,2048]{1,0:T(8,128)(2,1)}, u32[]{:S(2)}, u32[]{:S(2)}) collective-permute-start(bf16[128,2048]{1,0:T(8,128)(2,1)} %collective-permute-done.refs_1_), channel_id=1, source_target_pairs={{0,2},{2,4},{4,6},{6,0},{1,7},{3,1},{5,3},{7,5},{8,10},{10,12},{12... | collective-permute-start | bytes 1572872 | tf_op jit(solution)/shard_map/ppermute | solution.py:492
  53.5 17.6 %copy-start.5 = (bf16[128,2048]{1,0:T(8,128)(2,1)}, bf16[128,2048]{1,0:T(8,128)(2,1)S(1)}, u32[]{:S(2)}) copy-start(bf16[128,2048]{1,0:T(8,128)(2,1)S(1)} %collective-permute-done.1.refs_2_) | copy-start | bytes 1572868
  54.7 25.8 %all-to-all-start.1 = ((bf16[8,128,256]{2,1,0:T(8,128)(2,1)}), bf16[8,128,256]{2,1,0:T(8,128)(2,1)S(1)}, u32[]{:S(2)}, u32[]{:S(2)}) async-start(bf16[8,128,256]{2,1,0:T(8,128)(2,1)} %get-tuple-element.35), calls=%async_computation.1 | async-start | bytes 1048576 | tf_op jit(solution)/shard_map/all_to_all | solution.py:504
  63.1 9.8 %collective-permute-start.4 = (bf16[128,2048]{1,0:T(8,128)(2,1)S(1)}, bf16[128,2048]{1,0:T(8,128)(2,1)S(1)}, u32[]{:S(2)}, u32[]{:S(2)}) collective-permute-start(bf16[128,2048]{1,0:T(8,128)(2,1)S(1)} %collective-permute-done.1.refs_2_), channel_id=1, source_target_pairs={{0,2},{2,4},{4,6},{6,0},{1,7},{3,1},{5,3},{7,5},{8,10},{10,12},{12... | collective-permute-start | bytes 1572872 | tf_op jit(solution)/shard_map/ppermute | solution.py:492
  64.8 23.4 %collective-permute-start.5 = (bf16[128,2048]{1,0:T(8,128)(2,1)S(1)}, bf16[128,2048]{1,0:T(8,128)(2,1)S(1)}, u32[]{:S(2)}, u32[]{:S(2)}) collective-permute-start(bf16[128,2048]{1,0:T(8,128)(2,1)S(1)} %collective-permute-done.1.refs_2_), channel_id=1, source_target_pairs={{0,1},{1,0},{2,3},{3,2},{4,5},{5,4},{6,7},{7,6},{8,9},{9,8},{10,11... | collective-permute-start | bytes 1572872 | tf_op jit(solution)/shard_map/ppermute | solution.py:500
  64.8 23.4 %collective-permute-start.6 = (bf16[128,2048]{1,0:T(8,128)(2,1)}, bf16[128,2048]{1,0:T(8,128)(2,1)S(1)}, u32[]{:S(2)}, u32[]{:S(2)}) collective-permute-start(bf16[128,2048]{1,0:T(8,128)(2,1)} %collective-permute-done.2.refs_3_), channel_id=1, source_target_pairs={{0,1},{1,0},{2,3},{3,2},{4,5},{5,4},{6,7},{7,6},{8,9},{9,8},{10,11... | collective-permute-start | bytes 1572872 | tf_op jit(solution)/shard_map/ppermute | solution.py:500
  73.0 21.3 %copy-start.6 = (bf16[128,2048]{1,0:T(8,128)(2,1)}, bf16[128,2048]{1,0:T(8,128)(2,1)S(1)}, u32[]{:S(2)}) copy-start(bf16[128,2048]{1,0:T(8,128)(2,1)S(1)} %collective-permute-done.4.refs_4_) | copy-start | bytes 1572868
  73.0 15.2 %collective-permute-start.7 = (bf16[128,2048]{1,0:T(8,128)(2,1)S(1)}, bf16[128,2048]{1,0:T(8,128)(2,1)S(1)}, u32[]{:S(2)}, u32[]{:S(2)}) collective-permute-start(bf16[128,2048]{1,0:T(8,128)(2,1)S(1)} %collective-permute-done.4.refs_4_), channel_id=1, source_target_pairs={{0,1},{1,0},{2,3},{3,2},{4,5},{5,4},{6,7},{7,6},{8,9},{9,8},{10,11... | collective-permute-start | bytes 1572872 | tf_op jit(solution)/shard_map/ppermute | solution.py:500
  83.4 10.9 %all-to-all-start.2 = ((bf16[8,4,32,128]{3,2,1,0:T(8,128)(2,1)}), bf16[8,4,32,128]{3,2,1,0:T(8,128)(2,1)S(1)}, u32[]{:S(2)}, u32[]{:S(2)}) async-start(bf16[8,4,32,128]{3,2,1,0:T(8,128)(2,1)} %emit.1), calls=%async_computation.2 | async-start | bytes 524288 | tf_op jit(solution)/shard_map/all_to_all | solution.py:504
  88.2 6.1 %copy-start.7 = (bf16[128,2048]{1,0:T(8,128)(2,1)}, bf16[128,2048]{1,0:T(8,128)(2,1)S(1)}, u32[]{:S(2)}) copy-start(bf16[128,2048]{1,0:T(8,128)(2,1)S(1)} %collective-permute-done.5.refs_5_) | copy-start | bytes 1572868
  88.2 6.1 %copy-start.8 = (bf16[128,2048]{1,0:T(8,128)(2,1)}, bf16[128,2048]{1,0:T(8,128)(2,1)S(1)}, u32[]{:S(2)}) copy-start(bf16[128,2048]{1,0:T(8,128)(2,1)S(1)} %collective-permute-done.6.refs_6_) | copy-start | bytes 1572868
  88.2 6.1 %copy-start.9 = (bf16[128,2048]{1,0:T(8,128)(2,1)}, bf16[128,2048]{1,0:T(8,128)(2,1)S(1)}, u32[]{:S(2)}) copy-start(bf16[128,2048]{1,0:T(8,128)(2,1)S(1)} %collective-permute-done.7.refs_7_) | copy-start | bytes 1572868
  94.3 16.3 %copy-start.2 = (bf16[32,2048]{1,0:T(8,128)(2,1)S(1)}, bf16[32,2048]{1,0:T(8,128)(2,1)}, u32[]{:S(2)}) copy-start(bf16[32,2048]{1,0:T(8,128)(2,1)} %tokens_ref.3) | copy-start | bytes 393220
  97.7 16.2 %copy-start.1 = (bf16[1,512,2048]{2,1,0:T(8,128)(2,1)S(1)}, bf16[1,512,2048]{2,1,0:T(8,128)(2,1)}, u32[]{:S(2)}) copy-start(bf16[1,512,2048]{2,1,0:T(8,128)(2,1)} %down_a_ref.1) | copy-start | bytes 6291460
  113.7 34.6 %collective-permute-start.8 = (bf16[1,2048,1024]{2,1,0:T(8,128)(2,1)}, bf16[1,2048,1024]{2,1,0:T(8,128)(2,1)S(1)}, u32[]{:S(2)}, u32[]{:S(2)}) collective-permute-start(bf16[1,2048,1024]{2,1,0:T(8,128)(2,1)} %up_a_ref.1), channel_id=1, source_target_pairs={{0,1},{1,0},{2,3},{3,2},{4,5},{5,4},{6,7},{7,6},{8,9},{9,8},{10,11... | collective-permute-start | bytes 12582920 | tf_op jit(solution)/shard_map/ppermute | solution.py:500
  113.8 34.5 %collective-permute-start.9 = (bf16[1,512,2048]{2,1,0:T(8,128)(2,1)S(1)}, bf16[1,512,2048]{2,1,0:T(8,128)(2,1)S(1)}, u32[]{:S(2)}, u32[]{:S(2)}) collective-permute-start(bf16[1,512,2048]{2,1,0:T(8,128)(2,1)S(1)} %copy-done.1), channel_id=1, source_target_pairs={{0,1},{1,0},{2,3},{3,2},{4,5},{5,4},{6,7},{7,6},{8,9},{9,8},{10,11... | collective-permute-start | bytes 6291464 | tf_op jit(solution)/shard_map/ppermute | solution.py:500
  114.3 34.0 %copy-start = (bf16[1,2048,1024]{2,1,0:T(8,128)(2,1)S(1)}, bf16[1,2048,1024]{2,1,0:T(8,128)(2,1)}, u32[]{:S(2)}) copy-start(bf16[1,2048,1024]{2,1,0:T(8,128)(2,1)} %up_a_ref.1) | copy-start | bytes 12582916

commit v9 on v5

--- a/solution.py
+++ b/solution.py
@@ -388,7 +388,7 @@
             pltpu.SemaphoreType.DMA((payload.shape[0],)),
         ],
         name="join",
-    )(near(parts), tokens, gain[None], payload)
+    )(near(parts), near(tokens), gain[None], payload)
 
 
 def experts_body(x_ref, up_a_ref, down_a_ref, up_b_ref, down_b_ref, out_ref, *, tiles):
@@ -494,30 +494,10 @@
 
     copies = norm_copies(tokens, gain_in, chips)
     mine = exchange(copies, ("x", "y"))
-    pair = jnp.concatenate([w_output, swap_cores(w_output)], axis=0)
+    w_pair = (w_output, swap_cores(w_output))
     scalars = jnp.concatenate([strength_bias, decay_rate, decay_bias])
     w_logit = jnp.pad(w_scalar, ((0, 0), (0, LANES - w_scalar.shape[1])))
     spots = jnp.stack([core, lax.axis_index("y").astype(jnp.int32), place])
-    mine, pair, scalars, w_logit, spots = lax.optimization_barrier(
-        (mine, pair, scalars, w_logit, spots)
-    )
-    theirs = swap_cores(mine)
-    beside = send_y(pair)
-
-    *parts, maps = block_maps(spots, scalars, mine, theirs, w_heads, w_logit, dim, ctx_count, 4)
-    beside, maps = lax.optimization_barrier((beside, maps))
-    across = send_y(beside[:dim])
-    all_maps = exchange(maps, "ctx")
-    slope, base, gate = block_reads(spots, mine, theirs, w_heads, gain_head, parts, dim, PER_STEP)
-    across, slope = lax.optimization_barrier((across, slope))
-    w_rows = [pair, beside, across, swap_cores(beside), swap_cores(across)]
-    gated = emit(
-        spots, all_maps, state_init[0], slope, base, gate, x_count, y_count * core_count
-    )
-    heads = y_count * core_count
-    gated = exchange(gated, ("y", "core")).reshape(heads, x_count * tok_dev, dim)
-    partial = project(spots, gated, w_rows, x_count, 1024)
-
     numbers = jnp.arange(expert_total, dtype=jnp.int32)
     named = expert_ids[:, :, None] == numbers[None, None, :]
     routes = jnp.sum(jnp.where(named, gate_weights[:, :, None], 0.0), axis=1)
@@ -525,6 +505,27 @@
     routes = jnp.where(core == 0, routes, routes[:, :, ::-1])
     routes = jnp.stack(pieces(routes), axis=-1).reshape(chips, tok_dev, -1)
     payload = jnp.pad(routes, ((0, 0), (0, 0), (width, LANES - routes.shape[-1])))
+
+    mine, w_pair, scalars, w_logit, spots, payload = lax.optimization_barrier(
+        (mine, w_pair, scalars, w_logit, spots, payload)
+    )
+    theirs = swap_cores(mine)
+    beside = tuple(send_y(rows) for rows in w_pair)
+
+    *parts, maps = block_maps(spots, scalars, mine, theirs, w_heads, w_logit, dim, ctx_count, 4)
+    first, maps = lax.optimization_barrier((beside[0], maps))
+    across = send_y(first)
+    all_maps = exchange(maps, "ctx")
+    slope, base, gate = block_reads(spots, mine, theirs, w_heads, gain_head, parts, dim, PER_STEP)
+    across, second, slope = lax.optimization_barrier((across, beside[1], slope))
+    beside = (first, second)
+    w_rows = [*w_pair, *beside, across, *[swap_cores(rows) for rows in (*beside, across)]]
+    gated = emit(
+        spots, all_maps, state_init[0], slope, base, gate, x_count, y_count * core_count
+    )
+    heads = y_count * core_count
+    gated = exchange(gated, ("y", "core")).reshape(heads, x_count * tok_dev, dim)
+    partial = project(spots, gated, w_rows, x_count, 1024)
 
     summed, copies = join(exchange(partial, "x"), tokens, gain_expert, payload)
     far_gate_up, far_down, summed = lax.optimization_barrier((w_gate_up, w_down, summed))

time: 188 us -> 188 us (level)
  blocking collectives: 65.3 us -> 78.2 us
  waiting for transfers between devices: 50.6 us -> 43 us
  starting transfers between devices: 25.5 us -> 23.1 us
  local copies, waits for them, and re-layouts: 5.06 us -> 3.15 us
    all_to_all x2 -> x3, blocking collectives: 65.3 us -> 78.2 us  [exchange(): return lax.all_to_all(value, axes, split_axis=0, concat_axis=0, tiled=True)]
    all_to_all x4 -> x3, waiting for transfers between devices: 41.9 us -> 30.7 us  [exchange(): return lax.all_to_all(value, axes, split_axis=0, concat_axis=0, tiled=True)]
    ppermute x2 -> x3, waiting for transfers between devices: 4.42 us -> 8 us  [send_y(): return lax.ppermute(value, ('y', 'core'), up + down)]
    all_to_all x4 -> x3, starting transfers between devices: 24.2 us -> 20.8 us  [exchange(): return lax.all_to_all(value, axes, split_axis=0, concat_axis=0, tiled=True)]
    slice x1 -> x0, local copies, waits for them, and re-layouts: 1.91 us -> none  [shards(): across = send_y(beside[:dim])]
    ppermute x6 -> x7, waiting for transfers between devices: 4.3 us -> 4.3 us  [swap_cores(): return lax.ppermute(value, 'core', [(0, 1), (1, 0)])]
  transfers between devices with their start and end apart: 12 -> 13, of which waited for: 7 -> 6; matrix products, arithmetic and copies ran while one was open for 4% -> 2% of each run, Pallas kernels for 10% -> 10%
where the time goes in v9:
time: 188 us; the launch traced here: 187 us
  blocking collectives  78.2 us (42%)
  waiting for transfers between devices  43 us (23%)
  Pallas kernels  35.3 us (19%)
  starting transfers between devices  23.1 us (12%)
  local copies, waits for them, and re-layouts  3.15 us (2%)
  between operations  2.84 us (2%)
    all_to_all x3, blocking collectives, exchange(): return lax.all_to_all(value, axes, split_axis=0, concat_axis=0, tiled=True)  78.2 us
    all_to_all x3, waiting for transfers between devices, exchange(): return lax.all_to_all(value, axes, split_axis=0, concat_axis=0, tiled=True)  30.7 us
    all_to_all x3, starting transfers between devices, exchange(): return lax.all_to_all(value, axes, split_axis=0, concat_axis=0, tiled=True)  20.8 us
    pallas_call x1, Pallas kernels, block_maps(): pl.pallas_call(functools.partial(maps_body, parts=parts), in_specs=[scala...  9.81 us
    ppermute x3, waiting for transfers between devices, send_y(): return lax.ppermute(value, ('y', 'core'), up + down)  8 us
    pallas_call x1, Pallas kernels, experts_of(): pl.pallas_call(functools.partial(experts_body, tiles=tiles), in_specs=[re...  6.73 us
    pallas_call x1, Pallas kernels, block_reads(): pl.pallas_call(functools.partial(reads_body, per_step=per_step), grid=(sp...  5.88 us
    ppermute x7, waiting for transfers between devices, swap_cores(): return lax.ppermute(value, 'core', [(0, 1), (1, 0)])  4.3 us
  transfers between devices with their start and end apart: 13, of which 6 were waited for; matrix products, arithmetic and copies ran while one was open for 2% of the time, Pallas kernels for 10%

profile of v9, /device:TPU:8, one launch (start us, length us, event | category | flops | bytes accessed | tf_op | source)
XLA Modules:
  0.0 187.0 jit_solution(11154270136066789117)
XLA Ops:
  0.6 2.5 %norm_copies.1 = bf16[16,32,2048]{2,1,0:T(8,128)(2,1)} custom-call(bf16[32,2048]{1,0:T(8,128)(2,1)} %tokens_ref.3, f32[1,2048]{1,0:T(1,128)} %bitcast.23), custom_call_target="tpu_custom_call" | custom-call | tf_op jit(solution)/shard_map/norm_copies/pallas_call | solution.py:268
  3.1 0.0 copy-start.4
  3.2 0.0 copy-start.11
  3.2 0.0 copy-start.12
  3.2 0.0 copy-start.10
  3.2 7.5 %all-to-all-start = ((bf16[16,32,2048]{2,1,0:T(8,128)(2,1)}), bf16[16,32,2048]{2,1,0:T(8,128)(2,1)S(1)}, u32[]{:S(2)}, u32[]{:S(2)}) async-start(bf16[16,32,2048]{2,1,0:T(8,128)(2,1)} %norm_copies.1), calls=%async_computation | async-start | bytes 4194304 | tf_op jit(solution)/shard_map/all_to_all | solution.py:466
  10.7 0.1 collective-permute-start
  10.9 0.2 select_reduce_fusion
  11.0 0.1 copy.31
  11.3 0.2 copy.35
  11.5 0.3 copy.30
  11.8 1.6 pad.9._
  13.3 0.9 pad.8.ws_ref
  16.2 0.6 pad_add_fusion.core_ref.place_ref
  16.8 0.6 pad_maximum_fusion.1.scal_ref
  17.4 0.0 collective-permute-done.refs_1_
  17.4 22.4 %all-to-all-done.mine_ref = bf16[16,32,2048]{2,1,0:T(8,128)(2,1)S(1)} async-done(((bf16[16,32,2048]{2,1,0:T(8,128)(2,1)}), bf16[16,32,2048]{2,1,0:T(8,128)(2,1)S(1)}, u32[]{:S(2)}, u32[]{:S(2)}) %all-to-all-start) | async-done | bytes 2097184 | tf_op jit(solution)/shard_map/all_to_all | solution.py:466
  39.7 0.0 collective-permute-start.2
  39.7 0.0 collective-permute-start.1
  39.8 4.3 %collective-permute-done.2.theirs_ref = bf16[16,32,2048]{2,1,0:T(8,128)(2,1)} collective-permute-done((bf16[16,32,2048]{2,1,0:T(8,128)(2,1)S(1)}, bf16[16,32,2048]{2,1,0:T(8,128)(2,1)}, u32[]{:S(2)}, u32[]{:S(2)}) %collective-permute-start.2) | collective-permute-done | bytes 2097184 | tf_op jit(solution)/shard_map/ppermute | solution.py:462
  44.0 9.8 %block_maps.1 = (bf16[8,128,128]{2,1,0:T(8,128)(2,1)}, f32[8,128,128]{2,1,0:T(8,128)}, f32[8,128,128]{2,1,0:T(8,128)}, bf16[8,128,256]{2,1,0:T(8,128)(2,1)}, bf1...) custom-call(s32[3]{0:T(128)} %pad_add_fusion.core_ref.place_ref, f32[3]{0:T(128)} %pad_maximum_fusion.1.scal_ref, ...), custom_call_target="tpu_custom_call" | custom-call | tf_op jit(solution)/shard_map/block_maps/pallas_call | solution.py:172
  53.9 0.0 collective-permute-done.1.refs_2_
  53.9 8.5 %all-to-all-start.1 = ((bf16[8,128,256]{2,1,0:T(8,128)(2,1)}), bf16[8,128,256]{2,1,0:T(8,128)(2,1)S(1)}, u32[]{:S(2)}, u32[]{:S(2)}) async-start(bf16[8,128,256]{2,1,0:T(8,128)(2,1)} %get-tuple-element.34), calls=%async_computation.1 | async-start | bytes 1048576 | tf_op jit(solution)/shard_map/all_to_all | solution.py:466
  62.4 0.0 collective-permute-start.4
  62.4 0.8 collective-permute-start.3
  63.2 0.3 collective-permute-start.5
  63.5 5.9 %block_reads.1 = (bf16[1024,128]{1,0:T(8,128)(2,1)}, f32[1024,128]{1,0:T(8,128)}, f32[1024,128]{1,0:T(8,128)}) custom-call(s32[3]{0:T(128)} %pad_add_fusion.core_ref.place_ref, bf16[16,32,2048]{2,1,0:T(8,128)(2,1)} %copy-done.3, bf16[16,32,2048]{2,1,0:T(8,128)(2,1)} %collective-permute-done.2.theirs_ref, bf16[2048,512]{1,0:T(8,128)(2,1)} %wg_ref.1, ...), custom_call_target="tpu_custom_call" | custom-call | tf_op jit(solution)/shard_map/block_reads/pallas_call | solution.py:227
  69.4 2.4 %collective-permute-done.4.refs_3_ = bf16[128,2048]{1,0:T(8,128)(2,1)S(1)} collective-permute-done((bf16[128,2048]{1,0:T(8,128)(2,1)}, bf16[128,2048]{1,0:T(8,128)(2,1)S(1)}, u32[]{:S(2)}, u32[]{:S(2)}) %collective-permute-start.4) | collective-permute-done | bytes 524320 | tf_op jit(solution)/shard_map/ppermute | solution.py:454
  71.7 5.6 %collective-permute-done.3.refs_4_ = bf16[128,2048]{1,0:T(8,128)(2,1)S(1)} collective-permute-done((bf16[128,2048]{1,0:T(8,128)(2,1)S(1)}, bf16[128,2048]{1,0:T(8,128)(2,1)S(1)}, u32[]{:S(2)}, u32[]{:S(2)}) %collective-permute-start.3) | collective-permute-done | bytes 524320 | tf_op jit(solution)/shard_map/ppermute | solution.py:454
  77.4 0.0 collective-permute-start.6
  77.4 0.5 collective-permute-start.7
  77.9 2.3 %all-to-all-done.1.maps_ref = bf16[8,128,256]{2,1,0:T(8,128)(2,1)S(1)} async-done(((bf16[8,128,256]{2,1,0:T(8,128)(2,1)}), bf16[8,128,256]{2,1,0:T(8,128)(2,1)S(1)}, u32[]{:S(2)}, u32[]{:S(2)}) %all-to-all-start.1) | async-done | bytes 524320 | tf_op jit(solution)/shard_map/all_to_all | solution.py:466
  80.2 2.9 %emit.1 = bf16[8,4,32,128]{3,2,1,0:T(8,128)(2,1)} custom-call(s32[3]{0:T(128)} %pad_add_fusion.core_ref.place_ref, bf16[8,128,256]{2,1,0:T(8,128)(2,1)S(1)} %all-to-all-done.1.maps_ref, f32[128,128]{1,0:T(8,128)} %bitcast.22, bf16[1024,128]{1,0:T(8,128)(2,1)} %get-tuple-element.43.slope_ref, f32[1024,128]{1,0:T(8,128)} %get-tuple-element.44.base_ref, ...), custom_call_target="tpu_custom_call" | custom-call | tf_op jit(solution)/shard_map/emit/pallas_call | solution.py:314
  83.1 4.8 %all-to-all-start.2 = ((bf16[8,4,32,128]{3,2,1,0:T(8,128)(2,1)}), bf16[8,4,32,128]{3,2,1,0:T(8,128)(2,1)S(1)}, u32[]{:S(2)}, u32[]{:S(2)}) async-start(bf16[8,4,32,128]{3,2,1,0:T(8,128)(2,1)} %emit.1), calls=%async_computation.2 | async-start | bytes 524288 | tf_op jit(solution)/shard_map/all_to_all | solution.py:466
  87.9 0.0 collective-permute-done.5.refs_5_
  87.9 0.0 collective-permute-done.6.refs_6_
  87.9 0.0 collective-permute-done.7.refs_7_
  87.9 6.1 %all-to-all-done.2 = bf16[8,4,32,128]{3,2,1,0:T(8,128)(2,1)S(1)} async-done(((bf16[8,4,32,128]{3,2,1,0:T(8,128)(2,1)}), bf16[8,4,32,128]{3,2,1,0:T(8,128)(2,1)S(1)}, u32[]{:S(2)}, u32[]{:S(2)}) %all-to-all-start.2) | async-done | bytes 262176 | tf_op jit(solution)/shard_map/all_to_all | solution.py:466
  94.0 0.0 copy-start.2
  94.0 3.4 %project.1 = bf16[4,32,2048]{2,1,0:T(8,128)(2,1)} custom-call(s32[3]{0:T(128)} %pad_add_fusion.core_ref.place_ref, bf16[8,128,128]{2,1,0:T(8,128)(2,1)S(1)} %bitcast.18, bf16[128,2048]{1,0:T(8,128)(2,1)} %refs_0_, bf16[128,2048]{1,0:T(8,128)(2,1)} %collective-permute-done.refs_1_, bf16[128,2048]{1,0:T(8,128)(2,1)} %copy-done.5, bf16[128,2048]{1,0:T(8,128)(2,1)} %copy-done.6, ...), custom_call_target="tpu_custom_call" | custom-call | tf_op jit(solution)/shard_map/project/pallas_call | solution.py:344
  97.4 13.0 %all_to_all.30.parts_ref = bf16[4,32,2048]{2,1,0:T(8,128)(2,1)S(1)} all-to-all(bf16[4,32,2048]{2,1,0:T(8,128)(2,1)} %project.1), channel_id=1, replica_groups=mesh['ctx'=8,'x'=4,'y'=4,'core'=2] {'x'}, dimensions={0} | all-to-all | bytes 1048576 | tf_op jit(solution)/shard_map/all_to_all | solution.py:466
  110.4 3.1 %join.1 = (bf16[32,2048]{1,0:T(8,128)(2,1)}, bf16[16,32,2176]{2,1,0:T(8,128)(2,1)}) custom-call(bf16[4,32,2048]{2,1,0:T(8,128)(2,1)S(1)} %all_to_all.30.parts_ref, bf16[32,2048]{1,0:T(8,128)(2,1)S(1)} %copy-done.2, f32[1,2048]{1,0:T(1,128)} %bitcast.24, bf16[16,32,2176]{2,1,0:T(8,128)(2,1)} %pad.9._), custom_call_target="tpu_custom_call", output_to_operand_aliasing={{1}: (3, {})} | custom-call | tf_op jit(solution)/shard_map/join/pallas_call | solution.py:377
  113.5 0.1 collective-permute-start.8
  113.6 0.5 collective-permute-start.9
  114.1 34.0 %all_to_all.31.x_ref = bf16[16,32,2176]{2,1,0:T(8,128)(2,1)S(1)} all-to-all(bf16[16,32,2176]{2,1,0:T(8,128)(2,1)} %get-tuple-element.51), channel_id=1, replica_groups=mesh['ctx'=8,'x'=4,'y'=4,'core'=2] {'x','y'}, dimensions={0} | all-to-all | bytes 4456448 | tf_op jit(solution)/shard_map/all_to_all | solution.py:466
  148.1 6.7 %experts.1 = bf16[16,32,2048]{2,1,0:T(8,128)(2,1)S(1)} custom-call(bf16[16,32,2176]{2,1,0:T(8,128)(2,1)S(1)} %all_to_all.31.x_ref, bf16[1,2048,1024]{2,1,0:T(8,128)(2,1)S(1)} %copy-done, bf16[1,512,2048]{2,1,0:T(8,128)(2,1)S(1)} %copy-done.1, bf16[1,2048,1024]{2,1,0:T(8,128)(2,1)S(1)} %collective-permute-done.8.up_b_ref, ...), custom_call_target="tpu_custom_call" | custom-call | tf_op jit(solution)/shard_map/experts/pallas_call | solution.py:421
  154.8 31.3 %all_to_all.32.refs_0_ = bf16[16,32,2048]{2,1,0:T(8,128)(2,1)S(1)} all-to-all(bf16[16,32,2048]{2,1,0:T(8,128)(2,1)S(1)} %experts.1), channel_id=1, replica_groups=mesh['ctx'=8,'x'=4,'y'=4,'core'=2] {'x','y'}, dimensions={0} | all-to-all | bytes 4194304 | tf_op jit(solution)/shard_map/all_to_all | solution.py:466
  186.1 0.9 total.1
  (28 shorter events, 0.2 us)
Async XLA Ops:
  3.1 7.6 %copy-start.4 = (bf16[128,2048]{1,0:T(8,128)(2,1)S(1)}, bf16[128,2048]{1,0:T(8,128)(2,1)}, u32[]{:S(2)}) copy-start(bf16[128,2048]{1,0:T(8,128)(2,1)} %refs_0_) | copy-start | bytes 1572868
  3.2 7.7 %copy-start.11 = (f32[32,10]{0,1:T(8,128)S(1)}, f32[32,10]{0,1:T(8,128)}, u32[]{:S(2)}) copy-start(f32[32,10]{0,1:T(8,128)} %param.27) | copy-start | bytes 3844
  3.2 7.7 %copy-start.12 = (s32[32,10]{0,1:T(8,128)S(1)}, s32[32,10]{0,1:T(8,128)}, u32[]{:S(2)}) copy-start(s32[32,10]{0,1:T(8,128)} %param.26) | copy-start | bytes 3844
  3.2 8.3 %copy-start.10 = (bf16[2048,2]{0,1:T(2,128)(2,1)S(1)}, bf16[2048,2]{0,1:T(2,128)(2,1)}, u32[]{:S(2)}) copy-start(bf16[2048,2]{0,1:T(2,128)(2,1)} %param.18) | copy-start | bytes 24580
  3.2 36.6 %all-to-all-start = ((bf16[16,32,2048]{2,1,0:T(8,128)(2,1)}), bf16[16,32,2048]{2,1,0:T(8,128)(2,1)S(1)}, u32[]{:S(2)}, u32[]{:S(2)}) async-start(bf16[16,32,2048]{2,1,0:T(8,128)(2,1)} %norm_copies.1), calls=%async_computation | async-start | bytes 4194304 | tf_op jit(solution)/shard_map/all_to_all | solution.py:466
  10.7 6.6 %collective-permute-start = (bf16[128,2048]{1,0:T(8,128)(2,1)S(1)}, bf16[128,2048]{1,0:T(8,128)(2,1)}, u32[]{:S(2)}, u32[]{:S(2)}) collective-permute-start(bf16[128,2048]{1,0:T(8,128)(2,1)S(1)} %copy-done.4), channel_id=1, source_target_pairs={{0,1},{1,0},{2,3},{3,2},{4,5},{5,4},{6,7},{7,6},{8,9},{9,8},{10,11... | collective-permute-start | bytes 1572872 | tf_op jit(solution)/shard_map/ppermute | solution.py:462
  39.7 4.3 %copy-start.3 = (bf16[16,32,2048]{2,1,0:T(8,128)(2,1)}, bf16[16,32,2048]{2,1,0:T(8,128)(2,1)S(1)}, u32[]{:S(2)}) copy-start(bf16[16,32,2048]{2,1,0:T(8,128)(2,1)S(1)} %all-to-all-done.mine_ref) | copy-start | bytes 6291460
  39.7 4.3 %collective-permute-start.2 = (bf16[16,32,2048]{2,1,0:T(8,128)(2,1)S(1)}, bf16[16,32,2048]{2,1,0:T(8,128)(2,1)}, u32[]{:S(2)}, u32[]{:S(2)}) collective-permute-start(bf16[16,32,2048]{2,1,0:T(8,128)(2,1)S(1)} %all-to-all-done.mine_ref), channel_id=1, source_target_pairs={{0,1},{1,0},{2,3},{3,2},{4,5},{5,4},{6,7},{7,6},{8,9},{9,8},{10,11... | collective-permute-start | bytes 6291464 | tf_op jit(solution)/shard_map/ppermute | solution.py:462
  39.7 14.1 %collective-permute-start.1 = (bf16[128,2048]{1,0:T(8,128)(2,1)S(1)}, bf16[128,2048]{1,0:T(8,128)(2,1)S(1)}, u32[]{:S(2)}, u32[]{:S(2)}) collective-permute-start(bf16[128,2048]{1,0:T(8,128)(2,1)S(1)} %copy-done.4), channel_id=1, source_target_pairs={{0,2},{2,4},{4,6},{6,0},{1,7},{3,1},{5,3},{7,5},{8,10},{10,12},{12... | collective-permute-start | bytes 1572872 | tf_op jit(solution)/shard_map/ppermute | solution.py:454
  53.9 15.5 %copy-start.5 = (bf16[128,2048]{1,0:T(8,128)(2,1)}, bf16[128,2048]{1,0:T(8,128)(2,1)S(1)}, u32[]{:S(2)}) copy-start(bf16[128,2048]{1,0:T(8,128)(2,1)S(1)} %collective-permute-done.1.refs_2_) | copy-start | bytes 1572868
  53.9 26.3 %all-to-all-start.1 = ((bf16[8,128,256]{2,1,0:T(8,128)(2,1)}), bf16[8,128,256]{2,1,0:T(8,128)(2,1)S(1)}, u32[]{:S(2)}, u32[]{:S(2)}) async-start(bf16[8,128,256]{2,1,0:T(8,128)(2,1)} %get-tuple-element.34), calls=%async_computation.1 | async-start | bytes 1048576 | tf_op jit(solution)/shard_map/all_to_all | solution.py:466
  62.4 9.4 %collective-permute-start.4 = (bf16[128,2048]{1,0:T(8,128)(2,1)}, bf16[128,2048]{1,0:T(8,128)(2,1)S(1)}, u32[]{:S(2)}, u32[]{:S(2)}) collective-permute-start(bf16[128,2048]{1,0:T(8,128)(2,1)} %collective-permute-done.refs_1_), channel_id=1, source_target_pairs={{0,2},{2,4},{4,6},{6,0},{1,7},{3,1},{5,3},{7,5},{8,10},{10,12},{12... | collective-permute-start | bytes 1572872 | tf_op jit(solution)/shard_map/ppermute | solution.py:454
  62.4 15.0 %collective-permute-start.3 = (bf16[128,2048]{1,0:T(8,128)(2,1)S(1)}, bf16[128,2048]{1,0:T(8,128)(2,1)S(1)}, u32[]{:S(2)}, u32[]{:S(2)}) collective-permute-start(bf16[128,2048]{1,0:T(8,128)(2,1)S(1)} %collective-permute-done.1.refs_2_), channel_id=1, source_target_pairs={{0,2},{2,4},{4,6},{6,0},{1,7},{3,1},{5,3},{7,5},{8,10},{10,12},{12... | collective-permute-start | bytes 1572872 | tf_op jit(solution)/shard_map/ppermute | solution.py:454
  63.2 24.7 %collective-permute-start.5 = (bf16[128,2048]{1,0:T(8,128)(2,1)S(1)}, bf16[128,2048]{1,0:T(8,128)(2,1)S(1)}, u32[]{:S(2)}, u32[]{:S(2)}) collective-permute-start(bf16[128,2048]{1,0:T(8,128)(2,1)S(1)} %collective-permute-done.1.refs_2_), channel_id=1, source_target_pairs={{0,1},{1,0},{2,3},{3,2},{4,5},{5,4},{6,7},{7,6},{8,9},{9,8},{10,11... | collective-permute-start | bytes 1572872 | tf_op jit(solution)/shard_map/ppermute | solution.py:462
  71.7 22.2 %copy-start.6 = (bf16[128,2048]{1,0:T(8,128)(2,1)}, bf16[128,2048]{1,0:T(8,128)(2,1)S(1)}, u32[]{:S(2)}) copy-start(bf16[128,2048]{1,0:T(8,128)(2,1)S(1)} %collective-permute-done.4.refs_3_) | copy-start | bytes 1572868
  77.4 16.6 %copy-start.7 = (bf16[128,2048]{1,0:T(8,128)(2,1)}, bf16[128,2048]{1,0:T(8,128)(2,1)S(1)}, u32[]{:S(2)}) copy-start(bf16[128,2048]{1,0:T(8,128)(2,1)S(1)} %collective-permute-done.3.refs_4_) | copy-start | bytes 1572868
  77.4 10.5 %collective-permute-start.6 = (bf16[128,2048]{1,0:T(8,128)(2,1)S(1)}, bf16[128,2048]{1,0:T(8,128)(2,1)S(1)}, u32[]{:S(2)}, u32[]{:S(2)}) collective-permute-start(bf16[128,2048]{1,0:T(8,128)(2,1)S(1)} %collective-permute-done.4.refs_3_), channel_id=1, source_target_pairs={{0,1},{1,0},{2,3},{3,2},{4,5},{5,4},{6,7},{7,6},{8,9},{9,8},{10,11... | collective-permute-start | bytes 1572872 | tf_op jit(solution)/shard_map/ppermute | solution.py:462
  77.4 10.5 %collective-permute-start.7 = (bf16[128,2048]{1,0:T(8,128)(2,1)S(1)}, bf16[128,2048]{1,0:T(8,128)(2,1)}, u32[]{:S(2)}, u32[]{:S(2)}) collective-permute-start(bf16[128,2048]{1,0:T(8,128)(2,1)S(1)} %collective-permute-done.3.refs_4_), channel_id=1, source_target_pairs={{0,1},{1,0},{2,3},{3,2},{4,5},{5,4},{6,7},{7,6},{8,9},{9,8},{10,11... | collective-permute-start | bytes 1572872 | tf_op jit(solution)/shard_map/ppermute | solution.py:462
  83.1 10.9 %all-to-all-start.2 = ((bf16[8,4,32,128]{3,2,1,0:T(8,128)(2,1)}), bf16[8,4,32,128]{3,2,1,0:T(8,128)(2,1)S(1)}, u32[]{:S(2)}, u32[]{:S(2)}) async-start(bf16[8,4,32,128]{3,2,1,0:T(8,128)(2,1)} %emit.1), calls=%async_computation.2 | async-start | bytes 524288 | tf_op jit(solution)/shard_map/all_to_all | solution.py:466
  87.9 6.1 %copy-start.8 = (bf16[128,2048]{1,0:T(8,128)(2,1)}, bf16[128,2048]{1,0:T(8,128)(2,1)S(1)}, u32[]{:S(2)}) copy-start(bf16[128,2048]{1,0:T(8,128)(2,1)S(1)} %collective-permute-done.5.refs_5_) | copy-start | bytes 1572868
  87.9 6.1 %copy-start.9 = (bf16[128,2048]{1,0:T(8,128)(2,1)}, bf16[128,2048]{1,0:T(8,128)(2,1)S(1)}, u32[]{:S(2)}) copy-start(bf16[128,2048]{1,0:T(8,128)(2,1)S(1)} %collective-permute-done.6.refs_6_) | copy-start | bytes 1572868
  94.0 16.4 %copy-start.2 = (bf16[32,2048]{1,0:T(8,128)(2,1)S(1)}, bf16[32,2048]{1,0:T(8,128)(2,1)}, u32[]{:S(2)}) copy-start(bf16[32,2048]{1,0:T(8,128)(2,1)} %tokens_ref.3) | copy-start | bytes 393220
  97.4 16.2 %copy-start.1 = (bf16[1,512,2048]{2,1,0:T(8,128)(2,1)S(1)}, bf16[1,512,2048]{2,1,0:T(8,128)(2,1)}, u32[]{:S(2)}) copy-start(bf16[1,512,2048]{2,1,0:T(8,128)(2,1)} %down_a_ref.1) | copy-start | bytes 6291460
  113.5 34.6 %collective-permute-start.8 = (bf16[1,2048,1024]{2,1,0:T(8,128)(2,1)}, bf16[1,2048,1024]{2,1,0:T(8,128)(2,1)S(1)}, u32[]{:S(2)}, u32[]{:S(2)}) collective-permute-start(bf16[1,2048,1024]{2,1,0:T(8,128)(2,1)} %up_a_ref.1), channel_id=1, source_target_pairs={{0,1},{1,0},{2,3},{3,2},{4,5},{5,4},{6,7},{7,6},{8,9},{9,8},{10,11... | collective-permute-start | bytes 12582920 | tf_op jit(solution)/shard_map/ppermute | solution.py:462
  113.6 34.5 %collective-permute-start.9 = (bf16[1,512,2048]{2,1,0:T(8,128)(2,1)S(1)}, bf16[1,512,2048]{2,1,0:T(8,128)(2,1)S(1)}, u32[]{:S(2)}, u32[]{:S(2)}) collective-permute-start(bf16[1,512,2048]{2,1,0:T(8,128)(2,1)S(1)} %copy-done.1), channel_id=1, source_target_pairs={{0,1},{1,0},{2,3},{3,2},{4,5},{5,4},{6,7},{7,6},{8,9},{9,8},{10,11... | collective-permute-start | bytes 6291464 | tf_op jit(solution)/shard_map/ppermute | solution.py:462
  114.1 34.0 %copy-start = (bf16[1,2048,1024]{2,1,0:T(8,128)(2,1)S(1)}, bf16[1,2048,1024]{2,1,0:T(8,128)(2,1)}, u32[]{:S(2)}) copy-start(bf16[1,2048,1024]{2,1,0:T(8,128)(2,1)} %up_a_ref.1) | copy-start | bytes 12582916
